TPU v7x, 128 devices: a whole 4x4x4 slice. The times are simulated.
128 devices in a mesh: ctx: 16 (over y, x), head: 8 (over z, core).
Axes of the slice: x: 4, y: 4, z: 4, core: 2. Of those that a mesh axis runs over, the one named last changes fastest.
Arguments:
- queries: bfloat16 [16384, 40, 128], P('ctx', 'head'), may hold values from -6 to 6
- key_rows: bfloat16 [16384, 40, 128], P('ctx', 'head'), may hold values from -0.5390625 to 0.5390625
- value_rows: bfloat16 [16384, 40, 128], P('ctx', 'head'), may hold values from -6 to 6
- level_weight: float32 [16384, 40, 16], P('ctx', 'head'), may hold values from 0.001 to 2.5, as said below
- norm_gain: float32 [40, 128], P('head'), may hold values from 0.25 to 1.75
- out_weight: bfloat16 [5120, 5120], P('head'), may hold values from -0.078125 to 0.078125
Outputs:
- mixed: bfloat16 [16384, 5120], P(('ctx', 'head'))
Inputs may be any that keep to these rules, and one draw needn't show every extreme that they name: `level_weight`: positive level weights.
All inputs are finite; a program needn't handle non-finite values.
Results may differ from a plain program's by a relative error of at most 0.02.
Values may be sent and summed in bfloat16 or wider, within the bound.
No kernel may reach another device: no remote copies, remote signals or barrier semaphores. Data moves between devices by JAX's collectives and lax.ppermute only.
A program may use at most 128 MiB of HBM per device.

v0:
```python
import jax
import jax.numpy as jnp
from jax import lax
from jax.sharding import PartitionSpec as P

CH = 128


def level_table(stretch_len, level_count):
    position = jnp.arange(stretch_len, dtype=jnp.int32)
    xor_dist = jnp.bitwise_xor(position[:, None], position[None, :])
    level_ids = jnp.zeros((stretch_len, stretch_len), jnp.int32)
    for bit_idx in range(stretch_len.bit_length() - 1):
        level_ids = level_ids + (xor_dist >= 1 << bit_idx).astype(jnp.int32)
    level_onehot = (
        level_ids[:, :, None] == jnp.arange(level_count, dtype=jnp.int32)[None, None, :]
    ).astype(jnp.float32)
    causal_keep = (position[:, None] >= position[None, :]).astype(jnp.float32)
    return level_onehot * causal_keep[:, :, None]


def stretch_local(queries, key_rows, value_rows, level_weight, stretch_len):
    tok_count, head_count, head_width = queries.shape
    level_count = level_weight.shape[2]
    stretch_count = tok_count // stretch_len
    q_stretches = queries.reshape(stretch_count, stretch_len, head_count, head_width)
    k_stretches = key_rows.reshape(stretch_count, stretch_len, head_count, head_width)
    v_stretches = value_rows.reshape(stretch_count, stretch_len, head_count, head_width)
    w_stretches = level_weight.reshape(stretch_count, stretch_len, head_count, level_count)
    scores = jnp.einsum(
        "cthd,cshd->chts", q_stretches, k_stretches, preferred_element_type=jnp.float32
    )
    mix_weights = jnp.einsum(
        "cthl,tsl->chts",
        w_stretches,
        level_table(stretch_len, level_count),
        precision=lax.Precision.HIGHEST,
    )
    mixed_probs = (scores * mix_weights).astype(jnp.bfloat16)
    near = jnp.einsum(
        "chts,cshd->cthd", mixed_probs, v_stretches, preferred_element_type=jnp.float32
    )
    return near.reshape(tok_count, head_count, head_width)


def stretch_tree(queries, key_rows, value_rows, level_weight, stretch_len, first_level):
    tok_count, head_count, head_width = queries.shape
    stretch_count = tok_count // stretch_len
    q_stretches = queries.reshape(stretch_count, stretch_len, head_count, head_width)
    k_stretches = key_rows.reshape(stretch_count, stretch_len, head_count, head_width)
    v_stretches = value_rows.reshape(stretch_count, stretch_len, head_count, head_width)
    states = jnp.einsum(
        "cshd,cshe->chde", k_stretches, v_stretches, preferred_element_type=jnp.float32
    )
    result = jnp.zeros((stretch_count, stretch_len, head_count, head_width), jnp.float32)
    span_len = 1
    level_step = 0
    while span_len < stretch_count:
        groups = stretch_count // (2 * span_len)
        left_sum = states.reshape(groups, 2, span_len, head_count, head_width, head_width)[
            :, 0
        ].sum(axis=1)
        left_sum = left_sum.astype(jnp.bfloat16)
        upper_q = q_stretches.reshape(groups, 2, span_len, stretch_len, head_count, head_width)[
            :, 1
        ]
        readout = jnp.einsum(
            "gsthd,ghde->gsthe", upper_q, left_sum, preferred_element_type=jnp.float32
        )
        weights = level_weight.reshape(groups, 2, span_len, stretch_len, head_count, -1)[
            :, 1, :, :, :, first_level + level_step
        ]
        filled = jnp.stack([jnp.zeros_like(readout), readout * weights[..., None]], axis=1)
        result = result + filled.reshape(stretch_count, stretch_len, head_count, head_width)
        span_len = span_len * 2
        level_step = level_step + 1
    return (result.reshape(tok_count, head_count, head_width), states.sum(axis=0))


def on_device(queries, key_rows, value_rows, level_weight, norm_gain, out_weight):
    tok_count, head_count, head_width = queries.shape
    first_level = CH.bit_length()
    stretch_count = tok_count // CH
    near = stretch_local(queries, key_rows, value_rows, level_weight, CH)
    far, dev_state = stretch_tree(queries, key_rows, value_rows, level_weight, CH, first_level)
    attended = near + far
    device_level = first_level + stretch_count.bit_length() - 1
    ctx_index = lax.axis_index("ctx")
    bit_count = lax.axis_size("ctx").bit_length() - 1
    siblings = []
    gathered = lax.all_gather(
        dev_state[None].astype(jnp.bfloat16), "ctx", axis=0, tiled=True
    ).astype(jnp.float32)
    block_total = gathered.shape[0]
    for bit_idx in range(bit_count):
        groups = block_total // (2 << bit_idx)
        left_sum = gathered.reshape(groups, 2, 1 << bit_idx, head_count, head_width, head_width)[
            :, 0
        ].sum(axis=1)
        picked = lax.dynamic_index_in_dim(left_sum, ctx_index >> bit_idx + 1, 0, keepdims=False)
        siblings.append(picked)
    for bit_idx in range(bit_count):
        upper_flag = (ctx_index >> bit_idx & 1).astype(jnp.float32)
        sibling_state = (siblings[bit_idx] * upper_flag).astype(jnp.bfloat16)
        readout = jnp.einsum(
            "thd,hde->the", queries, sibling_state, preferred_element_type=jnp.float32
        )
        attended = attended + readout * level_weight[:, :, device_level + bit_idx][:, :, None]
    mean_sq = jnp.mean(attended * attended, axis=2, keepdims=True)
    normed = (attended * lax.rsqrt(mean_sq + 1e-06) * norm_gain[None, :, :]).astype(jnp.bfloat16)
    normed = normed.reshape(tok_count, head_count * head_width)
    return lax.psum_scatter(
        jnp.dot(normed, out_weight, preferred_element_type=jnp.float32).astype(jnp.bfloat16),
        "head",
        scatter_dimension=0,
        tiled=True,
    )


def solution(mesh):
    placed = (
        P("ctx", "head", None),
        P("ctx", "head", None),
        P("ctx", "head", None),
        P("ctx", "head", None),
        P("head", None),
        P("head", None),
    )
    return jax.shard_map(
        on_device, mesh=mesh, in_specs=placed, out_specs=P(("ctx", "head"), None), check_vma=False
    )
```

profile of v0, /device:TPU:1, one launch (start us, length us, event | category | flops | bytes accessed | tf_op | source)
XLA Modules:
  0.0 167.2 jit_solution(4082463604233687464)
XLA Ops:
  6.5 1.3 copy-done
  7.9 4.6 %fusion.48 = (bf16[8,5,128,128]{3,2,1,0:T(8,128)(2,1)}, bf16[5,128,128]{2,1,0:T(8,128)(2,1)}, f32[8,5,128,128]{3,2,1,0:T(8,128)}) fusion(bf16[8,128,5,128]{3,1,0,2:T(8,128)(2,1)S(1)} %bitcast.147, bf16[8,128,5,128]{3,1,0,2:T(8,128)(2,1)} %bitcast.163), kind=kOutput, calls=%fused_computation.80 | convolution fusion | flops 169000960 | bytes 6717440 | tf_op jit(solution)/shard_map/cshd,cshe->chde/dot_general | solution.py:52
  14.8 2.3 %copy.65 = f32[8,128,5,16]{3,0,2,1:T(8,128)} copy(f32[8,128,5,16]{1,0,3,2:T(8,128)S(1)} %bitcast.171) | data formatting | bytes 655360 | tf_op jit(solution)/shard_map/reshape | solution.py:29
  17.2 7.6 %fusion.15 = f32[128,128,8,5]{1,2,3,0:T(8,128)} fusion(f32[8,128,5,16]{3,0,2,1:T(8,128)} %copy.65, f32[128,128]{1,0:T(8,128)S(1)} %fusion.45, s32[128,128]{1,0:T(8,128)S(1)} %convert_add_fusion), kind=kOutput, calls=%fused_computation.30 | convolution fusion | flops 126353408 | bytes 3080192 | tf_op jit(solution)/shard_map/cthl,tsl->chts/dot_general | solution.py:33
  24.8 5.3 %convolution_bitcast_fusion = f32[8,128,5,128]{3,1,2,0:T(8,128)} fusion(f32[128,128,8,5]{1,2,3,0:T(8,128)} %fusion.15, bf16[8,128,5,128]{3,1,0,2:T(8,128)(2,1)S(1)} %bitcast.148, bf16[8,128,5,128]{3,1,0,2:T(8,128)(2,1)S(1)} %bitcast.146, bf16[8,128,5,128]{3,1,0,2:T(8,128)(2,1)} %bitcast.164), kind=kOutput, calls=%fused_computation.16 | convolution fusion | flops 336855040 | bytes 9175040 | tf_op jit(solution)/shard_map/chts,cshd->cthd/dot_general | solution.py:40
  30.2 3.6 %copy.68 = f32[8,128,5,128]{3,1,0,2:T(8,128)} copy(f32[8,128,5,128]{3,1,2,0:T(8,128)} %convolution_bitcast_fusion) | data formatting | bytes 5242880 | tf_op jit(solution)/shard_map/chts,cshd->cthd/transpose | solution.py:40
  33.8 3.3 %copy.84 = f32[1024,5,128]{0,2,1:T(8,128)} copy(f32[1024,5,128]{2,0,1:T(8,128)} %bitcast.159) | data formatting | bytes 5242880 | tf_op jit(solution)/shard_map/reshape | solution.py:43
  37.2 1.4 slice_reduce_fusion.3
  40.0 1.8 %stack.23.clone = f32[1,2,4,128,5,128]{5,3,2,1,4,0:T(8,128)} pad(f32[1,1,4,128,5,128]{5,3,2,1,4,0:T(8,128)S(1)} %multiply_bitcast_fusion, f32[]{:T(128)} %constant.21.clone.1), padding=0_0x1_0x0_0x0_0x0_0x0_0 | pad | bytes 3932164 | tf_op jit(solution)/shard_map/stack | solution.py:73
  41.8 3.3 %copy.83 = f32[1024,5,128]{0,2,1:T(8,128)} copy(f32[1024,5,128]{2,0,1:T(8,128)} %bitcast.160) | data formatting | bytes 5242880 | tf_op jit(solution)/shard_map/reshape | solution.py:74
  45.8 1.6 fusion.6
  47.6 1.8 %stack.19.clone = f32[4,2,1,128,5,128]{5,3,1,0,4,2:T(8,128)} pad(f32[4,1,1,128,5,128]{5,3,1,0,4,2:T(8,128)S(1)} %copy.110, f32[]{:T(128)} %constant.21.clone.1), padding=0_0x1_0x0_0x0_0x0_0x0_0 | pad | bytes 3932164 | tf_op jit(solution)/shard_map/stack | solution.py:73
  49.4 3.2 %copy.78 = f32[1024,5,128]{0,2,1:T(8,128)} copy(f32[1024,5,128]{2,0,1:T(8,128)} %bitcast.161) | data formatting | bytes 5242880 | tf_op jit(solution)/shard_map/reshape | solution.py:74
  52.8 1.7 %copy-done.6 = f32[8,5,128,128]{3,2,1,0:T(8,128)S(1)} copy-done((f32[8,5,128,128]{3,2,1,0:T(8,128)S(1)}, f32[8,5,128,128]{3,2,1,0:T(8,128)}, u32[]{:S(2)}) %copy-start.6) | copy-done | bytes 2621464
  55.4 1.8 %stack.21.clone = f32[2,2,2,128,5,128]{5,3,2,1,0,4:T(8,128)} pad(f32[2,1,2,128,5,128]{5,3,2,1,0,4:T(8,128)S(1)} %copy.111, f32[]{:T(128)} %constant.21.clone.1), padding=0_0x1_0x0_0x0_0x0_0x0_0 | pad | bytes 3932164 | tf_op jit(solution)/shard_map/stack | solution.py:73
  57.2 3.3 %copy.79 = f32[1024,5,128]{0,2,1:T(8,128)} copy(f32[1024,5,128]{2,0,1:T(8,128)} %bitcast.158) | data formatting | bytes 5242880 | tf_op jit(solution)/shard_map/reshape | solution.py:74
  61.7 2.4 %convert_element_type.157 = f32[80,128,128]{2,1,0:T(8,128)S(1)} convert(bf16[80,128,128]{2,1,0:T(8,128)(2,1)} %all-gather.3.cloned.1.call-done) | non-fusion elementwise | flops 1310720 | bytes 7864320 | tf_op jit(solution)/shard_map/convert_element_type | solution.py:93
  65.2 1.3 copy-done.3
  66.7 2.1 %slice_reduce_fusion.2 = f32[4,5,128,128]{3,2,1,0:T(8,128)S(1)} fusion(f32[4,2,2,5,128,128]{5,4,3,2,1,0:T(8,128)} %bitcast.154), kind=kLoop, calls=%fused_computation.3 | loop fusion | flops 327680 | bytes 3932160 | tf_op jit(solution)/shard_map/reduce_sum | solution.py:99
  69.0 4.9 %copy.85 = f32[80,128,128]{1,2,0:T(8,128)} copy(bf16[80,128,128]{2,1,0:T(8,128)(2,1)} %all-gather.3.cloned.1.call-done) | data formatting | bytes 7864320 | tf_op jit(solution)/shard_map/convert_element_type | solution.py:93
  73.9 2.0 %slice.78 = f32[8,1,1,5,128,128]{4,5,3,2,1,0:T(8,128)S(1)} slice(f32[8,2,1,5,128,128]{4,5,3,2,1,0:T(8,128)} %bitcast.155), slice={[0:8], [0:1], [0:1], [0:5], [0:128], [0:128]} | slice | bytes 5242880 | tf_op jit(solution)/shard_map/slice | solution.py:97
  80.2 1.7 %multiply_reduce_fusion = (f32[1024,5]{0,1:T(8,128)S(1)}, f32[1024,5,128]{0,2,1:T(8,128)S(1)}) fusion(f32[1024,5]{0,1:T(8,128)S(1)} %get-tuple-element.14, bf16[1024,5,128]{2,0,1:T(8,128)(2,1)S(1)} %copy-done.2, f32[5,128,128]{2,1,0:T(8,128)S(1)} %copy-done.10, f32[]{:T(128)S(6)} %convert_element_type.153, f32[1024,5]{0,1:T(8,128)S(1)} %get-tuple-element.15, ...), kind=kOutput, calls=%fused_computation.15 | convolution fusion | flops 176450560 | bytes 22712324 | tf_op jit(solution)/shard_map/thd,hde->the/dot_general | solution.py:105
  82.2 14.1 %convolution_convert_fusion = bf16[1024,5120]{1,0:T(8,128)(2,1)} fusion(bf16[1024,640]{0,1:T(8,128)(2,1)S(1)} %bitcast.170, bf16[640,5120]{1,0:T(8,128)(2,1)} %param.11), kind=kOutput, calls=%fused_computation | convolution fusion | flops 6716129280 | bytes 18350080 | tf_op jit(solution)/shard_map/dot_general | solution.py:113
  96.3 64.0 %reduce-scatter.2.cloned.1.call-done = bf16[128,5120]{1,0:T(8,128)(2,1)} async-done(((bf16[1024,5120]{1,0:T(8,128)(2,1)}), bf16[128,5120]{1,0:T(8,128)(2,1)}) %reduce-scatter.2.cloned.1.call-update) | async-done | bytes 1310736 | tf_op jit(solution)/shard_map/reduce_scatter | solution.py:112
  (60 shorter events, 12.9 us)
Async XLA Ops:
  6.5 1.3 copy-start
  6.5 55.1 %all-gather.3.cloned.1.call-start = ((), (), s32[]{:S(2)}) async-start(), calls=%async_computation.2 | async-start | bytes 2785280 | tf_op jit(solution)/shard_map/all_gather | solution.py:91
  7.9 4.7 %copy-start.9 = (f32[1024,5,16]{0,2,1:T(8,128)S(1)}, f32[1024,5,16]{0,2,1:T(8,128)}, u32[]{:S(2)}) copy-start(f32[1024,5,16]{0,2,1:T(8,128)} %param.9) | copy-start | bytes 983044
  12.5 147.8 %reduce-scatter.2.cloned.1.call-start = ((), (), s32[]{:S(2)}) async-start(), calls=%async_computation.1 | async-start | bytes 11796480 | tf_op jit(solution)/shard_map/reduce_scatter | solution.py:112
  17.2 7.6 %copy-start.2 = (bf16[1024,5,128]{2,0,1:T(8,128)(2,1)S(1)}, bf16[1024,5,128]{2,0,1:T(8,128)(2,1)}, u32[]{:S(2)}) copy-start(bf16[1024,5,128]{2,0,1:T(8,128)(2,1)} %param.6) | copy-start | bytes 3932164
  52.7 1.8 %copy-start.6 = (f32[8,5,128,128]{3,2,1,0:T(8,128)S(1)}, f32[8,5,128,128]{3,2,1,0:T(8,128)}, u32[]{:S(2)}) copy-start(f32[8,5,128,128]{3,2,1,0:T(8,128)} %get-tuple-element.11) | copy-start | bytes 7864324
  64.1 2.4 %copy-start.3 = (f32[80,128,128]{2,1,0:T(8,128)}, f32[80,128,128]{2,1,0:T(8,128)S(1)}, u32[]{:S(2)}) copy-start(f32[80,128,128]{2,1,0:T(8,128)S(1)} %convert_element_type.157) | copy-start | bytes 15728644
  75.9 1.7 %copy-start.8 = (f32[1024,5,128]{0,2,1:T(8,128)S(1)}, f32[1024,5,128]{0,2,1:T(8,128)}, u32[]{:S(2)}) copy-start(f32[1024,5,128]{0,2,1:T(8,128)} %copy.79) | copy-start | bytes 7864324
  76.4 2.1 %copy-start.5 = (f32[1024,5,128]{0,2,1:T(8,128)S(1)}, f32[1024,5,128]{0,2,1:T(8,128)}, u32[]{:S(2)}) copy-start(f32[1024,5,128]{0,2,1:T(8,128)} %copy.83) | copy-start | bytes 7864324
  76.4 2.9 %copy-start.7 = (f32[1024,5,128]{0,2,1:T(8,128)S(1)}, f32[1024,5,128]{0,2,1:T(8,128)}, u32[]{:S(2)}) copy-start(f32[1024,5,128]{0,2,1:T(8,128)} %copy.78) | copy-start | bytes 7864324
  77.0 3.2 %copy-start.4 = (f32[1024,5,128]{0,2,1:T(8,128)S(1)}, f32[1024,5,128]{0,2,1:T(8,128)}, u32[]{:S(2)}) copy-start(f32[1024,5,128]{0,2,1:T(8,128)} %copy.84) | copy-start | bytes 7864324
  77.0 3.2 %copy-start.10 = (f32[5,128,128]{2,1,0:T(8,128)S(1)}, f32[5,128,128]{2,1,0:T(8,128)}, u32[]{:S(2)}) copy-start(f32[5,128,128]{2,1,0:T(8,128)} %slice_reduce_fusion) | copy-start | bytes 983044
  80.2 1.8 %copy-start.11 = (f32[5,128]{1,0:T(8,128)S(1)}, f32[5,128]{1,0:T(8,128)}, u32[]{:S(2)}) copy-start(f32[5,128]{1,0:T(8,128)} %param.10) | copy-start | bytes 7684
  96.3 64.0 %copy-start.1 = (bf16[1024,5,128]{2,0,1:T(8,128)(2,1)S(1)}, bf16[1024,5,128]{2,0,1:T(8,128)(2,1)}, u32[]{:S(2)}) copy-start(bf16[1024,5,128]{2,0,1:T(8,128)(2,1)} %param.8) | copy-start | bytes 3932164
Sparse Core Ops, SparseCore 0:
  12.6 48.9 all-gather.2
  96.4 63.8 reduce-scatter.1
where the time goes:
time: 168 us; the launch traced here: 167 us
  waiting for transfers between devices  65.1 us (39%)
  local copies, waits for them, and re-layouts  43 us (26%)
  matrix products  37.1 us (22%)
  between operations  13.7 us (8%)
  other arithmetic  8.24 us (5%)
    reduce_scatter x1, waiting for transfers between devices, on_device(): lax.psum_scatter(jnp.dot(normed, out_weight, preferred_element_type=jnp.f...  64 us
    dot_general x1, matrix products, on_device(): jnp.dot(normed, out_weight, preferred_element_type=jnp.float32)  14.1 us
    reshape x3, local copies, waits for them, and re-layouts, stretch_tree(): filled.reshape(stretch_count, stretch_len, head_count, head_width)  9.78 us
    unnamed x31, local copies, waits for them, and re-layouts  7.68 us
    dot_general x1, matrix products, stretch_local(): jnp.einsum('cthl,tsl->chts', w_stretches, level_table(stretch_len, level_...  7.59 us
    another operation x3, local copies, waits for them, and re-layouts, stretch_tree(): jnp.stack([jnp.zeros_like(readout), readout * weights[..., None]], axis=1)  5.45 us
    dot_general x1, matrix products, stretch_local(): jnp.einsum('chts,cshd->cthd', mixed_probs, v_stretches, preferred_element...  5.33 us
    convert_element_type x1, local copies, waits for them, and re-layouts, on_device(): gathered = lax.all_gather(dev_state[None].astype(jnp.bfloat16), 'ctx', ax...  4.91 us
  transfers between devices with their start and end apart: 2, of which 2 were waited for; matrix products, arithmetic and copies ran while one was open for 28% of the time, Pallas kernels for 0%

commit v1 on v0

v1 whole, which is shorter than its diff:
```python
import jax
import jax.numpy as jnp
from jax import lax
from jax.experimental import pallas as pl
from jax.experimental.pallas import tpu as pltpu
from jax.sharding import PartitionSpec as P

CH = 128
F32 = jnp.float32
BF16 = jnp.bfloat16


def dot00(a, b):
    return lax.dot_general(a, b, (((0,), (0,)), ((), ())), preferred_element_type=F32)


def dot11(a, b):
    return lax.dot_general(a, b, (((1,), (1,)), ((), ())), preferred_element_type=F32)


def cost(flops, byte_count):
    return pl.CostEstimate(flops=flops, bytes_accessed=byte_count, transcendentals=0)


def state_body(k_ref, v_ref, out_ref):
    out_ref[0] = dot00(v_ref[0], k_ref[0])


def block_states(keys, values):
    heads, toks, dh = keys.shape
    spec = pl.BlockSpec((1, toks, dh), lambda h: (h, 0, 0))
    return pl.pallas_call(
        state_body,
        grid=(heads,),
        in_specs=[spec, spec],
        out_specs=pl.BlockSpec((1, dh, dh), lambda h: (h, 0, 0)),
        out_shape=jax.ShapeDtypeStruct((heads, dh, dh), F32),
        cost_estimate=cost(2 * heads * toks * dh * dh, 4 * heads * toks * dh),
        name="block_states",
    )(keys, values)


def local_body(q_ref, k_ref, v_ref, w_ref, out_ref):
    stretches = q_ref.shape[1] // CH
    key_pos = lax.broadcasted_iota(jnp.int32, (CH, CH), 0)
    tok_pos = lax.broadcasted_iota(jnp.int32, (CH, CH), 1)
    dist = jnp.bitwise_xor(key_pos, tok_pos)
    level = jnp.zeros((CH, CH), jnp.int32)
    for bit in range(CH.bit_length() - 1):
        level = level + (dist >= (1 << bit)).astype(jnp.int32)
    level = jnp.where(key_pos <= tok_pos, level, -1)
    first = CH.bit_length()
    states = []
    for c in range(stretches):
        rows = slice(c * CH, (c + 1) * CH)
        q, k, v = q_ref[0, rows, :], k_ref[0, rows, :], v_ref[0, rows, :]
        weights = w_ref[0, :, rows]
        mix = jnp.zeros((CH, CH), F32)
        for lev in range(first):
            mix = jnp.where(level == lev, weights[lev : lev + 1, :], mix)
        probs = (dot11(k, q) * mix).astype(BF16)
        total = dot00(v, probs)
        if c < stretches - 1:
            states.append(dot00(v, k))
        span, step = 1, 0
        while span < stretches:
            if c & span:
                base = (c // (2 * span)) * 2 * span
                left = states[base]
                for other in range(base + 1, base + span):
                    left = left + states[other]
                lev = first + step
                total = total + dot11(left.astype(BF16), q) * weights[lev : lev + 1, :]
            span, step = span * 2, step + 1
        out_ref[0, :, rows] = total


def local_part(queries, keys, values, weights, head):
    _, toks, dh = queries.shape
    levels = weights.shape[1]
    spec = pl.BlockSpec((1, toks, dh), lambda i: (head, 0, 0))
    return pl.pallas_call(
        local_body,
        grid=(1,),
        in_specs=[spec, spec, spec, pl.BlockSpec((1, levels, toks), lambda i: (head, 0, 0))],
        out_specs=pl.BlockSpec((1, dh, toks), lambda i: (0, 0, 0)),
        out_shape=jax.ShapeDtypeStruct((1, dh, toks), F32),
        cost_estimate=cost(2 * 5 * toks * dh * dh, 10 * toks * dh),
        name="local_part",
    )(queries, keys, values, weights)


def far_body(heads, bits, table_ref, *refs):
    half = heads + 2
    sib_refs = refs[2 * half : 2 * half + bits]
    gain_ref = refs[2 * half + bits]
    outs = refs[2 * half + bits + 1 :]
    first = CH.bit_length() + 3
    for side in range(2):
        acc_refs = refs[side * half : side * half + heads]
        q_ref, w_ref = refs[side * half + heads : (side + 1) * half]
        for h in range(heads):
            total = acc_refs[h][0]
            q = q_ref[h]
            for bit in range(bits):
                flag = table_ref[8 + bit].astype(F32)
                row = w_ref[h, first + bit : first + bit + 1, :] * flag
                total = total + dot11(sib_refs[bit][h], q) * row
            mean_sq = jnp.mean(total * total, axis=0, keepdims=True)
            normed = total * lax.rsqrt(mean_sq + 1e-06) * gain_ref[h]
            outs[side][0, :, h * CH : (h + 1) * CH] = normed.astype(BF16).T


def far_part(table, accs, queries, weights, sibs, gains, start, count):
    heads, toks, dh = queries.shape
    levels = weights.shape[1]
    bits = len(sibs)
    in_specs = []
    for side in range(2):
        pick = lambda j, tab, side=side: tab[2 * (start + j) + side]
        in_specs += [pl.BlockSpec((1, dh, CH), lambda j, tab, pick=pick: (0, 0, pick(j, tab)))] * heads
        in_specs.append(pl.BlockSpec((heads, CH, dh), lambda j, tab, pick=pick: (0, pick(j, tab), 0)))
        in_specs.append(pl.BlockSpec((heads, levels, CH), lambda j, tab, pick=pick: (0, 0, pick(j, tab))))
    in_specs += [pl.BlockSpec((heads, dh, dh), lambda j, tab: (0, 0, 0))] * (bits + 1)
    out_spec = pl.BlockSpec((1, CH, heads * dh), lambda j, tab: (j, 0, 0))
    out_shape = jax.ShapeDtypeStruct((count, CH, heads * dh), BF16)
    side_args = [*accs, queries, weights]
    return pl.pallas_call(
        lambda *refs: far_body(heads, bits, *refs),
        grid_spec=pltpu.PrefetchScalarGridSpec(
            num_scalar_prefetch=1,
            grid=(count,),
            in_specs=in_specs,
            out_specs=[out_spec, out_spec],
        ),
        out_shape=[out_shape, out_shape],
        cost_estimate=cost(2 * 2 * count * 4 * heads * CH * dh * dh, 2 * count * heads * CH * dh * 8),
        name="far_part",
    )(table, *side_args, *side_args, *sibs, gains)


def project_body(adds, own_ref, other_ref, wa_ref, wb_ref, *refs):
    total = jnp.dot(own_ref[0], wa_ref[...], preferred_element_type=F32)
    total = total + jnp.dot(other_ref[0], wb_ref[...], preferred_element_type=F32)
    for ref in refs[:adds]:
        total = total + ref[...].astype(F32)
    refs[adds][...] = total.astype(refs[adds].dtype)


def project(own, other, block, w_own, w_other, col_start, cols, adds=(), out_dtype=BF16, tile=512):
    _, rows, depth = own.shape
    first = col_start // tile
    row_spec = pl.BlockSpec((1, rows, depth), lambda n: (block, 0, 0))
    w_spec = pl.BlockSpec((depth, tile), lambda n: (0, first + n))
    tile_spec = pl.BlockSpec((rows, tile), lambda n: (0, n))
    return pl.pallas_call(
        lambda *refs: project_body(len(adds), *refs),
        grid=(cols // tile,),
        in_specs=[row_spec, row_spec, w_spec, w_spec] + [tile_spec] * len(adds),
        out_specs=tile_spec,
        out_shape=jax.ShapeDtypeStruct((rows, cols), out_dtype),
        cost_estimate=cost(2 * rows * cols * depth * 2, 4 * depth * cols + 4 * rows * cols),
        name="project",
    )(own, other, w_own, w_other, *adds)


def on_device(queries, key_rows, value_rows, level_weight, norm_gain, out_weight):
    toks, heads, dh = queries.shape
    q = jnp.transpose(queries, (1, 0, 2))
    k = jnp.transpose(key_rows, (1, 0, 2))
    v = jnp.transpose(value_rows, (1, 0, 2))
    w = jnp.transpose(level_weight, (1, 2, 0))
    width = out_weight.shape[1]
    half = width // 2
    ctx = lax.axis_index("ctx")
    place = lax.axis_index("head")
    z, core = place // 2, place % 2

    def along_z(x, step):
        pairs = [(2 * i + c, 2 * ((i + step) % 4) + c) for i in range(4) for c in range(2)]
        return lax.ppermute(x, "head", pairs)

    def across_cores(x):
        return lax.ppermute(x, "head", [(i, i ^ 1) for i in range(8)])

    def ctx_swap(x, bit):
        swap = ((1, 0, 3, 2), (3, 2, 1, 0))[bit % 2]
        if bit < 2:
            pairs = [(4 * y + i, 4 * y + swap[i]) for y in range(4) for i in range(4)]
        else:
            pairs = [(4 * i + x, 4 * swap[i] + x) for i in range(4) for x in range(4)]
        return lax.ppermute(x, "ctx", pairs)

    gains = jnp.broadcast_to(norm_gain[:, :, None], (heads, dh, CH))
    order = jnp.stack([(z + 2) % 4, (z + 1) % 4, (z + 3) % 4, z]).astype(jnp.int32)
    picks = jnp.stack([2 * order + core, 2 * order + 1 - core], axis=1).reshape(-1)
    flags = (ctx >> jnp.arange(4)) & 1
    table = jnp.concatenate([picks, flags]).astype(jnp.int32)

    running = block_states(k, v)
    w_other = across_cores(out_weight)
    accs = [local_part(q, k, v, w, h) for h in range(heads)]
    sibs = []
    for bit in range(4):
        got = ctx_swap(running.astype(BF16), bit)
        sibs.append(got)
        if bit < 3:
            running = running + got.astype(F32)

    own1, send1 = far_part(table, accs, q, w, sibs, gains, 0, 1)
    other1 = across_cores(send1)
    own2, send2 = far_part(table, accs, q, w, sibs, gains, 1, 3)
    other2 = across_cores(send2)

    relay_up = along_z(project(own1, other1, 0, out_weight, w_other, 0, half), 1)
    relay_down = along_z(project(own1, other1, 0, out_weight, w_other, half, half), -1)
    direct_up = along_z(project(own2, other2, 0, out_weight, w_other, half, half), 1)
    direct_down = along_z(project(own2, other2, 1, out_weight, w_other, 0, half), -1)
    joined_up = along_z(project(own2, other2, 0, out_weight, w_other, 0, half, (relay_up,)), 1)
    joined_down = along_z(project(own2, other2, 1, out_weight, w_other, half, half, (relay_down,)), -1)
    left = project(own2, other2, 2, out_weight, w_other, 0, half, (direct_down,), F32)
    right = project(own2, other2, 2, out_weight, w_other, half, half, (direct_up,), F32)
    left = (left + joined_up.astype(F32)).astype(BF16)
    right = (right + joined_down.astype(F32)).astype(BF16)
    return jnp.concatenate([left, right], axis=1)


def solution(mesh):
    placed = (
        P("ctx", "head", None),
        P("ctx", "head", None),
        P("ctx", "head", None),
        P("ctx", "head", None),
        P("head", None),
        P("head", None),
    )
    return jax.shard_map(
        on_device, mesh=mesh, in_specs=placed, out_specs=P(("ctx", "head"), None), check_vma=False
    )
```

time: 168 us -> 124 us (0.74)
  Pallas kernels: 0 us -> 80.7 us
  waiting for transfers between devices: 65.1 us -> 9.85 us
  local copies, waits for them, and re-layouts: 43 us -> 5.71 us
  matrix products: 37.1 us -> 0 us
  starting transfers between devices: 0.04 us -> 21.2 us
  between operations: 13.7 us -> 0.13 us
  other arithmetic: 8.24 us -> 5.52 us
    pallas_call x0 -> x16, Pallas kernels: none -> 80.7 us  [the longest x8 49.3 us: project(): pl.pallas_call(lambda *refs: project_body(len(adds), *refs), grid=(cols /...]
    reduce_scatter x1 -> x0, waiting for transfers between devices: 64 us -> none  [on_device(): lax.psum_scatter(jnp.dot(normed, out_weight, preferred_element_type=jnp.f...]
    dot_general x9 -> x0, matrix products: 36.5 us -> none  [the longest x1 14.1 us: on_device(): jnp.dot(normed, out_weight, preferred_element_type=jnp.float32)]
    ppermute x0 -> x13, starting transfers between devices: none -> 21.2 us  [the longest x4 7.98 us: ctx_swap(): return lax.ppermute(x, 'ctx', pairs)]
    reshape x8 -> x1, local copies, waits for them, and re-layouts: 17.6 us -> 0.09 us  [on_device(): jnp.stack([2 * order + core, 2 * order + 1 - core], axis=1).reshape(-1)]
    ppermute x0 -> x13, waiting for transfers between devices: none -> 9.85 us  [the longest x4 8.05 us: ctx_swap(): return lax.ppermute(x, 'ctx', pairs)]
    another operation x3 -> x1, local copies, waits for them, and re-layouts: 5.45 us -> 0.09 us  [on_device(): jnp.stack([2 * order + core, 2 * order + 1 - core], axis=1).reshape(-1)]
    convert_element_type x1 -> x0, local copies, waits for them, and re-layouts: 4.91 us -> none  [on_device(): gathered = lax.all_gather(dev_state[None].astype(jnp.bfloat16), 'ctx', ax...]
  transfers between devices with their start and end apart: 2 -> 13, of which waited for: 2 -> 4; matrix products, arithmetic and copies ran while one was open for 28% -> 3% of each run, Pallas kernels for 0% -> 61%
where the time goes in v1:
time: 124 us; the launch traced here: 123 us
  Pallas kernels  80.7 us (65%)
  starting transfers between devices  21.2 us (17%)
  waiting for transfers between devices  9.85 us (8%)
  local copies, waits for them, and re-layouts  5.71 us (5%)
  other arithmetic  5.52 us (4%)
    pallas_call x8, Pallas kernels, project(): pl.pallas_call(lambda *refs: project_body(len(adds), *refs), grid=(cols /...  49.3 us
    pallas_call x5, Pallas kernels, local_part(): pl.pallas_call(local_body, grid=(1,), in_specs=[spec, spec, spec, pl.Bloc...  15.7 us
    pallas_call x2, Pallas kernels, far_part(): pl.pallas_call(lambda *refs: far_body(heads, bits, *refs), grid_spec=pltp...  11.1 us
    ppermute x4, waiting for transfers between devices, ctx_swap(): return lax.ppermute(x, 'ctx', pairs)  8.05 us
    ppermute x4, starting transfers between devices, ctx_swap(): return lax.ppermute(x, 'ctx', pairs)  7.98 us
    ppermute x6, starting transfers between devices, along_z(): return lax.ppermute(x, 'head', pairs)  7.92 us
    ppermute x3, starting transfers between devices, across_cores(): return lax.ppermute(x, 'head', [(i, i ^ 1) for i in range(8)])  5.25 us
    unnamed x26, local copies, waits for them, and re-layouts  4.66 us
  transfers between devices with their start and end apart: 13, of which 4 were waited for; matrix products, arithmetic and copies ran while one was open for 3% of the time, Pallas kernels for 61%

profile of v1, /device:TPU:1, one launch (start us, length us, event | category | flops | bytes accessed | tf_op | source)
XLA Modules:
  0.0 123.1 jit_solution(5432095581617121442)
XLA Ops:
  1.4 4.6 %block_states.1 = f32[5,128,128]{2,1,0:T(8,128)} custom-call(bf16[5,1024,128]{2,1,0:T(8,128)(2,1)} %bitcast.17, bf16[5,1024,128]{2,1,0:T(8,128)(2,1)} %bitcast.23), custom_call_target="tpu_custom_call" | custom-call | flops 167772160 | bytes 2621440 | tf_op jit(solution)/shard_map/block_states/pallas_call | solution.py:32
  8.6 4.5 %collective-permute-done.refs_15_ = bf16[5,128,128]{2,1,0:T(8,128)(2,1)S(1)} collective-permute-done((bf16[5,128,128]{2,1,0:T(8,128)(2,1)S(1)}, bf16[5,128,128]{2,1,0:T(8,128)(2,1)S(1)}, u32[]{:S(2)}, u32[]{:S(2)}) %collective-permute-start) | collective-permute-done | bytes 163872 | tf_op jit(solution)/shard_map/ppermute | solution.py:192
  14.1 2.6 %collective-permute-start.1 = (bf16[5,128,128]{2,1,0:T(8,128)(2,1)S(1)}, bf16[5,128,128]{2,1,0:T(8,128)(2,1)S(1)}, u32[]{:S(2)}, u32[]{:S(2)}) collective-permute-start(bf16[5,128,128]{2,1,0:T(8,128)(2,1)S(1)} %fusion), channel_id=1, source_target_pairs={{0,24},{8,16},{16,8},{24,0},{32,56},{40,48},{48,40},{56,32},{64,88... | collective-permute-start | bytes 491528 | tf_op jit(solution)/shard_map/ppermute | solution.py:192
  16.7 3.6 %collective-permute-done.1.refs_16_ = bf16[5,128,128]{2,1,0:T(8,128)(2,1)S(1)} collective-permute-done((bf16[5,128,128]{2,1,0:T(8,128)(2,1)S(1)}, bf16[5,128,128]{2,1,0:T(8,128)(2,1)S(1)}, u32[]{:S(2)}, u32[]{:S(2)}) %collective-permute-start.1) | collective-permute-done | bytes 163872 | tf_op jit(solution)/shard_map/ppermute | solution.py:192
  21.9 3.1 %local_part.5.refs_1_.refs_8_ = f32[1,128,1024]{2,1,0:T(8,128)} custom-call(bf16[5,1024,128]{2,1,0:T(8,128)(2,1)} %bitcast.8, bf16[5,1024,128]{2,1,0:T(8,128)(2,1)} %bitcast.18, bf16[5,1024,128]{2,1,0:T(8,128)(2,1)} %bitcast.24, f32[5,16,1024]{2,1,0:T(8,128)} %bitcast.29), custom_call_target="tpu_custom_call" | custom-call | flops 167772160 | bytes 1310720 | tf_op jit(solution)/shard_map/local_part/pallas_call | solution.py:82
  25.1 2.5 %collective-permute-start.3 = (bf16[5,128,128]{2,1,0:T(8,128)(2,1)S(1)}, bf16[5,128,128]{2,1,0:T(8,128)(2,1)S(1)}, u32[]{:S(2)}, u32[]{:S(2)}) collective-permute-start(bf16[5,128,128]{2,1,0:T(8,128)(2,1)S(1)} %add_convert_fusion.2), channel_id=1, source_target_pairs={{0,96},{8,104},{16,112},{24,120},{32,64},{40,72},{48,80},{56,88},{... | collective-permute-start | bytes 491528 | tf_op jit(solution)/shard_map/ppermute | solution.py:192
  27.6 3.2 %local_part.6.refs_2_.refs_9_ = f32[1,128,1024]{2,1,0:T(8,128)} custom-call(bf16[5,1024,128]{2,1,0:T(8,128)(2,1)} %bitcast.9, bf16[5,1024,128]{2,1,0:T(8,128)(2,1)} %bitcast.19, bf16[5,1024,128]{2,1,0:T(8,128)(2,1)} %bitcast.25, f32[5,16,1024]{2,1,0:T(8,128)} %bitcast.30), custom_call_target="tpu_custom_call" | custom-call | flops 167772160 | bytes 1310720 | tf_op jit(solution)/shard_map/local_part/pallas_call | solution.py:82
  31.0 3.2 %local_part.7.refs_3_.refs_10_ = f32[1,128,1024]{2,1,0:T(8,128)} custom-call(bf16[5,1024,128]{2,1,0:T(8,128)(2,1)} %bitcast.10, bf16[5,1024,128]{2,1,0:T(8,128)(2,1)} %bitcast.20, bf16[5,1024,128]{2,1,0:T(8,128)(2,1)} %bitcast.26, f32[5,16,1024]{2,1,0:T(8,128)} %bitcast.31), custom_call_target="tpu_custom_call" | custom-call | flops 167772160 | bytes 1310720 | tf_op jit(solution)/shard_map/local_part/pallas_call | solution.py:82
  34.1 3.1 %local_part.8.refs_4_.refs_11_ = f32[1,128,1024]{2,1,0:T(8,128)} custom-call(bf16[5,1024,128]{2,1,0:T(8,128)(2,1)} %bitcast.11, bf16[5,1024,128]{2,1,0:T(8,128)(2,1)} %bitcast.21, bf16[5,1024,128]{2,1,0:T(8,128)(2,1)} %bitcast.27, f32[5,16,1024]{2,1,0:T(8,128)} %bitcast.32), custom_call_target="tpu_custom_call" | custom-call | flops 167772160 | bytes 1310720 | tf_op jit(solution)/shard_map/local_part/pallas_call | solution.py:82
  37.3 3.1 %local_part.9.refs_5_.refs_12_ = f32[1,128,1024]{2,1,0:T(8,128)} custom-call(bf16[5,1024,128]{2,1,0:T(8,128)(2,1)} %bitcast.12, bf16[5,1024,128]{2,1,0:T(8,128)(2,1)} %bitcast.22, bf16[5,1024,128]{2,1,0:T(8,128)(2,1)} %bitcast.28, f32[5,16,1024]{2,1,0:T(8,128)} %bitcast.33), custom_call_target="tpu_custom_call" | custom-call | flops 167772160 | bytes 1310720 | tf_op jit(solution)/shard_map/local_part/pallas_call | solution.py:82
  41.9 4.1 %far_part.3 = (bf16[1,128,640]{2,1,0:T(8,128)(2,1)}, bf16[1,128,640]{2,1,0:T(8,128)(2,1)}) custom-call(s32[12]{0:T(128)} %pad_add_fusion.1.refs_0_, f32[1,128,1024]{2,1,0:T(8,128)} %local_part.5.refs_1_.refs_8_, f32[1,128,1024]{2,1,0:T(8,128)} %local_part.6.refs_2_.refs_9_, f32[1,128,1024]{2,1,0:T(8,128)} %local_part.7.refs_3_.refs_10_, ...), custom_call_target="tpu_custom_call" | custom-call | flops 167772160 | bytes 1310720 | tf_op jit(solution)/shard_map/far_part/pallas_call | solution.py:128
  46.0 3.1 %collective-permute-start.7 = (bf16[1,128,640]{2,1,0:T(8,128)(2,1)}, bf16[1,128,640]{2,1,0:T(8,128)(2,1)S(1)}, u32[]{:S(2)}, u32[]{:S(2)}) collective-permute-start(bf16[1,128,640]{2,1,0:T(8,128)(2,1)} %get-tuple-element.12), channel_id=1, source_target_pairs={{0,1},{1,0},{2,3},{3,2},{4,5},{5,4},{6,7},{7,6},{8,9},{9,8},{10,11... | collective-permute-start | bytes 491528 | tf_op jit(solution)/shard_map/ppermute | solution.py:184
  51.0 6.0 %project.10 = bf16[128,2560]{1,0:T(8,128)(2,1)} custom-call(bf16[1,128,640]{2,1,0:T(8,128)(2,1)} %get-tuple-element.11.refs_0_, bf16[1,128,640]{2,1,0:T(8,128)(2,1)} %copy-done.7, bf16[640,5120]{1,0:T(8,128)(2,1)} %refs_2_.15, bf16[640,5120]{1,0:T(8,128)(2,1)} %collective-permute-done.5.refs_3_), custom_call_target="tpu_custom_call" | custom-call | flops 838860800 | bytes 7864320 | tf_op jit(solution)/shard_map/project/pallas_call | solution.py:156
  58.6 7.0 %far_part.2 = (bf16[3,128,640]{2,1,0:T(8,128)(2,1)}, bf16[3,128,640]{2,1,0:T(8,128)(2,1)}) custom-call(s32[12]{0:T(128)} %pad_add_fusion.1.refs_0_, f32[1,128,1024]{2,1,0:T(8,128)} %local_part.5.refs_1_.refs_8_, f32[1,128,1024]{2,1,0:T(8,128)} %local_part.6.refs_2_.refs_9_, f32[1,128,1024]{2,1,0:T(8,128)} %local_part.7.refs_3_.refs_10_, ...), custom_call_target="tpu_custom_call" | custom-call | flops 503316480 | bytes 3932160 | tf_op jit(solution)/shard_map/far_part/pallas_call | solution.py:128
  66.3 6.0 %project.14 = bf16[128,2560]{1,0:T(8,128)(2,1)} custom-call(bf16[1,128,640]{2,1,0:T(8,128)(2,1)} %get-tuple-element.11.refs_0_, bf16[1,128,640]{2,1,0:T(8,128)(2,1)} %copy-done.7, bf16[640,5120]{1,0:T(8,128)(2,1)} %refs_2_.15, bf16[640,5120]{1,0:T(8,128)(2,1)} %collective-permute-done.5.refs_3_), custom_call_target="tpu_custom_call" | custom-call | flops 838860800 | bytes 7864320 | tf_op jit(solution)/shard_map/project/pallas_call | solution.py:156
  72.3 1.8 %collective-permute-start.11 = (bf16[128,2560]{1,0:T(8,128)(2,1)}, bf16[128,2560]{1,0:T(8,128)(2,1)}, u32[]{:S(2)}, u32[]{:S(2)}) collective-permute-start(bf16[128,2560]{1,0:T(8,128)(2,1)} %project.14), channel_id=1, source_target_pairs={{0,6},{1,7},{2,0},{3,1},{4,2},{5,3},{6,4},{7,5},{8,14},{9,15},{10,... | collective-permute-start | bytes 1966088 | tf_op jit(solution)/shard_map/ppermute | solution.py:181
  75.0 6.0 %project.8 = bf16[128,2560]{1,0:T(8,128)(2,1)} custom-call(bf16[3,128,640]{2,1,0:T(8,128)(2,1)} %get-tuple-element.9.refs_0_, bf16[3,128,640]{2,1,0:T(8,128)(2,1)} %copy-done, bf16[640,5120]{1,0:T(8,128)(2,1)} %refs_2_.15, bf16[640,5120]{1,0:T(8,128)(2,1)} %collective-permute-done.5.refs_3_), custom_call_target="tpu_custom_call" | custom-call | flops 838860800 | bytes 7864320 | tf_op jit(solution)/shard_map/project/pallas_call | solution.py:156
  81.0 1.8 %collective-permute-start.6 = (bf16[128,2560]{1,0:T(8,128)(2,1)}, bf16[128,2560]{1,0:T(8,128)(2,1)S(1)}, u32[]{:S(2)}, u32[]{:S(2)}) collective-permute-start(bf16[128,2560]{1,0:T(8,128)(2,1)} %project.8), channel_id=1, source_target_pairs={{0,6},{1,7},{2,0},{3,1},{4,2},{5,3},{6,4},{7,5},{8,14},{9,15},{10,... | collective-permute-start | bytes 1966088 | tf_op jit(solution)/shard_map/ppermute | solution.py:181
  82.7 6.0 %project.12 = bf16[128,2560]{1,0:T(8,128)(2,1)} custom-call(bf16[3,128,640]{2,1,0:T(8,128)(2,1)} %get-tuple-element.9.refs_0_, bf16[3,128,640]{2,1,0:T(8,128)(2,1)} %copy-done, bf16[640,5120]{1,0:T(8,128)(2,1)} %refs_2_.15, bf16[640,5120]{1,0:T(8,128)(2,1)} %collective-permute-done.5.refs_3_), custom_call_target="tpu_custom_call" | custom-call | flops 838860800 | bytes 7864320 | tf_op jit(solution)/shard_map/project/pallas_call | solution.py:156
  89.6 6.2 %project.11 = bf16[128,2560]{1,0:T(8,128)(2,1)} custom-call(bf16[3,128,640]{2,1,0:T(8,128)(2,1)} %get-tuple-element.9.refs_0_, bf16[3,128,640]{2,1,0:T(8,128)(2,1)} %copy-done, bf16[640,5120]{1,0:T(8,128)(2,1)} %refs_2_.15, bf16[640,5120]{1,0:T(8,128)(2,1)} %collective-permute-done.5.refs_3_, bf16[128,2560]{1,0:T(8,128)(2,1)} %copy-done.10), custom_call_target="tpu_custom_call" | custom-call | flops 838860800 | bytes 7864320 | tf_op jit(solution)/shard_map/project/pallas_call | solution.py:156
  95.8 6.3 %project.15 = bf16[128,2560]{1,0:T(8,128)(2,1)} custom-call(bf16[3,128,640]{2,1,0:T(8,128)(2,1)} %get-tuple-element.9.refs_0_, bf16[3,128,640]{2,1,0:T(8,128)(2,1)} %copy-done, bf16[640,5120]{1,0:T(8,128)(2,1)} %refs_2_.15, bf16[640,5120]{1,0:T(8,128)(2,1)} %collective-permute-done.5.refs_3_, bf16[128,2560]{1,0:T(8,128)(2,1)} %collective-permute-done.11.refs_4_), custom_call_target="tpu_custom_call" | custom-call | flops 838860800 | bytes 7864320 | tf_op jit(solution)/shard_map/project/pallas_call | solution.py:156
  102.1 2.7 %collective-permute-start.12 = (bf16[128,2560]{1,0:T(8,128)(2,1)}, bf16[128,2560]{1,0:T(8,128)(2,1)}, u32[]{:S(2)}, u32[]{:S(2)}) collective-permute-start(bf16[128,2560]{1,0:T(8,128)(2,1)} %project.15), channel_id=1, source_target_pairs={{0,6},{1,7},{2,0},{3,1},{4,2},{5,3},{6,4},{7,5},{8,14},{9,15},{10,... | collective-permute-start | bytes 1966088 | tf_op jit(solution)/shard_map/ppermute | solution.py:181
  105.6 6.5 %project.9 = f32[128,2560]{1,0:T(8,128)} custom-call(bf16[3,128,640]{2,1,0:T(8,128)(2,1)} %get-tuple-element.9.refs_0_, bf16[3,128,640]{2,1,0:T(8,128)(2,1)} %copy-done, bf16[640,5120]{1,0:T(8,128)(2,1)} %refs_2_.15, bf16[640,5120]{1,0:T(8,128)(2,1)} %collective-permute-done.5.refs_3_, bf16[128,2560]{1,0:T(8,128)(2,1)} %copy-done.9), custom_call_target="tpu_custom_call" | custom-call | flops 838860800 | bytes 7864320 | tf_op jit(solution)/shard_map/project/pallas_call | solution.py:156
  112.9 6.4 %project.13 = f32[128,2560]{1,0:T(8,128)} custom-call(bf16[3,128,640]{2,1,0:T(8,128)(2,1)} %get-tuple-element.9.refs_0_, bf16[3,128,640]{2,1,0:T(8,128)(2,1)} %copy-done, bf16[640,5120]{1,0:T(8,128)(2,1)} %refs_2_.15, bf16[640,5120]{1,0:T(8,128)(2,1)} %collective-permute-done.5.refs_3_, bf16[128,2560]{1,0:T(8,128)(2,1)} %copy-done.8), custom_call_target="tpu_custom_call" | custom-call | flops 838860800 | bytes 7864320 | tf_op jit(solution)/shard_map/project/pallas_call | solution.py:156
  (59 shorter events, 19.6 us)
Async XLA Ops:
  0.0 50.3 %collective-permute-start.5 = (bf16[640,5120]{1,0:T(8,128)(2,1)}, bf16[640,5120]{1,0:T(8,128)(2,1)}, u32[]{:S(2)}, u32[]{:S(2)}) collective-permute-start(bf16[640,5120]{1,0:T(8,128)(2,1)} %refs_2_.15), channel_id=1, source_target_pairs={{0,1},{1,0},{2,3},{3,2},{4,5},{5,4},{6,7},{7,6},{8,9},{9,8},{10,11... | collective-permute-start | bytes 19660808 | tf_op jit(solution)/shard_map/ppermute | solution.py:184
  6.0 14.3 %copy-start.1 = (f32[5,128,128]{2,1,0:T(8,128)S(1)}, f32[5,128,128]{2,1,0:T(8,128)}, u32[]{:S(2)}) copy-start(f32[5,128,128]{2,1,0:T(8,128)} %block_states.1) | copy-start | bytes 983044
  7.1 5.9 %collective-permute-start = (bf16[5,128,128]{2,1,0:T(8,128)(2,1)S(1)}, bf16[5,128,128]{2,1,0:T(8,128)(2,1)S(1)}, u32[]{:S(2)}, u32[]{:S(2)}) collective-permute-start(bf16[5,128,128]{2,1,0:T(8,128)(2,1)S(1)} %convert_element_type.33), channel_id=1, source_target_pairs={{0,8},{8,0},{16,24},{24,16},{32,40},{40,32},{48,56},{56,48},{64,72... | collective-permute-start | bytes 491528 | tf_op jit(solution)/shard_map/ppermute | solution.py:192
  13.0 12.0 %copy-start.4 = (bf16[5,128,128]{2,1,0:T(8,128)(2,1)}, bf16[5,128,128]{2,1,0:T(8,128)(2,1)S(1)}, u32[]{:S(2)}) copy-start(bf16[5,128,128]{2,1,0:T(8,128)(2,1)S(1)} %collective-permute-done.refs_15_) | copy-start | bytes 491524
  14.1 6.2 %collective-permute-start.1 = (bf16[5,128,128]{2,1,0:T(8,128)(2,1)S(1)}, bf16[5,128,128]{2,1,0:T(8,128)(2,1)S(1)}, u32[]{:S(2)}, u32[]{:S(2)}) collective-permute-start(bf16[5,128,128]{2,1,0:T(8,128)(2,1)S(1)} %fusion), channel_id=1, source_target_pairs={{0,24},{8,16},{16,8},{24,0},{32,56},{40,48},{48,40},{56,32},{64,88... | collective-permute-start | bytes 491528 | tf_op jit(solution)/shard_map/ppermute | solution.py:192
  20.3 4.7 %copy-start.5 = (bf16[5,128,128]{2,1,0:T(8,128)(2,1)}, bf16[5,128,128]{2,1,0:T(8,128)(2,1)S(1)}, u32[]{:S(2)}) copy-start(bf16[5,128,128]{2,1,0:T(8,128)(2,1)S(1)} %collective-permute-done.1.refs_16_) | copy-start | bytes 491524
  20.4 4.6 %collective-permute-start.2 = (bf16[5,128,128]{2,1,0:T(8,128)(2,1)S(1)}, bf16[5,128,128]{2,1,0:T(8,128)(2,1)S(1)}, u32[]{:S(2)}, u32[]{:S(2)}) collective-permute-start(bf16[5,128,128]{2,1,0:T(8,128)(2,1)S(1)} %fusion.1), channel_id=1, source_target_pairs={{0,32},{8,40},{16,48},{24,56},{32,0},{40,8},{48,16},{56,24},{64,96... | collective-permute-start | bytes 491528 | tf_op jit(solution)/shard_map/ppermute | solution.py:192
  25.0 5.8 %copy-start.6 = (bf16[5,128,128]{2,1,0:T(8,128)(2,1)}, bf16[5,128,128]{2,1,0:T(8,128)(2,1)S(1)}, u32[]{:S(2)}) copy-start(bf16[5,128,128]{2,1,0:T(8,128)(2,1)S(1)} %collective-permute-done.2.refs_17_) | copy-start | bytes 491524
  25.1 15.9 %collective-permute-start.3 = (bf16[5,128,128]{2,1,0:T(8,128)(2,1)S(1)}, bf16[5,128,128]{2,1,0:T(8,128)(2,1)S(1)}, u32[]{:S(2)}, u32[]{:S(2)}) collective-permute-start(bf16[5,128,128]{2,1,0:T(8,128)(2,1)S(1)} %add_convert_fusion.2), channel_id=1, source_target_pairs={{0,96},{8,104},{16,112},{24,120},{32,64},{40,72},{48,80},{56,88},{... | collective-permute-start | bytes 491528 | tf_op jit(solution)/shard_map/ppermute | solution.py:192
  37.3 3.8 %copy-start.12 = (f32[5,128]{1,0:T(8,128)S(1)}, f32[5,128]{1,0:T(8,128)}, u32[]{:S(2)}) copy-start(f32[5,128]{1,0:T(8,128)} %param.10) | copy-start | bytes 7684
  41.0 0.9 copy-start.11
  46.0 4.3 %collective-permute-start.7 = (bf16[1,128,640]{2,1,0:T(8,128)(2,1)}, bf16[1,128,640]{2,1,0:T(8,128)(2,1)S(1)}, u32[]{:S(2)}, u32[]{:S(2)}) collective-permute-start(bf16[1,128,640]{2,1,0:T(8,128)(2,1)} %get-tuple-element.12), channel_id=1, source_target_pairs={{0,1},{1,0},{2,3},{3,2},{4,5},{5,4},{6,7},{7,6},{8,9},{9,8},{10,11... | collective-permute-start | bytes 491528 | tf_op jit(solution)/shard_map/ppermute | solution.py:184
  57.0 31.8 %collective-permute-start.8 = (bf16[128,2560]{1,0:T(8,128)(2,1)}, bf16[128,2560]{1,0:T(8,128)(2,1)S(1)}, u32[]{:S(2)}, u32[]{:S(2)}) collective-permute-start(bf16[128,2560]{1,0:T(8,128)(2,1)} %project.10), channel_id=1, source_target_pairs={{0,2},{1,3},{2,4},{3,5},{4,6},{5,7},{6,0},{7,1},{8,10},{9,11},{10,... | collective-permute-start | bytes 1966088 | tf_op jit(solution)/shard_map/ppermute | solution.py:181
  65.6 8.6 %collective-permute-start.4 = (bf16[3,128,640]{2,1,0:T(8,128)(2,1)}, bf16[3,128,640]{2,1,0:T(8,128)(2,1)S(1)}, u32[]{:S(2)}, u32[]{:S(2)}) collective-permute-start(bf16[3,128,640]{2,1,0:T(8,128)(2,1)} %get-tuple-element.10), channel_id=1, source_target_pairs={{0,1},{1,0},{2,3},{3,2},{4,5},{5,4},{6,7},{7,6},{8,9},{9,8},{10,11... | collective-permute-start | bytes 1474568 | tf_op jit(solution)/shard_map/ppermute | solution.py:184
  72.3 23.5 %collective-permute-start.11 = (bf16[128,2560]{1,0:T(8,128)(2,1)}, bf16[128,2560]{1,0:T(8,128)(2,1)}, u32[]{:S(2)}, u32[]{:S(2)}) collective-permute-start(bf16[128,2560]{1,0:T(8,128)(2,1)} %project.14), channel_id=1, source_target_pairs={{0,6},{1,7},{2,0},{3,1},{4,2},{5,3},{6,4},{7,5},{8,14},{9,15},{10,... | collective-permute-start | bytes 1966088 | tf_op jit(solution)/shard_map/ppermute | solution.py:181
  74.2 0.8 copy-start
  81.0 23.8 %collective-permute-start.6 = (bf16[128,2560]{1,0:T(8,128)(2,1)}, bf16[128,2560]{1,0:T(8,128)(2,1)S(1)}, u32[]{:S(2)}, u32[]{:S(2)}) collective-permute-start(bf16[128,2560]{1,0:T(8,128)(2,1)} %project.8), channel_id=1, source_target_pairs={{0,6},{1,7},{2,0},{3,1},{4,2},{5,3},{6,4},{7,5},{8,14},{9,15},{10,... | collective-permute-start | bytes 1966088 | tf_op jit(solution)/shard_map/ppermute | solution.py:181
  88.7 23.4 %collective-permute-start.10 = (bf16[128,2560]{1,0:T(8,128)(2,1)}, bf16[128,2560]{1,0:T(8,128)(2,1)S(1)}, u32[]{:S(2)}, u32[]{:S(2)}) collective-permute-start(bf16[128,2560]{1,0:T(8,128)(2,1)} %project.12), channel_id=1, source_target_pairs={{0,2},{1,3},{2,4},{3,5},{4,6},{5,7},{6,0},{7,1},{8,10},{9,11},{10,... | collective-permute-start | bytes 1966088 | tf_op jit(solution)/shard_map/ppermute | solution.py:181
  88.7 0.8 copy-start.10
  95.8 24.1 %collective-permute-start.9 = (bf16[128,2560]{1,0:T(8,128)(2,1)}, bf16[128,2560]{1,0:T(8,128)(2,1)S(1)}, u32[]{:S(2)}, u32[]{:S(2)}) collective-permute-start(bf16[128,2560]{1,0:T(8,128)(2,1)} %project.11), channel_id=1, source_target_pairs={{0,2},{1,3},{2,4},{3,5},{4,6},{5,7},{6,0},{7,1},{8,10},{9,11},{10,... | collective-permute-start | bytes 1966088 | tf_op jit(solution)/shard_map/ppermute | solution.py:181
  102.1 17.9 %collective-permute-start.12 = (bf16[128,2560]{1,0:T(8,128)(2,1)}, bf16[128,2560]{1,0:T(8,128)(2,1)}, u32[]{:S(2)}, u32[]{:S(2)}) collective-permute-start(bf16[128,2560]{1,0:T(8,128)(2,1)} %project.15), channel_id=1, source_target_pairs={{0,6},{1,7},{2,0},{3,1},{4,2},{5,3},{6,4},{7,5},{8,14},{9,15},{10,... | collective-permute-start | bytes 1966088 | tf_op jit(solution)/shard_map/ppermute | solution.py:181
  104.8 0.8 copy-start.9
  112.1 7.8 %copy-start.3 = (f32[128,2560]{1,0:T(8,128)S(1)}, f32[128,2560]{1,0:T(8,128)}, u32[]{:S(2)}) copy-start(f32[128,2560]{1,0:T(8,128)} %project.9) | copy-start | bytes 3932164
  119.3 1.3 %copy-start.2 = (f32[128,2560]{1,0:T(8,128)S(1)}, f32[128,2560]{1,0:T(8,128)}, u32[]{:S(2)}) copy-start(f32[128,2560]{1,0:T(8,128)} %project.13) | copy-start | bytes 3932164
  (2 other events, 1.5 us)

commit v2 on v1

v2 whole, which is shorter than its diff:
```python
import jax
import jax.numpy as jnp
from jax import lax
from jax.experimental import pallas as pl
from jax.experimental.pallas import tpu as pltpu
from jax.sharding import PartitionSpec as P

CH = 128
F32 = jnp.float32
BF16 = jnp.bfloat16
VMEM = pl.BlockSpec(memory_space=pltpu.VMEM)
LOCAL_LEVELS = CH.bit_length()


def dot00(a, b):
    return lax.dot_general(a, b, (((0,), (0,)), ((), ())), preferred_element_type=F32)


def dot11(a, b):
    return lax.dot_general(a, b, (((1,), (1,)), ((), ())), preferred_element_type=F32)


def cost(flops, byte_count):
    return pl.CostEstimate(flops=flops, bytes_accessed=byte_count, transcendentals=0)


def vmem(megabytes):
    return pltpu.CompilerParams(vmem_limit_bytes=megabytes << 20)


def local_body(heads, q_ref, k_ref, v_ref, w_ref, out_ref):
    stretches = q_ref.shape[1] // CH
    key_pos = lax.broadcasted_iota(jnp.int32, (CH, CH), 0)
    tok_pos = lax.broadcasted_iota(jnp.int32, (CH, CH), 1)
    dist = jnp.bitwise_xor(key_pos, tok_pos)
    level = jnp.zeros((CH, CH), jnp.int32)
    for bit in range(LOCAL_LEVELS - 1):
        level = level + (dist >= (1 << bit)).astype(jnp.int32)
    level = jnp.where(key_pos <= tok_pos, level, -1)
    for slot, h in enumerate(heads):
        states = []
        for c in range(stretches):
            rows = slice(c * CH, (c + 1) * CH)
            q, k, v = q_ref[h, rows, :], k_ref[h, rows, :], v_ref[h, rows, :]
            weights = w_ref[h, :, rows]
            mix = jnp.zeros((CH, CH), F32)
            for lev in range(LOCAL_LEVELS):
                mix = jnp.where(level == lev, weights[lev : lev + 1, :], mix)
            lefts, levs = [], []
            span, step = 1, 0
            while span < stretches:
                if c & span:
                    base = (c // (2 * span)) * 2 * span
                    left = states[base]
                    for other in range(base + 1, base + span):
                        left = left + states[other]
                    lefts.append(left.astype(BF16))
                    levs.append(LOCAL_LEVELS + step)
                span, step = span * 2, step + 1
            read = dot11(jnp.concatenate([k] + lefts, axis=0), q)
            probs = (read[:CH] * mix).astype(BF16)
            if c < stretches - 1:
                both = dot00(v, jnp.concatenate([probs, k], axis=1))
                total = both[:, :CH]
                states.append(both[:, CH:])
            else:
                total = dot00(v, probs)
            for i, lev in enumerate(levs):
                total = total + read[(1 + i) * CH : (2 + i) * CH] * weights[lev : lev + 1, :]
            out_ref[slot, :, rows] = total


def local_part(queries, keys, values, weights, heads):
    _, toks, dh = queries.shape
    count = len(heads)
    return pl.pallas_call(
        lambda *refs: local_body(heads, *refs),
        in_specs=[VMEM] * 4,
        out_specs=VMEM,
        out_shape=jax.ShapeDtypeStruct((count, dh, toks), F32),
        cost_estimate=cost(10 * count * toks * dh * dh, 10 * count * toks * dh),
        compiler_params=vmem(16),
        name="local_part",
    )(queries, keys, values, weights)


def far_body(parts, first, away, steps, q_ref, w_ref, gain_ref, sib_refs, acc_refs, out_ref):
    bits = len(sib_refs)
    ctx, place = lax.axis_index("ctx"), lax.axis_index("head")
    z, side = place // 2, (place + away) % 2
    flags = [((ctx >> bit) & 1).astype(F32) for bit in range(bits)]
    for j, step in enumerate(steps):
        start = pl.multiple_of((2 * ((z + step) % 4) + side) * CH, CH)
        span = pl.ds(start, CH)
        for a, group in enumerate(parts):
            for slot, h in enumerate(group):
                sib = jnp.concatenate([ref[h] for ref in sib_refs], axis=0)
                read = dot11(sib, q_ref[h, span, :])
                total = acc_refs[a][slot, :, span]
                for bit in range(bits):
                    row = w_ref[h, first + bit : first + bit + 1, span] * flags[bit]
                    total = total + read[bit * CH : (bit + 1) * CH] * row
                mean_sq = jnp.mean(total * total, axis=0, keepdims=True)
                normed = total * lax.rsqrt(mean_sq + 1e-06) * gain_ref[h]
                out_ref[j, :, h * CH : (h + 1) * CH] = normed.astype(BF16).T


def far_part(accs, parts, queries, weights, sibs, gains, away, steps):
    heads, toks, dh = queries.shape
    count = len(steps)
    first = LOCAL_LEVELS + (toks // CH).bit_length() - 1
    bits = len(sibs)

    def body(q_ref, w_ref, gain_ref, *refs):
        far_body(parts, first, away, steps, q_ref, w_ref, gain_ref, refs[:bits], refs[bits:-1], refs[-1])

    return pl.pallas_call(
        body,
        in_specs=[VMEM] * (3 + bits + len(accs)),
        out_specs=VMEM,
        out_shape=jax.ShapeDtypeStruct((count, CH, heads * dh), BF16),
        cost_estimate=cost(1000, 1000),
        compiler_params=vmem(16),
        name="far_part",
    )(queries, weights, gains, *sibs, *accs)


def project_body(block, col_start, tile, adds, own_ref, other_ref, wa_ref, wb_ref, *refs):
    out_ref = refs[-1]
    for n in range(out_ref.shape[1] // tile):
        here = slice(n * tile, (n + 1) * tile)
        there = slice(col_start + n * tile, col_start + (n + 1) * tile)
        total = jnp.dot(own_ref[block], wa_ref[:, there], preferred_element_type=F32)
        total = total + jnp.dot(other_ref[block], wb_ref[:, there], preferred_element_type=F32)
        for source, offset in adds:
            if offset <= n * tile < offset + refs[source].shape[1]:
                part = slice(n * tile - offset, (n + 1) * tile - offset)
                total = total + refs[source][:, part].astype(F32)
        out_ref[:, here] = total.astype(out_ref.dtype)


def project(own, other, block, w_own, w_other, col_start, cols, adds=(), out_dtype=BF16, tile=512):
    _, rows, depth = own.shape
    places = [(i, offset) for i, (_, offset) in enumerate(adds)]
    return pl.pallas_call(
        lambda *refs: project_body(block, col_start, tile, places, *refs),
        in_specs=[VMEM] * (4 + len(adds)),
        out_specs=VMEM,
        out_shape=jax.ShapeDtypeStruct((rows, cols), out_dtype),
        cost_estimate=cost(1000, 1000),
        compiler_params=vmem(24),
        name="project",
    )(own, other, w_own, w_other, *[x for x, _ in adds])


def finish_body(own_ref, left_ref, right_ref, out_ref):
    tile = out_ref.shape[1]
    half = left_ref.shape[1]
    step = pl.program_id(0)
    span = pl.ds(pl.multiple_of(step * tile, tile), tile)

    @pl.when(step * tile < half)
    def _():
        out_ref[...] = (own_ref[:, span] + left_ref[:, span].astype(F32)).astype(out_ref.dtype)

    @pl.when(step * tile >= half)
    def _():
        late = pl.ds(pl.multiple_of(step * tile - half, tile), tile)
        out_ref[...] = (own_ref[:, span] + right_ref[:, late].astype(F32)).astype(out_ref.dtype)


def finish(own, left, right, tile=1280):
    rows, cols = own.shape
    return pl.pallas_call(
        finish_body,
        grid=(cols // tile,),
        in_specs=[VMEM] * 3,
        out_specs=pl.BlockSpec((rows, tile), lambda n: (0, n)),
        out_shape=jax.ShapeDtypeStruct((rows, cols), BF16),
        cost_estimate=cost(rows * cols, 10 * rows * cols),
        compiler_params=vmem(16),
        name="finish",
    )(own, left, right)


def on_device(queries, key_rows, value_rows, level_weight, norm_gain, out_weight):
    toks, heads, dh = queries.shape
    q = jnp.transpose(queries, (1, 0, 2))
    k = jnp.transpose(key_rows, (1, 0, 2))
    v = jnp.transpose(value_rows, (1, 0, 2))
    w = jnp.transpose(level_weight, (1, 2, 0))
    width = out_weight.shape[1]
    half = width // 2

    def along_z(x, step):
        pairs = [(2 * i + c, 2 * ((i + step) % 4) + c) for i in range(4) for c in range(2)]
        return lax.ppermute(x, "head", pairs)

    def across_cores(x):
        return lax.ppermute(x, "head", [(i, i ^ 1) for i in range(8)])

    def ctx_swap(x, bit):
        swap = ((1, 0, 3, 2), (3, 2, 1, 0))[bit % 2]
        if bit < 2:
            pairs = [(4 * y + i, 4 * y + swap[i]) for y in range(4) for i in range(4)]
        else:
            pairs = [(4 * i + x, 4 * swap[i] + x) for i in range(4) for x in range(4)]
        return lax.ppermute(x, "ctx", pairs)

    gains = jnp.broadcast_to(norm_gain[:, :, None], (heads, dh, CH))
    message = jnp.einsum("hse,hsd->hed", v, k, preferred_element_type=F32).astype(BF16)
    w_other = across_cores(out_weight)
    parts = [(0,), (1,), (2,), (3, 4)]
    sibs, accs = [], []
    for bit in range(4):
        got = ctx_swap(message, bit)
        tied, _ = lax.optimization_barrier((w, message))
        acc = local_part(q, k, v, tied, parts[bit])
        got, acc = lax.optimization_barrier((got, acc))
        if bit == 2:
            got, w_other = lax.optimization_barrier((got, w_other))
        sibs.append(got)
        accs.append(acc)
        if bit < 3:
            message = (message.astype(F32) + got.astype(F32)).astype(BF16)

    send1 = far_part(accs, parts, q, w, sibs, gains, 1, (2,))
    other1 = across_cores(send1)
    own1 = far_part(accs, parts, q, w, sibs, gains, 0, (2,))
    first_up = project(own1, other1, 0, out_weight, w_other, 0, half)
    first_down = project(own1, other1, 0, out_weight, w_other, half, half)
    late_q, first_up, first_down = lax.optimization_barrier((q, first_up, first_down))
    relay_up = along_z(first_up, 1)
    relay_down = along_z(first_down, -1)
    send2 = far_part(accs, parts, late_q, w, sibs, gains, 1, (1, 3, 0))
    other2 = across_cores(send2)
    own2 = far_part(accs, parts, late_q, w, sibs, gains, 0, (1, 3, 0))
    direct_up = along_z(project(own2, other2, 0, out_weight, w_other, half, half), 1)
    direct_down = along_z(project(own2, other2, 1, out_weight, w_other, 0, half), -1)
    joined_up = along_z(project(own2, other2, 0, out_weight, w_other, 0, half, ((relay_up, 0),)), 1)
    joined_down = along_z(project(own2, other2, 1, out_weight, w_other, half, half, ((relay_down, 0),)), -1)
    mine = project(
        own2, other2, 2, out_weight, w_other, 0, width, ((direct_down, 0), (direct_up, half)), F32
    )
    return finish(mine, joined_up, joined_down)


def solution(mesh):
    placed = (
        P("ctx", "head", None),
        P("ctx", "head", None),
        P("ctx", "head", None),
        P("ctx", "head", None),
        P("head", None),
        P("head", None),
    )
    return jax.shard_map(
        on_device, mesh=mesh, in_specs=placed, out_specs=P(("ctx", "head"), None), check_vma=False
    )
```

time: 124 us -> 82.5 us (0.67)
  Pallas kernels: 80.7 us -> 20.6 us
  waiting for transfers between devices: 9.85 us -> 32.8 us
  other arithmetic: 5.52 us -> 0.14 us
  local copies, waits for them, and re-layouts: 5.71 us -> 2.46 us
  starting transfers between devices: 21.2 us -> 23.8 us
  matrix products: 0 us -> 2.26 us
    pallas_call x16, Pallas kernels: 80.7 us -> 20.6 us  [the longest x7 9.29 us: project(): pl.pallas_call(lambda *refs: project_body(block, col_start, tile, places,...]
    ppermute x6, waiting for transfers between devices: 0.55 us -> 28 us  [along_z(): return lax.ppermute(x, 'head', pairs)]
    ppermute x4, waiting for transfers between devices: 8.05 us -> 3.58 us  [ctx_swap(): return lax.ppermute(x, 'ctx', pairs)]
    convert_element_type x6 -> x3, other arithmetic: 3.63 us -> 0.14 us  [on_device(): message = (message.astype(F32) + got.astype(F32)).astype(BF16)]
    unnamed x26 -> x16, local copies, waits for them, and re-layouts: 4.66 us -> 2.32 us
    dot_general x0 -> x1, matrix products: none -> 2.26 us  [on_device(): jnp.einsum('hse,hsd->hed', v, k, preferred_element_type=F32).astype(BF16)]
    concatenate x2 -> x0, other arithmetic: 1.8 us -> none  [the longest x1 1.18 us: on_device(): return jnp.concatenate([left, right], axis=1)]
  transfers between devices with their start and end apart: 13 -> 13, of which waited for: 4 -> 9; matrix products, arithmetic and copies ran while one was open for 3% -> 3% of each run, Pallas kernels for 61% -> 20%
where the time goes in v2:
time: 82.5 us; the launch traced here: 82.4 us
  waiting for transfers between devices  32.8 us (40%)
  starting transfers between devices  23.8 us (29%)
  Pallas kernels  20.6 us (25%)
  local copies, waits for them, and re-layouts  2.46 us (3%)
  matrix products  2.26 us (3%)
    ppermute x6, waiting for transfers between devices, along_z(): return lax.ppermute(x, 'head', pairs)  28 us
    pallas_call x7, Pallas kernels, project(): pl.pallas_call(lambda *refs: project_body(block, col_start, tile, places,...  9.29 us
    ppermute x4, starting transfers between devices, ctx_swap(): return lax.ppermute(x, 'ctx', pairs)  8.9 us
    ppermute x6, starting transfers between devices, along_z(): return lax.ppermute(x, 'head', pairs)  8.7 us
    pallas_call x4, Pallas kernels, local_part(): pl.pallas_call(lambda *refs: local_body(heads, *refs), in_specs=[VMEM] *...  7.17 us
    ppermute x3, starting transfers between devices, across_cores(): return lax.ppermute(x, 'head', [(i, i ^ 1) for i in range(8)])  6.19 us
    ppermute x4, waiting for transfers between devices, ctx_swap(): return lax.ppermute(x, 'ctx', pairs)  3.58 us
    pallas_call x4, Pallas kernels, far_part(): pl.pallas_call(body, in_specs=[VMEM] * (3 + bits + len(accs)), out_specs=...  2.49 us
  transfers between devices with their start and end apart: 13, of which 9 were waited for; matrix products, arithmetic and copies ran while one was open for 3% of the time, Pallas kernels for 20%

profile of v2, /device:TPU:1, one launch (start us, length us, event | category | flops | bytes accessed | tf_op | source)
XLA Modules:
  0.0 82.4 jit_solution(12070317590685357314)
XLA Ops:
  0.0 1.4 %collective-permute-start.3 = (bf16[640,5120]{1,0:T(8,128)(2,1)}, bf16[640,5120]{1,0:T(8,128)(2,1)S(1)}, u32[]{:S(2)}, u32[]{:S(2)}) collective-permute-start(bf16[640,5120]{1,0:T(8,128)(2,1)} %refs_2_.13), channel_id=1, source_target_pairs={{0,1},{1,0},{2,3},{3,2},{4,5},{5,4},{6,7},{7,6},{8,9},{9,8},{10,11... | collective-permute-start | bytes 19660808 | tf_op jit(solution)/shard_map/ppermute | solution.py:200
  1.4 2.3 %convolution_convert_fusion = bf16[5,128,128]{2,1,0:T(8,128)(2,1)S(1)} fusion(bf16[1024,5,128]{2,0,1:T(8,128)(2,1)} %param.7, bf16[1024,5,128]{2,0,1:T(8,128)(2,1)} %param.8), kind=kOutput, calls=%fused_computation | convolution fusion | flops 167854080 | bytes 2785280 | tf_op jit(solution)/shard_map/hse,hsd->hed/dot_general | solution.py:211
  3.7 1.5 %collective-permute-start = (bf16[5,128,128]{2,1,0:T(8,128)(2,1)S(1)}, bf16[5,128,128]{2,1,0:T(8,128)(2,1)S(1)}, u32[]{:S(2)}, u32[]{:S(2)}) collective-permute-start(bf16[5,128,128]{2,1,0:T(8,128)(2,1)S(1)} %convolution_convert_fusion), channel_id=1, source_target_pairs={{0,8},{8,0},{16,24},{24,16},{32,40},{40,32},{48,56},{56,48},{64,72... | collective-permute-start | bytes 491528 | tf_op jit(solution)/shard_map/ppermute | solution.py:208
  5.2 1.3 %copy-done.2 = bf16[1024,5,128]{2,0,1:T(8,128)(2,1)S(1)} copy-done((bf16[1024,5,128]{2,0,1:T(8,128)(2,1)S(1)}, bf16[1024,5,128]{2,0,1:T(8,128)(2,1)}, u32[]{:S(2)}) %copy-start.2) | copy-done | bytes 1310744
  7.5 1.5 %local_part.4.refs_4_ = f32[1,128,1024]{2,1,0:T(8,128)S(1)} custom-call(bf16[5,1024,128]{2,1,0:T(8,128)(2,1)S(1)} %bitcast.10, bf16[5,1024,128]{2,1,0:T(8,128)(2,1)S(1)} %bitcast.18, bf16[5,1024,128]{2,1,0:T(8,128)(2,1)S(1)} %bitcast.22, f32[5,16,1024]{2,1,0:T(8,128)S(1)} %bitcast.26), custom_call_target="tpu_custom_call" | custom-call | flops 167772160 | bytes 1310720 | tf_op jit(solution)/shard_map/local_part/pallas_call | solution.py:76
  9.5 2.9 %collective-permute-start.1 = (bf16[5,128,128]{2,1,0:T(8,128)(2,1)S(1)}, bf16[5,128,128]{2,1,0:T(8,128)(2,1)S(1)}, u32[]{:S(2)}, u32[]{:S(2)}) collective-permute-start(bf16[5,128,128]{2,1,0:T(8,128)(2,1)S(1)} %add_convert_fusion.2), channel_id=1, source_target_pairs={{0,24},{8,16},{16,8},{24,0},{32,56},{40,48},{48,40},{56,32},{64,88... | collective-permute-start | bytes 491528 | tf_op jit(solution)/shard_map/ppermute | solution.py:208
  12.3 1.5 %local_part.5.refs_5_ = f32[1,128,1024]{2,1,0:T(8,128)S(1)} custom-call(bf16[5,1024,128]{2,1,0:T(8,128)(2,1)S(1)} %bitcast.11, bf16[5,1024,128]{2,1,0:T(8,128)(2,1)S(1)} %bitcast.19, bf16[5,1024,128]{2,1,0:T(8,128)(2,1)S(1)} %bitcast.23, f32[5,16,1024]{2,1,0:T(8,128)S(1)} %bitcast.27), custom_call_target="tpu_custom_call" | custom-call | flops 167772160 | bytes 1310720 | tf_op jit(solution)/shard_map/local_part/pallas_call | solution.py:76
  13.8 1.9 %collective-permute-done.1.refs_1_ = bf16[5,128,128]{2,1,0:T(8,128)(2,1)S(1)} collective-permute-done((bf16[5,128,128]{2,1,0:T(8,128)(2,1)S(1)}, bf16[5,128,128]{2,1,0:T(8,128)(2,1)S(1)}, u32[]{:S(2)}, u32[]{:S(2)}) %collective-permute-start.1) | collective-permute-done | bytes 163872 | tf_op jit(solution)/shard_map/ppermute | solution.py:208
  15.8 1.6 %collective-permute-start.2 = (bf16[5,128,128]{2,1,0:T(8,128)(2,1)S(1)}, bf16[5,128,128]{2,1,0:T(8,128)(2,1)S(1)}, u32[]{:S(2)}, u32[]{:S(2)}) collective-permute-start(bf16[5,128,128]{2,1,0:T(8,128)(2,1)S(1)} %add_convert_fusion.1), channel_id=1, source_target_pairs={{0,32},{8,40},{16,48},{24,56},{32,0},{40,8},{48,16},{56,24},{64,96... | collective-permute-start | bytes 491528 | tf_op jit(solution)/shard_map/ppermute | solution.py:208
  17.4 1.5 %local_part.6.refs_6_ = f32[1,128,1024]{2,1,0:T(8,128)S(1)} custom-call(bf16[5,1024,128]{2,1,0:T(8,128)(2,1)S(1)} %bitcast.12, bf16[5,1024,128]{2,1,0:T(8,128)(2,1)S(1)} %bitcast.20, bf16[5,1024,128]{2,1,0:T(8,128)(2,1)S(1)} %bitcast.24, f32[5,16,1024]{2,1,0:T(8,128)S(1)} %bitcast.28), custom_call_target="tpu_custom_call" | custom-call | flops 167772160 | bytes 1310720 | tf_op jit(solution)/shard_map/local_part/pallas_call | solution.py:76
  18.9 1.2 %collective-permute-done.2.refs_2_ = bf16[5,128,128]{2,1,0:T(8,128)(2,1)S(1)} collective-permute-done((bf16[5,128,128]{2,1,0:T(8,128)(2,1)S(1)}, bf16[5,128,128]{2,1,0:T(8,128)(2,1)S(1)}, u32[]{:S(2)}, u32[]{:S(2)}) %collective-permute-start.2) | collective-permute-done | bytes 163872 | tf_op jit(solution)/shard_map/ppermute | solution.py:208
  20.2 3.0 %collective-permute-start.4 = (bf16[5,128,128]{2,1,0:T(8,128)(2,1)S(1)}, bf16[5,128,128]{2,1,0:T(8,128)(2,1)S(1)}, u32[]{:S(2)}, u32[]{:S(2)}) collective-permute-start(bf16[5,128,128]{2,1,0:T(8,128)(2,1)S(1)} %add_convert_fusion), channel_id=1, source_target_pairs={{0,96},{8,104},{16,112},{24,120},{32,64},{40,72},{48,80},{56,88},{... | collective-permute-start | bytes 491528 | tf_op jit(solution)/shard_map/ppermute | solution.py:208
  23.1 2.7 %local_part.7.refs_7_ = f32[2,128,1024]{2,1,0:T(8,128)S(1)} custom-call(bf16[5,1024,128]{2,1,0:T(8,128)(2,1)S(1)} %bitcast.13, bf16[5,1024,128]{2,1,0:T(8,128)(2,1)S(1)} %bitcast.21, bf16[5,1024,128]{2,1,0:T(8,128)(2,1)S(1)} %bitcast.25, f32[5,16,1024]{2,1,0:T(8,128)S(1)} %bitcast.29), custom_call_target="tpu_custom_call" | custom-call | flops 335544320 | bytes 2621440 | tf_op jit(solution)/shard_map/local_part/pallas_call | solution.py:76
  26.5 3.9 %collective-permute-start.5 = (bf16[1,128,640]{2,1,0:T(8,128)(2,1)S(1)}, bf16[1,128,640]{2,1,0:T(8,128)(2,1)S(1)}, u32[]{:S(2)}, u32[]{:S(2)}) collective-permute-start(bf16[1,128,640]{2,1,0:T(8,128)(2,1)S(1)} %far_part.5), channel_id=1, source_target_pairs={{0,1},{1,0},{2,3},{3,2},{4,5},{5,4},{6,7},{7,6},{8,9},{9,8},{10,11... | collective-permute-start | bytes 491528 | tf_op jit(solution)/shard_map/ppermute | solution.py:200
  33.8 1.9 %collective-permute-start.9 = (bf16[128,2560]{1,0:T(8,128)(2,1)S(1)}, bf16[128,2560]{1,0:T(8,128)(2,1)S(1)}, u32[]{:S(2)}, u32[]{:S(2)}) collective-permute-start(bf16[128,2560]{1,0:T(8,128)(2,1)S(1)} %project.7), channel_id=1, source_target_pairs={{0,2},{1,3},{2,4},{3,5},{4,6},{5,7},{6,0},{7,1},{8,10},{9,11},{10,... | collective-permute-start | bytes 1966088 | tf_op jit(solution)/shard_map/ppermute | solution.py:197
  35.6 2.2 %collective-permute-start.11 = (bf16[128,2560]{1,0:T(8,128)(2,1)S(1)}, bf16[128,2560]{1,0:T(8,128)(2,1)S(1)}, u32[]{:S(2)}, u32[]{:S(2)}) collective-permute-start(bf16[128,2560]{1,0:T(8,128)(2,1)S(1)} %project.8), channel_id=1, source_target_pairs={{0,6},{1,7},{2,0},{3,1},{4,2},{5,3},{6,4},{7,5},{8,14},{9,15},{10,... | collective-permute-start | bytes 1966088 | tf_op jit(solution)/shard_map/ppermute | solution.py:197
  42.2 1.7 %collective-permute-start.7 = (bf16[128,2560]{1,0:T(8,128)(2,1)S(1)}, bf16[128,2560]{1,0:T(8,128)(2,1)S(1)}, u32[]{:S(2)}, u32[]{:S(2)}) collective-permute-start(bf16[128,2560]{1,0:T(8,128)(2,1)S(1)} %project.9), channel_id=1, source_target_pairs={{0,6},{1,7},{2,0},{3,1},{4,2},{5,3},{6,4},{7,5},{8,14},{9,15},{10,... | collective-permute-start | bytes 1966088 | tf_op jit(solution)/shard_map/ppermute | solution.py:197
  45.3 7.3 %collective-permute-done.9.refs_4_ = bf16[128,2560]{1,0:T(8,128)(2,1)S(1)} collective-permute-done((bf16[128,2560]{1,0:T(8,128)(2,1)S(1)}, bf16[128,2560]{1,0:T(8,128)(2,1)S(1)}, u32[]{:S(2)}, u32[]{:S(2)}) %collective-permute-start.9) | collective-permute-done | bytes 655392 | tf_op jit(solution)/shard_map/ppermute | solution.py:197
  53.9 1.2 %project.13 = bf16[128,2560]{1,0:T(8,128)(2,1)S(1)} custom-call(bf16[3,128,640]{2,1,0:T(8,128)(2,1)S(1)} %far_part.6.refs_0_, bf16[3,128,640]{2,1,0:T(8,128)(2,1)S(1)} %collective-permute-done.6.refs_1_, bf16[640,5120]{1,0:T(8,128)(2,1)S(1)} %bitcast.9, bf16[640,5120]{1,0:T(8,128)(2,1)S(1)} %collective-permute-done.3.refs_3_, ...), custom_call_target="tpu_custom_call" | custom-call | flops 1000 | bytes 1000 | tf_op jit(solution)/shard_map/project/pallas_call | solution.py:145
  55.0 2.7 %collective-permute-start.12 = (bf16[128,2560]{1,0:T(8,128)(2,1)S(1)}, bf16[128,2560]{1,0:T(8,128)(2,1)S(1)}, u32[]{:S(2)}, u32[]{:S(2)}) collective-permute-start(bf16[128,2560]{1,0:T(8,128)(2,1)S(1)} %project.13), channel_id=1, source_target_pairs={{0,6},{1,7},{2,0},{3,1},{4,2},{5,3},{6,4},{7,5},{8,14},{9,15},{10,... | collective-permute-start | bytes 1966088 | tf_op jit(solution)/shard_map/ppermute | solution.py:197
  57.8 7.9 %collective-permute-done.7.refs_4_ = bf16[128,2560]{1,0:T(8,128)(2,1)S(1)} collective-permute-done((bf16[128,2560]{1,0:T(8,128)(2,1)S(1)}, bf16[128,2560]{1,0:T(8,128)(2,1)S(1)}, u32[]{:S(2)}, u32[]{:S(2)}) %collective-permute-start.7) | collective-permute-done | bytes 655392 | tf_op jit(solution)/shard_map/ppermute | solution.py:197
  66.6 2.2 %project.11.own_ref = f32[128,5120]{1,0:T(8,128)S(1)} custom-call(bf16[3,128,640]{2,1,0:T(8,128)(2,1)S(1)} %far_part.6.refs_0_, bf16[3,128,640]{2,1,0:T(8,128)(2,1)S(1)} %collective-permute-done.6.refs_1_, bf16[640,5120]{1,0:T(8,128)(2,1)S(1)} %bitcast.9, bf16[640,5120]{1,0:T(8,128)(2,1)S(1)} %collective-permute-done.3.refs_3_, ...), custom_call_target="tpu_custom_call" | custom-call | flops 1000 | bytes 1000 | tf_op jit(solution)/shard_map/project/pallas_call | solution.py:145
  68.8 11.8 %collective-permute-done.10.left_ref = bf16[128,2560]{1,0:T(8,128)(2,1)S(1)} collective-permute-done((bf16[128,2560]{1,0:T(8,128)(2,1)S(1)}, bf16[128,2560]{1,0:T(8,128)(2,1)S(1)}, u32[]{:S(2)}, u32[]{:S(2)}) %collective-permute-start.10) | collective-permute-done | bytes 655392 | tf_op jit(solution)/shard_map/ppermute | solution.py:197
  80.7 1.7 %finish.1 = bf16[128,5120]{1,0:T(8,128)(2,1)} custom-call(f32[128,5120]{1,0:T(8,128)S(1)} %project.11.own_ref, bf16[128,2560]{1,0:T(8,128)(2,1)S(1)} %collective-permute-done.10.left_ref, bf16[128,2560]{1,0:T(8,128)(2,1)S(1)} %collective-permute-done.12.right_ref), custom_call_target="tpu_custom_call" | custom-call | flops 655360 | bytes 6553600 | tf_op jit(solution)/shard_map/finish/pallas_call | solution.py:174
  (40 shorter events, 13.4 us)
Async XLA Ops:
  0.0 5.2 %copy-start.1 = (bf16[1024,5,128]{2,0,1:T(8,128)(2,1)S(1)}, bf16[1024,5,128]{2,0,1:T(8,128)(2,1)}, u32[]{:S(2)}) copy-start(bf16[1024,5,128]{2,0,1:T(8,128)(2,1)} %param.7) | copy-start | bytes 3932164
  0.0 5.2 %copy-start = (bf16[1024,5,128]{2,0,1:T(8,128)(2,1)S(1)}, bf16[1024,5,128]{2,0,1:T(8,128)(2,1)}, u32[]{:S(2)}) copy-start(bf16[1024,5,128]{2,0,1:T(8,128)(2,1)} %param.6) | copy-start | bytes 3932164
  0.0 20.1 %collective-permute-start.3 = (bf16[640,5120]{1,0:T(8,128)(2,1)}, bf16[640,5120]{1,0:T(8,128)(2,1)S(1)}, u32[]{:S(2)}, u32[]{:S(2)}) collective-permute-start(bf16[640,5120]{1,0:T(8,128)(2,1)} %refs_2_.13), channel_id=1, source_target_pairs={{0,1},{1,0},{2,3},{3,2},{4,5},{5,4},{6,7},{7,6},{8,9},{9,8},{10,11... | collective-permute-start | bytes 19660808 | tf_op jit(solution)/shard_map/ppermute | solution.py:200
  3.7 5.7 %collective-permute-start = (bf16[5,128,128]{2,1,0:T(8,128)(2,1)S(1)}, bf16[5,128,128]{2,1,0:T(8,128)(2,1)S(1)}, u32[]{:S(2)}, u32[]{:S(2)}) collective-permute-start(bf16[5,128,128]{2,1,0:T(8,128)(2,1)S(1)} %convolution_convert_fusion), channel_id=1, source_target_pairs={{0,8},{8,0},{16,24},{24,16},{32,40},{40,32},{48,56},{56,48},{64,72... | collective-permute-start | bytes 491528 | tf_op jit(solution)/shard_map/ppermute | solution.py:208
  5.2 1.3 %copy-start.2 = (bf16[1024,5,128]{2,0,1:T(8,128)(2,1)S(1)}, bf16[1024,5,128]{2,0,1:T(8,128)(2,1)}, u32[]{:S(2)}) copy-start(bf16[1024,5,128]{2,0,1:T(8,128)(2,1)} %param.8) | copy-start | bytes 3932164
  6.5 1.0 %copy-start.3 = (f32[1024,5,16]{0,2,1:T(8,128)S(1)}, f32[1024,5,16]{0,2,1:T(8,128)}, u32[]{:S(2)}) copy-start(f32[1024,5,16]{0,2,1:T(8,128)} %param.9) | copy-start | bytes 983044
  9.5 6.3 %collective-permute-start.1 = (bf16[5,128,128]{2,1,0:T(8,128)(2,1)S(1)}, bf16[5,128,128]{2,1,0:T(8,128)(2,1)S(1)}, u32[]{:S(2)}, u32[]{:S(2)}) collective-permute-start(bf16[5,128,128]{2,1,0:T(8,128)(2,1)S(1)} %add_convert_fusion.2), channel_id=1, source_target_pairs={{0,24},{8,16},{16,8},{24,0},{32,56},{40,48},{48,40},{56,32},{64,88... | collective-permute-start | bytes 491528 | tf_op jit(solution)/shard_map/ppermute | solution.py:208
  15.8 4.3 %collective-permute-start.2 = (bf16[5,128,128]{2,1,0:T(8,128)(2,1)S(1)}, bf16[5,128,128]{2,1,0:T(8,128)(2,1)S(1)}, u32[]{:S(2)}, u32[]{:S(2)}) collective-permute-start(bf16[5,128,128]{2,1,0:T(8,128)(2,1)S(1)} %add_convert_fusion.1), channel_id=1, source_target_pairs={{0,32},{8,40},{16,48},{24,56},{32,0},{40,8},{48,16},{56,24},{64,96... | collective-permute-start | bytes 491528 | tf_op jit(solution)/shard_map/ppermute | solution.py:208
  20.1 5.7 %copy-start.5 = (f32[5,128]{1,0:T(8,128)S(1)}, f32[5,128]{1,0:T(8,128)}, u32[]{:S(2)}) copy-start(f32[5,128]{1,0:T(8,128)} %param.10) | copy-start | bytes 7684
  20.2 5.7 %collective-permute-start.4 = (bf16[5,128,128]{2,1,0:T(8,128)(2,1)S(1)}, bf16[5,128,128]{2,1,0:T(8,128)(2,1)S(1)}, u32[]{:S(2)}, u32[]{:S(2)}) collective-permute-start(bf16[5,128,128]{2,1,0:T(8,128)(2,1)S(1)} %add_convert_fusion), channel_id=1, source_target_pairs={{0,96},{8,104},{16,112},{24,120},{32,64},{40,72},{48,80},{56,88},{... | collective-permute-start | bytes 491528 | tf_op jit(solution)/shard_map/ppermute | solution.py:208
  23.1 8.2 %slice-start = ((s8[6553600]{0:T(1024)(128)(4,1)}), s8[4194304]{0:T(1024)(128)(4,1)S(1)}, s32[]{:S(2)}) async-start(s8[6553600]{0:T(1024)(128)(4,1)} %bitcast.8), calls=%async_computation | async-start | bytes 8388608
  26.0 5.4 %slice-start.1 = ((s8[6553600]{0:T(1024)(128)(4,1)}), s8[2359296]{0:T(1024)(128)(4,1)S(1)}, s32[]{:S(2)}) async-start(s8[6553600]{0:T(1024)(128)(4,1)} %bitcast.8), calls=%async_computation.1 | async-start | bytes 4718592
  26.5 4.9 %collective-permute-start.5 = (bf16[1,128,640]{2,1,0:T(8,128)(2,1)S(1)}, bf16[1,128,640]{2,1,0:T(8,128)(2,1)S(1)}, u32[]{:S(2)}, u32[]{:S(2)}) collective-permute-start(bf16[1,128,640]{2,1,0:T(8,128)(2,1)S(1)} %far_part.5), channel_id=1, source_target_pairs={{0,1},{1,0},{2,3},{3,2},{4,5},{5,4},{6,7},{7,6},{8,9},{9,8},{10,11... | collective-permute-start | bytes 491528 | tf_op jit(solution)/shard_map/ppermute | solution.py:200
  32.5 5.3 %copy-start.4 = (f32[1024,5,16]{0,2,1:T(8,128)S(1)}, f32[1024,5,16]{0,2,1:T(8,128)}, u32[]{:S(2)}) copy-start(f32[1024,5,16]{0,2,1:T(8,128)} %param.9) | copy-start | bytes 983044
  33.8 18.8 %collective-permute-start.9 = (bf16[128,2560]{1,0:T(8,128)(2,1)S(1)}, bf16[128,2560]{1,0:T(8,128)(2,1)S(1)}, u32[]{:S(2)}, u32[]{:S(2)}) collective-permute-start(bf16[128,2560]{1,0:T(8,128)(2,1)S(1)} %project.7), channel_id=1, source_target_pairs={{0,2},{1,3},{2,4},{3,5},{4,6},{5,7},{6,0},{7,1},{8,10},{9,11},{10,... | collective-permute-start | bytes 1966088 | tf_op jit(solution)/shard_map/ppermute | solution.py:197
  35.6 18.2 %collective-permute-start.11 = (bf16[128,2560]{1,0:T(8,128)(2,1)S(1)}, bf16[128,2560]{1,0:T(8,128)(2,1)S(1)}, u32[]{:S(2)}, u32[]{:S(2)}) collective-permute-start(bf16[128,2560]{1,0:T(8,128)(2,1)S(1)} %project.8), channel_id=1, source_target_pairs={{0,6},{1,7},{2,0},{3,1},{4,2},{5,3},{6,4},{7,5},{8,14},{9,15},{10,... | collective-permute-start | bytes 1966088 | tf_op jit(solution)/shard_map/ppermute | solution.py:197
  38.7 2.4 %collective-permute-start.6 = (bf16[3,128,640]{2,1,0:T(8,128)(2,1)S(1)}, bf16[3,128,640]{2,1,0:T(8,128)(2,1)S(1)}, u32[]{:S(2)}, u32[]{:S(2)}) collective-permute-start(bf16[3,128,640]{2,1,0:T(8,128)(2,1)S(1)} %far_part.7), channel_id=1, source_target_pairs={{0,1},{1,0},{2,3},{3,2},{4,5},{5,4},{6,7},{7,6},{8,9},{9,8},{10,11... | collective-permute-start | bytes 1474568 | tf_op jit(solution)/shard_map/ppermute | solution.py:200
  42.2 23.4 %collective-permute-start.7 = (bf16[128,2560]{1,0:T(8,128)(2,1)S(1)}, bf16[128,2560]{1,0:T(8,128)(2,1)S(1)}, u32[]{:S(2)}, u32[]{:S(2)}) collective-permute-start(bf16[128,2560]{1,0:T(8,128)(2,1)S(1)} %project.9), channel_id=1, source_target_pairs={{0,6},{1,7},{2,0},{3,1},{4,2},{5,3},{6,4},{7,5},{8,14},{9,15},{10,... | collective-permute-start | bytes 1966088 | tf_op jit(solution)/shard_map/ppermute | solution.py:197
  45.2 21.4 %collective-permute-start.8 = (bf16[128,2560]{1,0:T(8,128)(2,1)S(1)}, bf16[128,2560]{1,0:T(8,128)(2,1)S(1)}, u32[]{:S(2)}, u32[]{:S(2)}) collective-permute-start(bf16[128,2560]{1,0:T(8,128)(2,1)S(1)} %project.10), channel_id=1, source_target_pairs={{0,2},{1,3},{2,4},{3,5},{4,6},{5,7},{6,0},{7,1},{8,10},{9,11},{10,... | collective-permute-start | bytes 1966088 | tf_op jit(solution)/shard_map/ppermute | solution.py:197
  53.8 26.9 %collective-permute-start.10 = (bf16[128,2560]{1,0:T(8,128)(2,1)S(1)}, bf16[128,2560]{1,0:T(8,128)(2,1)S(1)}, u32[]{:S(2)}, u32[]{:S(2)}) collective-permute-start(bf16[128,2560]{1,0:T(8,128)(2,1)S(1)} %project.12), channel_id=1, source_target_pairs={{0,2},{1,3},{2,4},{3,5},{4,6},{5,7},{6,0},{7,1},{8,10},{9,11},{10,... | collective-permute-start | bytes 1966088 | tf_op jit(solution)/shard_map/ppermute | solution.py:197
  55.0 25.6 %collective-permute-start.12 = (bf16[128,2560]{1,0:T(8,128)(2,1)S(1)}, bf16[128,2560]{1,0:T(8,128)(2,1)S(1)}, u32[]{:S(2)}, u32[]{:S(2)}) collective-permute-start(bf16[128,2560]{1,0:T(8,128)(2,1)S(1)} %project.13), channel_id=1, source_target_pairs={{0,6},{1,7},{2,0},{3,1},{4,2},{5,3},{6,4},{7,5},{8,14},{9,15},{10,... | collective-permute-start | bytes 1966088 | tf_op jit(solution)/shard_map/ppermute | solution.py:197

commit v3 on v2

v3 whole, which is shorter than its diff:
```python
import jax
import jax.numpy as jnp
from jax import lax
from jax.experimental import pallas as pl
from jax.experimental.pallas import tpu as pltpu
from jax.sharding import PartitionSpec as P

CH = 128
F32 = jnp.float32
BF16 = jnp.bfloat16
VMEM = pl.BlockSpec(memory_space=pltpu.VMEM)
LOCAL_LEVELS = CH.bit_length()
FINISH_TILE = 1280
MINE_FLOPS = 1000
FAR_FLOPS = 1000


def dot00(a, b):
    return lax.dot_general(a, b, (((0,), (0,)), ((), ())), preferred_element_type=F32)


def dot11(a, b):
    return lax.dot_general(a, b, (((1,), (1,)), ((), ())), preferred_element_type=F32)


def cost(flops, byte_count):
    return pl.CostEstimate(flops=flops, bytes_accessed=byte_count, transcendentals=0)


def vmem(megabytes):
    return pltpu.CompilerParams(vmem_limit_bytes=megabytes << 20)


def local_body(heads, q_ref, k_ref, v_ref, w_ref, out_ref):
    stretches = q_ref.shape[1] // CH
    key_pos = lax.broadcasted_iota(jnp.int32, (CH, CH), 0)
    tok_pos = lax.broadcasted_iota(jnp.int32, (CH, CH), 1)
    dist = jnp.bitwise_xor(key_pos, tok_pos)
    level = jnp.zeros((CH, CH), jnp.int32)
    for bit in range(LOCAL_LEVELS - 1):
        level = level + (dist >= (1 << bit)).astype(jnp.int32)
    level = jnp.where(key_pos <= tok_pos, level, -1)
    for slot, h in enumerate(heads):
        states = []
        for c in range(stretches):
            rows = slice(c * CH, (c + 1) * CH)
            q, k, v = q_ref[h, rows, :], k_ref[h, rows, :], v_ref[h, rows, :]
            weights = w_ref[h, :, rows]
            mix = jnp.zeros((CH, CH), F32)
            for lev in range(LOCAL_LEVELS):
                mix = jnp.where(level == lev, weights[lev : lev + 1, :], mix)
            lefts, levs = [], []
            span, step = 1, 0
            while span < stretches:
                if c & span:
                    base = (c // (2 * span)) * 2 * span
                    left = states[base]
                    for other in range(base + 1, base + span):
                        left = left + states[other]
                    lefts.append(left.astype(BF16))
                    levs.append(LOCAL_LEVELS + step)
                span, step = span * 2, step + 1
            read = dot11(jnp.concatenate([k] + lefts, axis=0), q)
            probs = (read[:CH] * mix).astype(BF16)
            if c < stretches - 1:
                both = dot00(v, jnp.concatenate([probs, k], axis=1))
                total = both[:, :CH]
                states.append(both[:, CH:])
            else:
                total = dot00(v, probs)
            for i, lev in enumerate(levs):
                total = total + read[(1 + i) * CH : (2 + i) * CH] * weights[lev : lev + 1, :]
            out_ref[slot, :, rows] = total


def local_part(queries, keys, values, weights, heads, held=()):
    _, toks, dh = queries.shape
    count = len(heads)
    return pl.pallas_call(
        lambda *refs: local_body(heads, *refs[:4], refs[-1]),
        in_specs=[VMEM] * (4 + len(held)),
        out_specs=VMEM,
        out_shape=jax.ShapeDtypeStruct((count, dh, toks), F32),
        cost_estimate=cost(10 * count * toks * dh * dh, 10 * count * toks * dh),
        compiler_params=vmem(16),
        name="local_part",
    )(queries, keys, values, weights, *held)


def far_body(parts, first, away, steps, q_ref, w_ref, gain_ref, sib_refs, acc_refs, out_ref):
    ctx, place = lax.axis_index("ctx"), lax.axis_index("head")
    z, side = place // 2, (place + away) % 2
    bits = [((ctx >> bit) & 1).astype(F32) for bit in range(4)]
    for j, step in enumerate(steps):
        start = pl.multiple_of((2 * ((z + step) % 4) + side) * CH, CH)
        span = pl.ds(start, CH)
        for a, group in enumerate(parts):
            for slot, h in enumerate(group):
                sib = jnp.concatenate([ref[h] for ref in sib_refs], axis=0)
                read = dot11(sib, q_ref[h, span, :])
                total = acc_refs[a][slot, :, span]
                for bit, scale in enumerate(bits):
                    row = w_ref[h, first + bit : first + bit + 1, span] * scale
                    total = total + read[bit * CH : (bit + 1) * CH] * row
                mean_sq = jnp.mean(total * total, axis=0, keepdims=True)
                normed = total * lax.rsqrt(mean_sq + 1e-06) * gain_ref[h]
                out_ref[j, :, h * CH : (h + 1) * CH] = normed.astype(BF16).T


def far_part(accs, parts, queries, weights, sibs, gains, away, steps, flops=1000):
    heads, toks, dh = queries.shape
    count = len(steps)
    first = LOCAL_LEVELS + (toks // CH).bit_length() - 1
    held = len(sibs)

    def body(q_ref, w_ref, gain_ref, *refs):
        far_body(parts, first, away, steps, q_ref, w_ref, gain_ref, refs[:held], refs[held:-1], refs[-1])

    return pl.pallas_call(
        body,
        in_specs=[VMEM] * (3 + held + len(accs)),
        out_specs=VMEM,
        out_shape=jax.ShapeDtypeStruct((count, CH, heads * dh), BF16),
        cost_estimate=cost(flops, 1000),
        compiler_params=vmem(16),
        name="far_part",
    )(queries, weights, gains, *sibs, *accs)


def tiles_of(cols, tile=512):
    return [(n, min(tile, cols - n)) for n in range(0, cols, tile)]


def project_body(pairs, col_start, adds, refs):
    out_ref = refs[-1]
    sources = refs[2 * len(pairs) : -1]
    cuts = sorted({0, out_ref.shape[1], *adds})
    places = [(lo + n, size) for lo, hi in zip(cuts, cuts[1:]) for n, size in tiles_of(hi - lo)]
    for n, size in places:
        there = slice(col_start + n, col_start + n + size)
        total = None
        for i, block in enumerate(pairs):
            part = jnp.dot(refs[2 * i][block], refs[2 * i + 1][:, there], preferred_element_type=F32)
            total = part if total is None else total + part
        for source, lo in zip(sources, adds):
            if lo <= n < lo + source.shape[1]:
                total = total + source[:, n - lo : n - lo + size].astype(F32)
        out_ref[:, n : n + size] = total.astype(out_ref.dtype)


def project(pairs, col_start, cols, adds=(), out_dtype=BF16, flops=1000):
    rows = pairs[0][0].shape[1]
    blocks = [block for _, block, _ in pairs]
    args = [x for value, _, weight in pairs for x in (value, weight)]
    return pl.pallas_call(
        lambda *refs: project_body(blocks, col_start, [lo for _, lo in adds], refs),
        in_specs=[VMEM] * (len(args) + len(adds)),
        out_specs=VMEM,
        out_shape=jax.ShapeDtypeStruct((rows, cols), out_dtype),
        cost_estimate=cost(flops, 1000),
        compiler_params=vmem(24),
        name="project",
    )(*args, *[x for x, _ in adds])


def finish_body(own_ref, right_ref, left_ref, out_ref, hold_ref, sems):
    split = left_ref.shape[1]
    copies = []
    for late_ref, start in ((left_ref, 0), (right_ref, split)):
        for n, size in tiles_of(late_ref.shape[1], FINISH_TILE):
            there = slice(start + n, start + n + size)
            total = own_ref[:, there] + late_ref[:, n : n + size].astype(F32)
            hold_ref[:, there] = total.astype(BF16)
            i = len(copies)
            copies.append(pltpu.make_async_copy(hold_ref.at[:, there], out_ref.at[:, there], sems.at[i]))
            copies[-1].start()
    for copy in copies:
        copy.wait()


def finish(own, left, right):
    rows, width = own.shape
    count = len(tiles_of(left.shape[1], FINISH_TILE)) + len(tiles_of(right.shape[1], FINISH_TILE))
    return pl.pallas_call(
        finish_body,
        in_specs=[VMEM] * 3,
        out_specs=pl.BlockSpec(memory_space=pl.ANY),
        out_shape=jax.ShapeDtypeStruct((rows, width), BF16),
        scratch_shapes=[pltpu.VMEM((rows, width), BF16), pltpu.SemaphoreType.DMA((count,))],
        cost_estimate=cost(1000, 1000),
        compiler_params=vmem(16),
        name="finish",
    )(own, right, left)


def on_device(queries, key_rows, value_rows, level_weight, norm_gain, out_weight):
    toks, heads, dh = queries.shape
    q = jnp.transpose(queries, (1, 0, 2))
    k = jnp.transpose(key_rows, (1, 0, 2))
    v = jnp.transpose(value_rows, (1, 0, 2))
    w = jnp.transpose(level_weight, (1, 2, 0))
    width = out_weight.shape[1]
    split = width // 2
    rest = width - split

    def along_z(x, step):
        pairs = [(2 * i + c, 2 * ((i + step) % 4) + c) for i in range(4) for c in range(2)]
        return lax.ppermute(x, "head", pairs)

    def across_cores(x):
        return lax.ppermute(x, "head", [(i, i ^ 1) for i in range(8)])

    def ctx_swap(x, bit):
        swap = ((1, 0, 3, 2), (3, 2, 1, 0))[bit % 2]
        if bit < 2:
            pairs = [(4 * y + i, 4 * y + swap[i]) for y in range(4) for i in range(4)]
        else:
            pairs = [(4 * i + x, 4 * swap[i] + x) for i in range(4) for x in range(4)]
        return lax.ppermute(x, "ctx", pairs)

    gains = jnp.broadcast_to(norm_gain[:, :, None], (heads, dh, CH))
    message = jnp.einsum("hse,hsd->hed", v, k, preferred_element_type=F32).astype(BF16)
    w_other = across_cores(out_weight)
    parts = [(0,), (1,), (2,), (3, 4)]
    sibs, accs = [], []
    for bit in range(4):
        got = ctx_swap(message, bit)
        tied, _ = lax.optimization_barrier((w, message))
        held = (out_weight,) if bit == 2 else ()
        got, acc = lax.optimization_barrier((got, local_part(q, k, v, tied, parts[bit], held)))
        if bit == 2:
            got, w_other = lax.optimization_barrier((got, w_other))
        sibs.append(got)
        accs.append(acc)
        if bit < 3:
            message = (message.astype(F32) + got.astype(F32)).astype(BF16)

    send1 = far_part(accs, parts, q, w, sibs, gains, 1, (2,))
    other1 = across_cores(send1)
    own1 = far_part(accs, parts, q, w, sibs, gains, 0, (2,))
    early_up = project([(own1, 0, out_weight)], 0, split, (), F32)
    early_down = project([(own1, 0, out_weight)], split, rest, (), F32)
    first_up = project([(other1, 0, w_other)], 0, split, ((early_up, 0),))
    late_other, first_up = lax.optimization_barrier((other1, first_up))
    first_down = project([(late_other, 0, w_other)], split, rest, ((early_down, 0),))
    late_q, first_down = lax.optimization_barrier((q, first_down))
    relay_up = along_z(first_up, 1)
    relay_down = along_z(first_down, -1)
    send2 = far_part(accs, parts, late_q, w, sibs, gains, 1, (1, 3, 0))
    other2 = across_cores(send2)
    own2 = far_part(accs, parts, late_q, w, sibs, gains, 0, (1, 3, 0), FAR_FLOPS)

    def block(i):
        return [(own2, i, out_weight), (other2, i, w_other)]

    next_up = project(block(0), split, rest)
    next_down = project(block(1), 0, split)
    direct_up = along_z(next_up, 1)
    direct_down = along_z(next_down, -1)
    joined_up = along_z(project(block(0), 0, split, ((relay_up, 0),)), 1)
    joined_down = along_z(project(block(1), split, rest, ((relay_down, 0),)), -1)
    mine = project(block(2), 0, width, ((direct_down, 0), (direct_up, split)), F32, MINE_FLOPS)
    return finish(mine, joined_up, joined_down)


def solution(mesh):
    placed = (
        P("ctx", "head", None),
        P("ctx", "head", None),
        P("ctx", "head", None),
        P("ctx", "head", None),
        P("head", None),
        P("head", None),
    )
    return jax.shard_map(
        on_device, mesh=mesh, in_specs=placed, out_specs=P(("ctx", "head"), None), check_vma=False
    )
```

time: 82.5 us -> 82.2 us (level)
    ppermute x6, starting transfers between devices: 8.7 us -> 9.57 us  [along_z(): return lax.ppermute(x, 'head', pairs)]
    pallas_call x16 -> x18, Pallas kernels: 20.6 us -> 20.4 us  [the longest x9 9.66 us: project(): pl.pallas_call(lambda *refs: project_body(blocks, col_start, [lo for _, l...]
  transfers between devices with their start and end apart: 13 -> 13, of which waited for: 9 -> 7; matrix products, arithmetic and copies ran while one was open for 3% -> 3% of each run, Pallas kernels for 20% -> 21%
where the time goes in v3:
time: 82.2 us; the launch traced here: 82.1 us
  waiting for transfers between devices  32.4 us (39%)
  starting transfers between devices  23.8 us (29%)
  Pallas kernels  20.4 us (25%)
  local copies, waits for them, and re-layouts  2.45 us (3%)
  matrix products  2.41 us (3%)
    ppermute x6, waiting for transfers between devices, along_z(): return lax.ppermute(x, 'head', pairs)  27.5 us
    pallas_call x9, Pallas kernels, project(): pl.pallas_call(lambda *refs: project_body(blocks, col_start, [lo for _, l...  9.66 us
    ppermute x6, starting transfers between devices, along_z(): return lax.ppermute(x, 'head', pairs)  9.57 us
    ppermute x4, starting transfers between devices, ctx_swap(): return lax.ppermute(x, 'ctx', pairs)  8.33 us
    pallas_call x4, Pallas kernels, local_part(): pl.pallas_call(lambda *refs: local_body(heads, *refs[:4], refs[-1]), in_s...  7.17 us
    ppermute x3, starting transfers between devices, across_cores(): return lax.ppermute(x, 'head', [(i, i ^ 1) for i in range(8)])  5.92 us
    ppermute x4, waiting for transfers between devices, ctx_swap(): return lax.ppermute(x, 'ctx', pairs)  4.13 us
    pallas_call x4, Pallas kernels, far_part(): pl.pallas_call(body, in_specs=[VMEM] * (3 + held + len(accs)), out_specs=...  2.48 us
  transfers between devices with their start and end apart: 13, of which 7 were waited for; matrix products, arithmetic and copies ran while one was open for 3% of the time, Pallas kernels for 21%

profile of v3, /device:TPU:1, one launch (start us, length us, event | category | flops | bytes accessed | tf_op | source)
XLA Modules:
  0.0 82.1 jit_solution(11910930181942778075)
XLA Ops:
  0.0 1.4 %collective-permute-start.3 = (bf16[640,5120]{1,0:T(8,128)(2,1)}, bf16[640,5120]{1,0:T(8,128)(2,1)S(1)}, u32[]{:S(2)}, u32[]{:S(2)}) collective-permute-start(bf16[640,5120]{1,0:T(8,128)(2,1)} %refs_1_.13), channel_id=1, source_target_pairs={{0,1},{1,0},{2,3},{3,2},{4,5},{5,4},{6,7},{7,6},{8,9},{9,8},{10,11... | collective-permute-start | bytes 19660808 | tf_op jit(solution)/shard_map/ppermute | solution.py:211
  1.4 2.4 %convolution_convert_fusion = bf16[5,128,128]{2,1,0:T(8,128)(2,1)S(1)} fusion(bf16[1024,5,128]{2,0,1:T(8,128)(2,1)} %param.7, bf16[1024,5,128]{2,0,1:T(8,128)(2,1)} %param.8), kind=kOutput, calls=%fused_computation | convolution fusion | flops 167854080 | bytes 2785280 | tf_op jit(solution)/shard_map/hse,hsd->hed/dot_general | solution.py:222
  3.8 1.4 %collective-permute-start = (bf16[5,128,128]{2,1,0:T(8,128)(2,1)S(1)}, bf16[5,128,128]{2,1,0:T(8,128)(2,1)S(1)}, u32[]{:S(2)}, u32[]{:S(2)}) collective-permute-start(bf16[5,128,128]{2,1,0:T(8,128)(2,1)S(1)} %convolution_convert_fusion), channel_id=1, source_target_pairs={{0,8},{8,0},{16,24},{24,16},{32,40},{40,32},{48,56},{56,48},{64,72... | collective-permute-start | bytes 491528 | tf_op jit(solution)/shard_map/ppermute | solution.py:219
  5.2 1.3 %copy-done.2 = bf16[1024,5,128]{2,0,1:T(8,128)(2,1)S(1)} copy-done((bf16[1024,5,128]{2,0,1:T(8,128)(2,1)S(1)}, bf16[1024,5,128]{2,0,1:T(8,128)(2,1)}, u32[]{:S(2)}) %copy-start.2) | copy-done | bytes 1310744
  7.5 1.5 %local_part.4.refs_4_ = f32[1,128,1024]{2,1,0:T(8,128)S(1)} custom-call(bf16[5,1024,128]{2,1,0:T(8,128)(2,1)S(1)} %bitcast.10, bf16[5,1024,128]{2,1,0:T(8,128)(2,1)S(1)} %bitcast.18, bf16[5,1024,128]{2,1,0:T(8,128)(2,1)S(1)} %bitcast.22, f32[5,16,1024]{2,1,0:T(8,128)S(1)} %bitcast.26), custom_call_target="tpu_custom_call" | custom-call | flops 167772160 | bytes 1310720 | tf_op jit(solution)/shard_map/local_part/pallas_call | solution.py:79
  9.8 2.6 %collective-permute-start.1 = (bf16[5,128,128]{2,1,0:T(8,128)(2,1)S(1)}, bf16[5,128,128]{2,1,0:T(8,128)(2,1)S(1)}, u32[]{:S(2)}, u32[]{:S(2)}) collective-permute-start(bf16[5,128,128]{2,1,0:T(8,128)(2,1)S(1)} %add_convert_fusion.2), channel_id=1, source_target_pairs={{0,24},{8,16},{16,8},{24,0},{32,56},{40,48},{48,40},{56,32},{64,88... | collective-permute-start | bytes 491528 | tf_op jit(solution)/shard_map/ppermute | solution.py:219
  12.4 1.5 %local_part.5.refs_5_ = f32[1,128,1024]{2,1,0:T(8,128)S(1)} custom-call(bf16[5,1024,128]{2,1,0:T(8,128)(2,1)S(1)} %bitcast.11, bf16[5,1024,128]{2,1,0:T(8,128)(2,1)S(1)} %bitcast.19, bf16[5,1024,128]{2,1,0:T(8,128)(2,1)S(1)} %bitcast.23, f32[5,16,1024]{2,1,0:T(8,128)S(1)} %bitcast.27), custom_call_target="tpu_custom_call" | custom-call | flops 167772160 | bytes 1310720 | tf_op jit(solution)/shard_map/local_part/pallas_call | solution.py:79
  13.9 2.1 %collective-permute-done.1.refs_1_ = bf16[5,128,128]{2,1,0:T(8,128)(2,1)S(1)} collective-permute-done((bf16[5,128,128]{2,1,0:T(8,128)(2,1)S(1)}, bf16[5,128,128]{2,1,0:T(8,128)(2,1)S(1)}, u32[]{:S(2)}, u32[]{:S(2)}) %collective-permute-start.1) | collective-permute-done | bytes 163872 | tf_op jit(solution)/shard_map/ppermute | solution.py:219
  16.1 1.4 %collective-permute-start.2 = (bf16[5,128,128]{2,1,0:T(8,128)(2,1)S(1)}, bf16[5,128,128]{2,1,0:T(8,128)(2,1)S(1)}, u32[]{:S(2)}, u32[]{:S(2)}) collective-permute-start(bf16[5,128,128]{2,1,0:T(8,128)(2,1)S(1)} %add_convert_fusion.1), channel_id=1, source_target_pairs={{0,32},{8,40},{16,48},{24,56},{32,0},{40,8},{48,16},{56,24},{64,96... | collective-permute-start | bytes 491528 | tf_op jit(solution)/shard_map/ppermute | solution.py:219
  17.5 1.5 %local_part.6.refs_6_ = f32[1,128,1024]{2,1,0:T(8,128)S(1)} custom-call(bf16[5,1024,128]{2,1,0:T(8,128)(2,1)S(1)} %bitcast.12, bf16[5,1024,128]{2,1,0:T(8,128)(2,1)S(1)} %bitcast.20, bf16[5,1024,128]{2,1,0:T(8,128)(2,1)S(1)} %bitcast.24, f32[5,16,1024]{2,1,0:T(8,128)S(1)} %bitcast.28, bf16[640,5120]{1,0:T(8,128)(2,1)S(1)} %bitcast.9), custom_call_target="tpu_custom_call" | custom-call | flops 167772160 | bytes 1310720 | tf_op jit(solution)/shard_map/local_part/pallas_call | solution.py:79
  19.0 1.3 %collective-permute-done.2.refs_2_ = bf16[5,128,128]{2,1,0:T(8,128)(2,1)S(1)} collective-permute-done((bf16[5,128,128]{2,1,0:T(8,128)(2,1)S(1)}, bf16[5,128,128]{2,1,0:T(8,128)(2,1)S(1)}, u32[]{:S(2)}, u32[]{:S(2)}) %collective-permute-start.2) | collective-permute-done | bytes 163872 | tf_op jit(solution)/shard_map/ppermute | solution.py:219
  20.4 2.9 %collective-permute-start.4 = (bf16[5,128,128]{2,1,0:T(8,128)(2,1)S(1)}, bf16[5,128,128]{2,1,0:T(8,128)(2,1)S(1)}, u32[]{:S(2)}, u32[]{:S(2)}) collective-permute-start(bf16[5,128,128]{2,1,0:T(8,128)(2,1)S(1)} %add_convert_fusion), channel_id=1, source_target_pairs={{0,96},{8,104},{16,112},{24,120},{32,64},{40,72},{48,80},{56,88},{... | collective-permute-start | bytes 491528 | tf_op jit(solution)/shard_map/ppermute | solution.py:219
  23.3 2.7 %local_part.7.refs_7_ = f32[2,128,1024]{2,1,0:T(8,128)S(1)} custom-call(bf16[5,1024,128]{2,1,0:T(8,128)(2,1)S(1)} %bitcast.13, bf16[5,1024,128]{2,1,0:T(8,128)(2,1)S(1)} %bitcast.21, bf16[5,1024,128]{2,1,0:T(8,128)(2,1)S(1)} %bitcast.25, f32[5,16,1024]{2,1,0:T(8,128)S(1)} %bitcast.29), custom_call_target="tpu_custom_call" | custom-call | flops 335544320 | bytes 2621440 | tf_op jit(solution)/shard_map/local_part/pallas_call | solution.py:79
  26.6 3.9 %collective-permute-start.5 = (bf16[1,128,640]{2,1,0:T(8,128)(2,1)S(1)}, bf16[1,128,640]{2,1,0:T(8,128)(2,1)S(1)}, u32[]{:S(2)}, u32[]{:S(2)}) collective-permute-start(bf16[1,128,640]{2,1,0:T(8,128)(2,1)S(1)} %far_part.4), channel_id=1, source_target_pairs={{0,1},{1,0},{2,3},{3,2},{4,5},{5,4},{6,7},{7,6},{8,9},{9,8},{10,11... | collective-permute-start | bytes 491528 | tf_op jit(solution)/shard_map/ppermute | solution.py:211
  33.7 1.8 %collective-permute-start.11 = (bf16[128,2560]{1,0:T(8,128)(2,1)S(1)}, bf16[128,2560]{1,0:T(8,128)(2,1)S(1)}, u32[]{:S(2)}, u32[]{:S(2)}) collective-permute-start(bf16[128,2560]{1,0:T(8,128)(2,1)S(1)} %project.10), channel_id=1, source_target_pairs={{0,2},{1,3},{2,4},{3,5},{4,6},{5,7},{6,0},{7,1},{8,10},{9,11},{10,... | collective-permute-start | bytes 1966088 | tf_op jit(solution)/shard_map/ppermute | solution.py:208
  35.5 2.2 %collective-permute-start.9 = (bf16[128,2560]{1,0:T(8,128)(2,1)S(1)}, bf16[128,2560]{1,0:T(8,128)(2,1)S(1)}, u32[]{:S(2)}, u32[]{:S(2)}) collective-permute-start(bf16[128,2560]{1,0:T(8,128)(2,1)S(1)} %project.12), channel_id=1, source_target_pairs={{0,6},{1,7},{2,0},{3,1},{4,2},{5,3},{6,4},{7,5},{8,14},{9,15},{10,... | collective-permute-start | bytes 1966088 | tf_op jit(solution)/shard_map/ppermute | solution.py:208
  40.6 1.2 %project.14 = bf16[128,2560]{1,0:T(8,128)(2,1)S(1)} custom-call(bf16[3,128,640]{2,1,0:T(8,128)(2,1)S(1)} %far_part.6.refs_0_, bf16[640,5120]{1,0:T(8,128)(2,1)S(1)} %bitcast.9, bf16[3,128,640]{2,1,0:T(8,128)(2,1)S(1)} %collective-permute-done.6.refs_2_, bf16[640,5120]{1,0:T(8,128)(2,1)S(1)} %collective-permute-done.3.refs_1_.refs_3_), custom_call_target="tpu_custom_call" | custom-call | flops 1000 | bytes 1000 | tf_op jit(solution)/shard_map/project/pallas_call | solution.py:155
  43.1 2.7 %collective-permute-start.7 = (bf16[128,2560]{1,0:T(8,128)(2,1)S(1)}, bf16[128,2560]{1,0:T(8,128)(2,1)S(1)}, u32[]{:S(2)}, u32[]{:S(2)}) collective-permute-start(bf16[128,2560]{1,0:T(8,128)(2,1)S(1)} %project.13), channel_id=1, source_target_pairs={{0,6},{1,7},{2,0},{3,1},{4,2},{5,3},{6,4},{7,5},{8,14},{9,15},{10,... | collective-permute-start | bytes 1966088 | tf_op jit(solution)/shard_map/ppermute | solution.py:208
  45.8 6.8 %collective-permute-done.11.refs_4_ = bf16[128,2560]{1,0:T(8,128)(2,1)S(1)} collective-permute-done((bf16[128,2560]{1,0:T(8,128)(2,1)S(1)}, bf16[128,2560]{1,0:T(8,128)(2,1)S(1)}, u32[]{:S(2)}, u32[]{:S(2)}) %collective-permute-start.11) | collective-permute-done | bytes 655392 | tf_op jit(solution)/shard_map/ppermute | solution.py:208
  54.0 1.2 %project.16 = bf16[128,2560]{1,0:T(8,128)(2,1)S(1)} custom-call(bf16[3,128,640]{2,1,0:T(8,128)(2,1)S(1)} %far_part.6.refs_0_, bf16[640,5120]{1,0:T(8,128)(2,1)S(1)} %bitcast.9, bf16[3,128,640]{2,1,0:T(8,128)(2,1)S(1)} %collective-permute-done.6.refs_2_, bf16[640,5120]{1,0:T(8,128)(2,1)S(1)} %collective-permute-done.3.refs_1_.refs_3_, ...), custom_call_target="tpu_custom_call" | custom-call | flops 1000 | bytes 1000 | tf_op jit(solution)/shard_map/project/pallas_call | solution.py:155
  55.1 2.7 %collective-permute-start.10 = (bf16[128,2560]{1,0:T(8,128)(2,1)S(1)}, bf16[128,2560]{1,0:T(8,128)(2,1)S(1)}, u32[]{:S(2)}, u32[]{:S(2)}) collective-permute-start(bf16[128,2560]{1,0:T(8,128)(2,1)S(1)} %project.16), channel_id=1, source_target_pairs={{0,6},{1,7},{2,0},{3,1},{4,2},{5,3},{6,4},{7,5},{8,14},{9,15},{10,... | collective-permute-start | bytes 1966088 | tf_op jit(solution)/shard_map/ppermute | solution.py:208
  57.9 8.8 %collective-permute-done.8.refs_5_ = bf16[128,2560]{1,0:T(8,128)(2,1)S(1)} collective-permute-done((bf16[128,2560]{1,0:T(8,128)(2,1)S(1)}, bf16[128,2560]{1,0:T(8,128)(2,1)S(1)}, u32[]{:S(2)}, u32[]{:S(2)}) %collective-permute-start.8) | collective-permute-done | bytes 655392 | tf_op jit(solution)/shard_map/ppermute | solution.py:208
  66.7 2.2 %project.15.own_ref = f32[128,5120]{1,0:T(8,128)S(1)} custom-call(bf16[3,128,640]{2,1,0:T(8,128)(2,1)S(1)} %far_part.6.refs_0_, bf16[640,5120]{1,0:T(8,128)(2,1)S(1)} %bitcast.9, bf16[3,128,640]{2,1,0:T(8,128)(2,1)S(1)} %collective-permute-done.6.refs_2_, bf16[640,5120]{1,0:T(8,128)(2,1)S(1)} %collective-permute-done.3.refs_1_.refs_3_, ...), custom_call_target="tpu_custom_call" | custom-call | flops 1000 | bytes 1000 | tf_op jit(solution)/shard_map/project/pallas_call | solution.py:155
  68.9 11.8 %collective-permute-done.12.left_ref = bf16[128,2560]{1,0:T(8,128)(2,1)S(1)} collective-permute-done((bf16[128,2560]{1,0:T(8,128)(2,1)S(1)}, bf16[128,2560]{1,0:T(8,128)(2,1)S(1)}, u32[]{:S(2)}, u32[]{:S(2)}) %collective-permute-start.12) | collective-permute-done | bytes 655392 | tf_op jit(solution)/shard_map/ppermute | solution.py:208
  (42 shorter events, 12.2 us)
Async XLA Ops:
  0.0 5.2 %copy-start.1 = (bf16[1024,5,128]{2,0,1:T(8,128)(2,1)S(1)}, bf16[1024,5,128]{2,0,1:T(8,128)(2,1)}, u32[]{:S(2)}) copy-start(bf16[1024,5,128]{2,0,1:T(8,128)(2,1)} %param.7) | copy-start | bytes 3932164
  0.0 5.2 %copy-start = (bf16[1024,5,128]{2,0,1:T(8,128)(2,1)S(1)}, bf16[1024,5,128]{2,0,1:T(8,128)(2,1)}, u32[]{:S(2)}) copy-start(bf16[1024,5,128]{2,0,1:T(8,128)(2,1)} %param.6) | copy-start | bytes 3932164
  0.0 20.3 %collective-permute-start.3 = (bf16[640,5120]{1,0:T(8,128)(2,1)}, bf16[640,5120]{1,0:T(8,128)(2,1)S(1)}, u32[]{:S(2)}, u32[]{:S(2)}) collective-permute-start(bf16[640,5120]{1,0:T(8,128)(2,1)} %refs_1_.13), channel_id=1, source_target_pairs={{0,1},{1,0},{2,3},{3,2},{4,5},{5,4},{6,7},{7,6},{8,9},{9,8},{10,11... | collective-permute-start | bytes 19660808 | tf_op jit(solution)/shard_map/ppermute | solution.py:211
  1.4 16.1 %slice-start = ((s8[6553600]{0:T(1024)(128)(4,1)}), s8[4194304]{0:T(1024)(128)(4,1)S(1)}, s32[]{:S(2)}) async-start(s8[6553600]{0:T(1024)(128)(4,1)} %bitcast.8), calls=%async_computation | async-start | bytes 8388608
  3.8 5.9 %collective-permute-start = (bf16[5,128,128]{2,1,0:T(8,128)(2,1)S(1)}, bf16[5,128,128]{2,1,0:T(8,128)(2,1)S(1)}, u32[]{:S(2)}, u32[]{:S(2)}) collective-permute-start(bf16[5,128,128]{2,1,0:T(8,128)(2,1)S(1)} %convolution_convert_fusion), channel_id=1, source_target_pairs={{0,8},{8,0},{16,24},{24,16},{32,40},{40,32},{48,56},{56,48},{64,72... | collective-permute-start | bytes 491528 | tf_op jit(solution)/shard_map/ppermute | solution.py:219
  5.2 1.3 %copy-start.2 = (bf16[1024,5,128]{2,0,1:T(8,128)(2,1)S(1)}, bf16[1024,5,128]{2,0,1:T(8,128)(2,1)}, u32[]{:S(2)}) copy-start(bf16[1024,5,128]{2,0,1:T(8,128)(2,1)} %param.8) | copy-start | bytes 3932164
  6.5 1.0 %copy-start.3 = (f32[1024,5,16]{0,2,1:T(8,128)S(1)}, f32[1024,5,16]{0,2,1:T(8,128)}, u32[]{:S(2)}) copy-start(f32[1024,5,16]{0,2,1:T(8,128)} %param.9) | copy-start | bytes 983044
  7.5 10.0 %slice-start.1 = ((s8[6553600]{0:T(1024)(128)(4,1)}), s8[2359296]{0:T(1024)(128)(4,1)S(1)}, s32[]{:S(2)}) async-start(s8[6553600]{0:T(1024)(128)(4,1)} %bitcast.8), calls=%async_computation.1 | async-start | bytes 4718592
  9.8 6.2 %collective-permute-start.1 = (bf16[5,128,128]{2,1,0:T(8,128)(2,1)S(1)}, bf16[5,128,128]{2,1,0:T(8,128)(2,1)S(1)}, u32[]{:S(2)}, u32[]{:S(2)}) collective-permute-start(bf16[5,128,128]{2,1,0:T(8,128)(2,1)S(1)} %add_convert_fusion.2), channel_id=1, source_target_pairs={{0,24},{8,16},{16,8},{24,0},{32,56},{40,48},{48,40},{56,32},{64,88... | collective-permute-start | bytes 491528 | tf_op jit(solution)/shard_map/ppermute | solution.py:219
  16.1 4.2 %collective-permute-start.2 = (bf16[5,128,128]{2,1,0:T(8,128)(2,1)S(1)}, bf16[5,128,128]{2,1,0:T(8,128)(2,1)S(1)}, u32[]{:S(2)}, u32[]{:S(2)}) collective-permute-start(bf16[5,128,128]{2,1,0:T(8,128)(2,1)S(1)} %add_convert_fusion.1), channel_id=1, source_target_pairs={{0,32},{8,40},{16,48},{24,56},{32,0},{40,8},{48,16},{56,24},{64,96... | collective-permute-start | bytes 491528 | tf_op jit(solution)/shard_map/ppermute | solution.py:219
  20.4 5.6 %copy-start.5 = (f32[5,128]{1,0:T(8,128)S(1)}, f32[5,128]{1,0:T(8,128)}, u32[]{:S(2)}) copy-start(f32[5,128]{1,0:T(8,128)} %param.10) | copy-start | bytes 7684
  20.4 5.6 %collective-permute-start.4 = (bf16[5,128,128]{2,1,0:T(8,128)(2,1)S(1)}, bf16[5,128,128]{2,1,0:T(8,128)(2,1)S(1)}, u32[]{:S(2)}, u32[]{:S(2)}) collective-permute-start(bf16[5,128,128]{2,1,0:T(8,128)(2,1)S(1)} %add_convert_fusion), channel_id=1, source_target_pairs={{0,96},{8,104},{16,112},{24,120},{32,64},{40,72},{48,80},{56,88},{... | collective-permute-start | bytes 491528 | tf_op jit(solution)/shard_map/ppermute | solution.py:219
  26.6 5.7 %collective-permute-start.5 = (bf16[1,128,640]{2,1,0:T(8,128)(2,1)S(1)}, bf16[1,128,640]{2,1,0:T(8,128)(2,1)S(1)}, u32[]{:S(2)}, u32[]{:S(2)}) collective-permute-start(bf16[1,128,640]{2,1,0:T(8,128)(2,1)S(1)} %far_part.4), channel_id=1, source_target_pairs={{0,1},{1,0},{2,3},{3,2},{4,5},{5,4},{6,7},{7,6},{8,9},{9,8},{10,11... | collective-permute-start | bytes 491528 | tf_op jit(solution)/shard_map/ppermute | solution.py:211
  33.0 4.7 %copy-start.4 = (f32[1024,5,16]{0,2,1:T(8,128)S(1)}, f32[1024,5,16]{0,2,1:T(8,128)}, u32[]{:S(2)}) copy-start(f32[1024,5,16]{0,2,1:T(8,128)} %param.9) | copy-start | bytes 983044
  33.7 19.0 %collective-permute-start.11 = (bf16[128,2560]{1,0:T(8,128)(2,1)S(1)}, bf16[128,2560]{1,0:T(8,128)(2,1)S(1)}, u32[]{:S(2)}, u32[]{:S(2)}) collective-permute-start(bf16[128,2560]{1,0:T(8,128)(2,1)S(1)} %project.10), channel_id=1, source_target_pairs={{0,2},{1,3},{2,4},{3,5},{4,6},{5,7},{6,0},{7,1},{8,10},{9,11},{10,... | collective-permute-start | bytes 1966088 | tf_op jit(solution)/shard_map/ppermute | solution.py:208
  35.5 18.5 %collective-permute-start.9 = (bf16[128,2560]{1,0:T(8,128)(2,1)S(1)}, bf16[128,2560]{1,0:T(8,128)(2,1)S(1)}, u32[]{:S(2)}, u32[]{:S(2)}) collective-permute-start(bf16[128,2560]{1,0:T(8,128)(2,1)S(1)} %project.12), channel_id=1, source_target_pairs={{0,6},{1,7},{2,0},{3,1},{4,2},{5,3},{6,4},{7,5},{8,14},{9,15},{10,... | collective-permute-start | bytes 1966088 | tf_op jit(solution)/shard_map/ppermute | solution.py:208
  38.5 2.1 %collective-permute-start.6 = (bf16[3,128,640]{2,1,0:T(8,128)(2,1)S(1)}, bf16[3,128,640]{2,1,0:T(8,128)(2,1)S(1)}, u32[]{:S(2)}, u32[]{:S(2)}) collective-permute-start(bf16[3,128,640]{2,1,0:T(8,128)(2,1)S(1)} %far_part.7), channel_id=1, source_target_pairs={{0,1},{1,0},{2,3},{3,2},{4,5},{5,4},{6,7},{7,6},{8,9},{9,8},{10,11... | collective-permute-start | bytes 1474568 | tf_op jit(solution)/shard_map/ppermute | solution.py:211
  41.8 24.9 %collective-permute-start.8 = (bf16[128,2560]{1,0:T(8,128)(2,1)S(1)}, bf16[128,2560]{1,0:T(8,128)(2,1)S(1)}, u32[]{:S(2)}, u32[]{:S(2)}) collective-permute-start(bf16[128,2560]{1,0:T(8,128)(2,1)S(1)} %project.14), channel_id=1, source_target_pairs={{0,2},{1,3},{2,4},{3,5},{4,6},{5,7},{6,0},{7,1},{8,10},{9,11},{10,... | collective-permute-start | bytes 1966088 | tf_op jit(solution)/shard_map/ppermute | solution.py:208
  43.1 23.6 %collective-permute-start.7 = (bf16[128,2560]{1,0:T(8,128)(2,1)S(1)}, bf16[128,2560]{1,0:T(8,128)(2,1)S(1)}, u32[]{:S(2)}, u32[]{:S(2)}) collective-permute-start(bf16[128,2560]{1,0:T(8,128)(2,1)S(1)} %project.13), channel_id=1, source_target_pairs={{0,6},{1,7},{2,0},{3,1},{4,2},{5,3},{6,4},{7,5},{8,14},{9,15},{10,... | collective-permute-start | bytes 1966088 | tf_op jit(solution)/shard_map/ppermute | solution.py:208
  53.9 26.9 %collective-permute-start.12 = (bf16[128,2560]{1,0:T(8,128)(2,1)S(1)}, bf16[128,2560]{1,0:T(8,128)(2,1)S(1)}, u32[]{:S(2)}, u32[]{:S(2)}) collective-permute-start(bf16[128,2560]{1,0:T(8,128)(2,1)S(1)} %project.17), channel_id=1, source_target_pairs={{0,2},{1,3},{2,4},{3,5},{4,6},{5,7},{6,0},{7,1},{8,10},{9,11},{10,... | collective-permute-start | bytes 1966088 | tf_op jit(solution)/shard_map/ppermute | solution.py:208
  55.1 25.6 %collective-permute-start.10 = (bf16[128,2560]{1,0:T(8,128)(2,1)S(1)}, bf16[128,2560]{1,0:T(8,128)(2,1)S(1)}, u32[]{:S(2)}, u32[]{:S(2)}) collective-permute-start(bf16[128,2560]{1,0:T(8,128)(2,1)S(1)} %project.16), channel_id=1, source_target_pairs={{0,6},{1,7},{2,0},{3,1},{4,2},{5,3},{6,4},{7,5},{8,14},{9,15},{10,... | collective-permute-start | bytes 1966088 | tf_op jit(solution)/shard_map/ppermute | solution.py:208

commit v4 on v3

--- a/solution.py
+++ b/solution.py
@@ -131,45 +131,55 @@
     return [(n, min(tile, cols - n)) for n in range(0, cols, tile)]
 
 
-def project_body(pairs, col_start, adds, refs):
-    out_ref = refs[-1]
-    sources = refs[2 * len(pairs) : -1]
-    cuts = sorted({0, out_ref.shape[1], *adds})
-    places = [(lo + n, size) for lo, hi in zip(cuts, cuts[1:]) for n, size in tiles_of(hi - lo)]
-    for n, size in places:
+def project_body(blocks, col_start, adds, outs, refs):
+    out_refs = refs[len(refs) - len(outs) :]
+    sources = refs[2 * len(blocks) : len(refs) - len(outs)]
+    spans = [(lo, lo + source.shape[1]) for source, lo in zip(sources, adds)]
+    ends = [(sum(outs[:i]), sum(outs[: i + 1])) for i in range(len(outs))]
+    cuts = sorted({cut for span in spans + ends for cut in span})
+    for n, size in [(lo + n, size) for lo, hi in zip(cuts, cuts[1:]) for n, size in tiles_of(hi - lo)]:
         there = slice(col_start + n, col_start + n + size)
         total = None
-        for i, block in enumerate(pairs):
+        for i, block in enumerate(blocks):
             part = jnp.dot(refs[2 * i][block], refs[2 * i + 1][:, there], preferred_element_type=F32)
             total = part if total is None else total + part
-        for source, lo in zip(sources, adds):
-            if lo <= n < lo + source.shape[1]:
+        for source, (lo, hi) in zip(sources, spans):
+            if lo <= n < hi:
                 total = total + source[:, n - lo : n - lo + size].astype(F32)
-        out_ref[:, n : n + size] = total.astype(out_ref.dtype)
-
-
-def project(pairs, col_start, cols, adds=(), out_dtype=BF16, flops=1000):
+        for out_ref, (lo, hi) in zip(out_refs, ends):
+            if lo <= n < hi:
+                out_ref[:, n - lo : n - lo + size] = total.astype(out_ref.dtype)
+
+
+def project(pairs, col_start, outs, adds=(), out_dtype=BF16, flops=1000):
     rows = pairs[0][0].shape[1]
     blocks = [block for _, block, _ in pairs]
     args = [x for value, _, weight in pairs for x in (value, weight)]
-    return pl.pallas_call(
-        lambda *refs: project_body(blocks, col_start, [lo for _, lo in adds], refs),
+    shapes = [jax.ShapeDtypeStruct((rows, cols), out_dtype) for cols in outs]
+    return pl.pallas_call(
+        lambda *refs: project_body(blocks, col_start, [lo for _, lo in adds], outs, refs),
         in_specs=[VMEM] * (len(args) + len(adds)),
-        out_specs=VMEM,
-        out_shape=jax.ShapeDtypeStruct((rows, cols), out_dtype),
+        out_specs=[VMEM] * len(outs),
+        out_shape=shapes,
         cost_estimate=cost(flops, 1000),
         compiler_params=vmem(24),
         name="project",
     )(*args, *[x for x, _ in adds])
 
 
-def finish_body(own_ref, right_ref, left_ref, out_ref, hold_ref, sems):
-    split = left_ref.shape[1]
+def finish_body(own_ref, left_ref, right_ref, out_ref, hold_ref, sems):
+    width = own_ref.shape[1]
+    ends, start = left_ref.shape[1], width - right_ref.shape[1]
+    cuts = [0, start, ends, width] if start < ends else [0, ends, width]
     copies = []
-    for late_ref, start in ((left_ref, 0), (right_ref, split)):
-        for n, size in tiles_of(late_ref.shape[1], FINISH_TILE):
-            there = slice(start + n, start + n + size)
-            total = own_ref[:, there] + late_ref[:, n : n + size].astype(F32)
+    for lo, hi in zip(cuts, cuts[1:]):
+        for n, size in tiles_of(hi - lo, FINISH_TILE):
+            there = slice(lo + n, lo + n + size)
+            total = own_ref[:, there]
+            if lo < ends:
+                total = total + left_ref[:, there].astype(F32)
+            if lo >= start:
+                total = total + right_ref[:, lo + n - start : lo + n - start + size].astype(F32)
             hold_ref[:, there] = total.astype(BF16)
             i = len(copies)
             copies.append(pltpu.make_async_copy(hold_ref.at[:, there], out_ref.at[:, there], sems.at[i]))
@@ -180,7 +190,7 @@
 
 def finish(own, left, right):
     rows, width = own.shape
-    count = len(tiles_of(left.shape[1], FINISH_TILE)) + len(tiles_of(right.shape[1], FINISH_TILE))
+    count = 3 * len(tiles_of(width, FINISH_TILE))
     return pl.pallas_call(
         finish_body,
         in_specs=[VMEM] * 3,
@@ -190,7 +200,7 @@
         cost_estimate=cost(1000, 1000),
         compiler_params=vmem(16),
         name="finish",
-    )(own, right, left)
+    )(own, left, right)
 
 
 def on_device(queries, key_rows, value_rows, level_weight, norm_gain, out_weight):
@@ -210,40 +220,39 @@
     def across_cores(x):
         return lax.ppermute(x, "head", [(i, i ^ 1) for i in range(8)])
 
-    def ctx_swap(x, bit):
-        swap = ((1, 0, 3, 2), (3, 2, 1, 0))[bit % 2]
-        if bit < 2:
-            pairs = [(4 * y + i, 4 * y + swap[i]) for y in range(4) for i in range(4)]
-        else:
-            pairs = [(4 * i + x, 4 * swap[i] + x) for i in range(4) for x in range(4)]
-        return lax.ppermute(x, "ctx", pairs)
+    def swaps(x, along):
+        got = []
+        for swap in ((3, 2, 1, 0), (1, 0, 3, 2), (2, 3, 0, 1)):
+            if along == "x":
+                pairs = [(4 * y + i, 4 * y + swap[i]) for y in range(4) for i in range(4)]
+            else:
+                pairs = [(4 * i + c, 4 * swap[i] + c) for i in range(4) for c in range(4)]
+            got.append(lax.ppermute(x, "ctx", pairs))
+        return got
 
     gains = jnp.broadcast_to(norm_gain[:, :, None], (heads, dh, CH))
     message = jnp.einsum("hse,hsd->hed", v, k, preferred_element_type=F32).astype(BF16)
     w_other = across_cores(out_weight)
-    parts = [(0,), (1,), (2,), (3, 4)]
+    parts = [(0, 1, 2), (3, 4)]
     sibs, accs = [], []
-    for bit in range(4):
-        got = ctx_swap(message, bit)
+    for step, along in enumerate("xy"):
+        got = swaps(message, along)
         tied, _ = lax.optimization_barrier((w, message))
-        held = (out_weight,) if bit == 2 else ()
-        got, acc = lax.optimization_barrier((got, local_part(q, k, v, tied, parts[bit], held)))
-        if bit == 2:
-            got, w_other = lax.optimization_barrier((got, w_other))
-        sibs.append(got)
+        acc = local_part(q, k, v, tied, parts[step], (out_weight,) if step else ())
+        low, near, far, acc = lax.optimization_barrier((*got, acc))
+        far, low = far.astype(F32), low.astype(F32)
+        sibs += [near, (far + low).astype(BF16)]
         accs.append(acc)
-        if bit < 3:
-            message = (message.astype(F32) + got.astype(F32)).astype(BF16)
+        if not step:
+            near, w_other = lax.optimization_barrier((near, w_other))
+            message = (message.astype(F32) + near.astype(F32) + (far + low)).astype(BF16)
 
     send1 = far_part(accs, parts, q, w, sibs, gains, 1, (2,))
     other1 = across_cores(send1)
     own1 = far_part(accs, parts, q, w, sibs, gains, 0, (2,))
-    early_up = project([(own1, 0, out_weight)], 0, split, (), F32)
-    early_down = project([(own1, 0, out_weight)], split, rest, (), F32)
-    first_up = project([(other1, 0, w_other)], 0, split, ((early_up, 0),))
-    late_other, first_up = lax.optimization_barrier((other1, first_up))
-    first_down = project([(late_other, 0, w_other)], split, rest, ((early_down, 0),))
-    late_q, first_down = lax.optimization_barrier((q, first_down))
+    (early,) = project([(own1, 0, out_weight)], 0, (width,), (), F32)
+    first_up, first_down = project([(other1, 0, w_other)], 0, (split, rest), ((early, 0),))
+    late_q, first_up, first_down = lax.optimization_barrier((q, first_up, first_down))
     relay_up = along_z(first_up, 1)
     relay_down = along_z(first_down, -1)
     send2 = far_part(accs, parts, late_q, w, sibs, gains, 1, (1, 3, 0))
@@ -253,13 +262,11 @@
     def block(i):
         return [(own2, i, out_weight), (other2, i, w_other)]
 
-    next_up = project(block(0), split, rest)
-    next_down = project(block(1), 0, split)
-    direct_up = along_z(next_up, 1)
-    direct_down = along_z(next_down, -1)
-    joined_up = along_z(project(block(0), 0, split, ((relay_up, 0),)), 1)
-    joined_down = along_z(project(block(1), split, rest, ((relay_down, 0),)), -1)
-    mine = project(block(2), 0, width, ((direct_down, 0), (direct_up, split)), F32, MINE_FLOPS)
+    direct_up = along_z(project(block(0), split, (rest,))[0], 1)
+    direct_down = along_z(project(block(1), 0, (rest,))[0], -1)
+    joined_up = along_z(project(block(0), 0, (split,), ((relay_up, 0),))[0], 1)
+    joined_down = along_z(project(block(1), rest, (split,), ((relay_down, split - rest),))[0], -1)
+    (mine,) = project(block(2), 0, (width,), ((direct_down, 0), (direct_up, split)), F32, MINE_FLOPS)
     return finish(mine, joined_up, joined_down)
 
 

time: 82.2 us -> 79.1 us (0.962)
  starting transfers between devices: 23.8 us -> 19.5 us
  waiting for transfers between devices: 32.4 us -> 34.3 us
    ppermute x3, starting transfers between devices: 5.92 us -> 3.52 us  [across_cores(): return lax.ppermute(x, 'head', [(i, i ^ 1) for i in range(8)])]
    ppermute x6, starting transfers between devices: 9.57 us -> 8.46 us  [along_z(): return lax.ppermute(x, 'head', pairs)]
    ppermute x6, waiting for transfers between devices: 27.5 us -> 28.6 us  [along_z(): return lax.ppermute(x, 'head', pairs)]
    ppermute x4 -> x6, starting transfers between devices: 8.33 us -> 7.54 us  [swaps(): got.append(lax.ppermute(x, 'ctx', pairs))]
    ppermute x4 -> x6, waiting for transfers between devices: 4.13 us -> 4.91 us  [swaps(): got.append(lax.ppermute(x, 'ctx', pairs))]
    pallas_call x4 -> x2, Pallas kernels: 7.17 us -> 6.59 us  [local_part(): pl.pallas_call(lambda *refs: local_body(heads, *refs[:4], refs[-1]), in_s...]
    pallas_call x9 -> x7, Pallas kernels: 9.66 us -> 9.31 us  [project(): pl.pallas_call(lambda *refs: project_body(blocks, col_start, [lo for _, l...]
    unnamed x16 -> x12, local copies, waits for them, and re-layouts: 2.32 us -> 2.65 us
  transfers between devices with their start and end apart: 13 -> 15, of which waited for: 7 -> 8; matrix products, arithmetic and copies ran while one was open for 3% -> 3% of each run, Pallas kernels for 21% -> 21%
where the time goes in v4:
time: 79.1 us; the launch traced here: 78.9 us
  waiting for transfers between devices  34.3 us (43%)
  Pallas kernels  19.6 us (25%)
  starting transfers between devices  19.5 us (25%)
  local copies, waits for them, and re-layouts  2.79 us (4%)
  matrix products  2.26 us (3%)
    ppermute x6, waiting for transfers between devices, along_z(): return lax.ppermute(x, 'head', pairs)  28.6 us
    pallas_call x7, Pallas kernels, project(): pl.pallas_call(lambda *refs: project_body(blocks, col_start, [lo for _, l...  9.31 us
    ppermute x6, starting transfers between devices, along_z(): return lax.ppermute(x, 'head', pairs)  8.46 us
    ppermute x6, starting transfers between devices, swaps(): got.append(lax.ppermute(x, 'ctx', pairs))  7.54 us
    pallas_call x2, Pallas kernels, local_part(): pl.pallas_call(lambda *refs: local_body(heads, *refs[:4], refs[-1]), in_s...  6.59 us
    ppermute x6, waiting for transfers between devices, swaps(): got.append(lax.ppermute(x, 'ctx', pairs))  4.91 us
    ppermute x3, starting transfers between devices, across_cores(): return lax.ppermute(x, 'head', [(i, i ^ 1) for i in range(8)])  3.52 us
    unnamed x12, local copies, waits for them, and re-layouts  2.65 us
  transfers between devices with their start and end apart: 15, of which 8 were waited for; matrix products, arithmetic and copies ran while one was open for 3% of the time, Pallas kernels for 21%

profile of v4, /device:TPU:1, one launch (start us, length us, event | category | flops | bytes accessed | tf_op | source)
XLA Modules:
  0.0 78.9 jit_solution(17619348253135081372)
XLA Ops:
  0.0 1.4 %collective-permute-start.3 = (bf16[640,5120]{1,0:T(8,128)(2,1)}, bf16[640,5120]{1,0:T(8,128)(2,1)S(1)}, u32[]{:S(2)}, u32[]{:S(2)}) collective-permute-start(bf16[640,5120]{1,0:T(8,128)(2,1)} %refs_1_.11), channel_id=1, source_target_pairs={{0,1},{1,0},{2,3},{3,2},{4,5},{5,4},{6,7},{7,6},{8,9},{9,8},{10,11... | collective-permute-start | bytes 19660808 | tf_op jit(solution)/shard_map/ppermute | solution.py:221
  1.4 2.3 %convolution_convert_fusion = bf16[5,128,128]{2,1,0:T(8,128)(2,1)S(1)} fusion(bf16[1024,5,128]{2,0,1:T(8,128)(2,1)} %param.7, bf16[1024,5,128]{2,0,1:T(8,128)(2,1)} %param.8), kind=kOutput, calls=%fused_computation | convolution fusion | flops 167854080 | bytes 2785280 | tf_op jit(solution)/shard_map/hse,hsd->hed/dot_general | solution.py:234
  3.7 2.9 %collective-permute-start.2 = (bf16[5,128,128]{2,1,0:T(8,128)(2,1)S(1)}, bf16[5,128,128]{2,1,0:T(8,128)(2,1)S(1)}, u32[]{:S(2)}, u32[]{:S(2)}) collective-permute-start(bf16[5,128,128]{2,1,0:T(8,128)(2,1)S(1)} %convolution_convert_fusion), channel_id=1, source_target_pairs={{0,16},{8,24},{16,0},{24,8},{32,48},{40,56},{48,32},{56,40},{64,80... | collective-permute-start | bytes 491528 | tf_op jit(solution)/shard_map/ppermute | solution.py:230
  7.5 1.3 %copy-done.3 = bf16[1024,5,128]{2,0,1:T(8,128)(2,1)S(1)} copy-done((bf16[1024,5,128]{2,0,1:T(8,128)(2,1)S(1)}, bf16[1024,5,128]{2,0,1:T(8,128)(2,1)}, u32[]{:S(2)}) %copy-start.3) | copy-done | bytes 1310744
  8.8 1.3 %copy-done.4 = bf16[1024,5,128]{2,0,1:T(8,128)(2,1)S(1)} copy-done((bf16[1024,5,128]{2,0,1:T(8,128)(2,1)S(1)}, bf16[1024,5,128]{2,0,1:T(8,128)(2,1)}, u32[]{:S(2)}) %copy-start.4) | copy-done | bytes 1310744
  10.1 3.9 %local_part.2.refs_4_ = f32[3,128,1024]{2,1,0:T(8,128)S(1)} custom-call(bf16[5,1024,128]{2,1,0:T(8,128)(2,1)S(1)} %bitcast.8, bf16[5,1024,128]{2,1,0:T(8,128)(2,1)S(1)} %bitcast.20, bf16[5,1024,128]{2,1,0:T(8,128)(2,1)S(1)} %bitcast.22, f32[5,16,1024]{2,1,0:T(8,128)S(1)} %bitcast.14), custom_call_target="tpu_custom_call" | custom-call | flops 503316480 | bytes 3932160 | tf_op jit(solution)/shard_map/local_part/pallas_call | solution.py:79
  14.8 3.0 %collective-permute-start.6 = (bf16[5,128,128]{2,1,0:T(8,128)(2,1)S(1)}, bf16[5,128,128]{2,1,0:T(8,128)(2,1)S(1)}, u32[]{:S(2)}, u32[]{:S(2)}) collective-permute-start(bf16[5,128,128]{2,1,0:T(8,128)(2,1)S(1)} %get-tuple-element.39), channel_id=1, source_target_pairs={{0,64},{8,72},{16,80},{24,88},{32,96},{40,104},{48,112},{56,120},{... | collective-permute-start | bytes 491528 | tf_op jit(solution)/shard_map/ppermute | solution.py:230
  18.6 2.7 %local_part.3.refs_5_ = f32[2,128,1024]{2,1,0:T(8,128)S(1)} custom-call(bf16[5,1024,128]{2,1,0:T(8,128)(2,1)S(1)} %bitcast.9, bf16[5,1024,128]{2,1,0:T(8,128)(2,1)S(1)} %bitcast.21, bf16[5,1024,128]{2,1,0:T(8,128)(2,1)S(1)} %bitcast.23, f32[5,16,1024]{2,1,0:T(8,128)S(1)} %bitcast.15, bf16[640,5120]{1,0:T(8,128)(2,1)S(1)} %copy-done), custom_call_target="tpu_custom_call" | custom-call | flops 335544320 | bytes 2621440 | tf_op jit(solution)/shard_map/local_part/pallas_call | solution.py:79
  21.3 3.7 %collective-permute-done.5.refs_2_ = bf16[5,128,128]{2,1,0:T(8,128)(2,1)S(1)} collective-permute-done((bf16[5,128,128]{2,1,0:T(8,128)(2,1)S(1)}, bf16[5,128,128]{2,1,0:T(8,128)(2,1)S(1)}, u32[]{:S(2)}, u32[]{:S(2)}) %collective-permute-start.5) | collective-permute-done | bytes 163872 | tf_op jit(solution)/shard_map/ppermute | solution.py:230
  26.2 1.5 %collective-permute-start.7 = (bf16[1,128,640]{2,1,0:T(8,128)(2,1)S(1)}, bf16[1,128,640]{2,1,0:T(8,128)(2,1)S(1)}, u32[]{:S(2)}, u32[]{:S(2)}) collective-permute-start(bf16[1,128,640]{2,1,0:T(8,128)(2,1)S(1)} %far_part.4), channel_id=1, source_target_pairs={{0,1},{1,0},{2,3},{3,2},{4,5},{5,4},{6,7},{7,6},{8,9},{9,8},{10,11... | collective-permute-start | bytes 491528 | tf_op jit(solution)/shard_map/ppermute | solution.py:221
  28.2 1.2 %project.7.refs_2_ = f32[128,5120]{1,0:T(8,128)S(1)} custom-call(bf16[1,128,640]{2,1,0:T(8,128)(2,1)S(1)} %far_part.5.refs_0_, bf16[640,5120]{1,0:T(8,128)(2,1)S(1)} %copy-done), custom_call_target="tpu_custom_call" | custom-call | flops 1000 | bytes 1000 | tf_op jit(solution)/shard_map/project/pallas_call | solution.py:159
  29.4 1.2 %project.8 = (bf16[128,2560]{1,0:T(8,128)(2,1)S(1)}, bf16[128,2560]{1,0:T(8,128)(2,1)S(1)}) custom-call(bf16[1,128,640]{2,1,0:T(8,128)(2,1)S(1)} %collective-permute-done.7.refs_0_, bf16[640,5120]{1,0:T(8,128)(2,1)S(1)} %collective-permute-done.3.refs_1_.refs_3_, f32[128,5120]{1,0:T(8,128)S(1)} %project.7.refs_2_), custom_call_target="tpu_custom_call" | custom-call | flops 1000 | bytes 1000 | tf_op jit(solution)/shard_map/project/pallas_call | solution.py:159
  30.6 1.7 %collective-permute-start.11 = (bf16[128,2560]{1,0:T(8,128)(2,1)S(1)}, bf16[128,2560]{1,0:T(8,128)(2,1)S(1)}, u32[]{:S(2)}, u32[]{:S(2)}) collective-permute-start(bf16[128,2560]{1,0:T(8,128)(2,1)S(1)} %get-tuple-element.37), channel_id=1, source_target_pairs={{0,2},{1,3},{2,4},{3,5},{4,6},{5,7},{6,0},{7,1},{8,10},{9,11},{10,... | collective-permute-start | bytes 1966088 | tf_op jit(solution)/shard_map/ppermute | solution.py:218
  32.3 2.2 %collective-permute-start.13 = (bf16[128,2560]{1,0:T(8,128)(2,1)S(1)}, bf16[128,2560]{1,0:T(8,128)(2,1)S(1)}, u32[]{:S(2)}, u32[]{:S(2)}) collective-permute-start(bf16[128,2560]{1,0:T(8,128)(2,1)S(1)} %get-tuple-element.38), channel_id=1, source_target_pairs={{0,6},{1,7},{2,0},{3,1},{4,2},{5,3},{6,4},{7,5},{8,14},{9,15},{10,... | collective-permute-start | bytes 1966088 | tf_op jit(solution)/shard_map/ppermute | solution.py:218
  37.4 1.2 %project.9 = bf16[128,2560]{1,0:T(8,128)(2,1)S(1)} custom-call(bf16[3,128,640]{2,1,0:T(8,128)(2,1)S(1)} %far_part.6.refs_0_, bf16[640,5120]{1,0:T(8,128)(2,1)S(1)} %copy-done, bf16[3,128,640]{2,1,0:T(8,128)(2,1)S(1)} %collective-permute-done.8.refs_2_, bf16[640,5120]{1,0:T(8,128)(2,1)S(1)} %collective-permute-done.3.refs_1_.refs_3_), custom_call_target="tpu_custom_call" | custom-call | flops 1000 | bytes 1000 | tf_op jit(solution)/shard_map/project/pallas_call | solution.py:159
  38.6 1.7 %collective-permute-start.9 = (bf16[128,2560]{1,0:T(8,128)(2,1)S(1)}, bf16[128,2560]{1,0:T(8,128)(2,1)S(1)}, u32[]{:S(2)}, u32[]{:S(2)}) collective-permute-start(bf16[128,2560]{1,0:T(8,128)(2,1)S(1)} %project.9), channel_id=1, source_target_pairs={{0,6},{1,7},{2,0},{3,1},{4,2},{5,3},{6,4},{7,5},{8,14},{9,15},{10,... | collective-permute-start | bytes 1966088 | tf_op jit(solution)/shard_map/ppermute | solution.py:218
  41.5 7.9 %collective-permute-done.11.refs_4_ = bf16[128,2560]{1,0:T(8,128)(2,1)S(1)} collective-permute-done((bf16[128,2560]{1,0:T(8,128)(2,1)S(1)}, bf16[128,2560]{1,0:T(8,128)(2,1)S(1)}, u32[]{:S(2)}, u32[]{:S(2)}) %collective-permute-start.11) | collective-permute-done | bytes 655392 | tf_op jit(solution)/shard_map/ppermute | solution.py:218
  49.5 1.2 %project.12 = bf16[128,2560]{1,0:T(8,128)(2,1)S(1)} custom-call(bf16[3,128,640]{2,1,0:T(8,128)(2,1)S(1)} %far_part.6.refs_0_, bf16[640,5120]{1,0:T(8,128)(2,1)S(1)} %copy-done, bf16[3,128,640]{2,1,0:T(8,128)(2,1)S(1)} %collective-permute-done.8.refs_2_, bf16[640,5120]{1,0:T(8,128)(2,1)S(1)} %collective-permute-done.3.refs_1_.refs_3_, ...), custom_call_target="tpu_custom_call" | custom-call | flops 1000 | bytes 1000 | tf_op jit(solution)/shard_map/project/pallas_call | solution.py:159
  50.8 1.2 %project.13 = bf16[128,2560]{1,0:T(8,128)(2,1)S(1)} custom-call(bf16[3,128,640]{2,1,0:T(8,128)(2,1)S(1)} %far_part.6.refs_0_, bf16[640,5120]{1,0:T(8,128)(2,1)S(1)} %copy-done, bf16[3,128,640]{2,1,0:T(8,128)(2,1)S(1)} %collective-permute-done.8.refs_2_, bf16[640,5120]{1,0:T(8,128)(2,1)S(1)} %collective-permute-done.3.refs_1_.refs_3_, ...), custom_call_target="tpu_custom_call" | custom-call | flops 1000 | bytes 1000 | tf_op jit(solution)/shard_map/project/pallas_call | solution.py:159
  52.0 2.7 %collective-permute-start.14 = (bf16[128,2560]{1,0:T(8,128)(2,1)S(1)}, bf16[128,2560]{1,0:T(8,128)(2,1)S(1)}, u32[]{:S(2)}, u32[]{:S(2)}) collective-permute-start(bf16[128,2560]{1,0:T(8,128)(2,1)S(1)} %project.13), channel_id=1, source_target_pairs={{0,6},{1,7},{2,0},{3,1},{4,2},{5,3},{6,4},{7,5},{8,14},{9,15},{10,... | collective-permute-start | bytes 1966088 | tf_op jit(solution)/shard_map/ppermute | solution.py:218
  54.7 8.0 %collective-permute-done.9.refs_4_ = bf16[128,2560]{1,0:T(8,128)(2,1)S(1)} collective-permute-done((bf16[128,2560]{1,0:T(8,128)(2,1)S(1)}, bf16[128,2560]{1,0:T(8,128)(2,1)S(1)}, u32[]{:S(2)}, u32[]{:S(2)}) %collective-permute-start.9) | collective-permute-done | bytes 655392 | tf_op jit(solution)/shard_map/ppermute | solution.py:218
  63.5 2.2 %project.11.own_ref = f32[128,5120]{1,0:T(8,128)S(1)} custom-call(bf16[3,128,640]{2,1,0:T(8,128)(2,1)S(1)} %far_part.6.refs_0_, bf16[640,5120]{1,0:T(8,128)(2,1)S(1)} %copy-done, bf16[3,128,640]{2,1,0:T(8,128)(2,1)S(1)} %collective-permute-done.8.refs_2_, bf16[640,5120]{1,0:T(8,128)(2,1)S(1)} %collective-permute-done.3.refs_1_.refs_3_, ...), custom_call_target="tpu_custom_call" | custom-call | flops 1000 | bytes 1000 | tf_op jit(solution)/shard_map/project/pallas_call | solution.py:159
  65.7 11.8 %collective-permute-done.12.left_ref = bf16[128,2560]{1,0:T(8,128)(2,1)S(1)} collective-permute-done((bf16[128,2560]{1,0:T(8,128)(2,1)S(1)}, bf16[128,2560]{1,0:T(8,128)(2,1)S(1)}, u32[]{:S(2)}, u32[]{:S(2)}) %collective-permute-start.12) | collective-permute-done | bytes 655392 | tf_op jit(solution)/shard_map/ppermute | solution.py:218
  77.6 1.2 %finish.1 = bf16[128,5120]{1,0:T(8,128)(2,1)} custom-call(f32[128,5120]{1,0:T(8,128)S(1)} %project.11.own_ref, bf16[128,2560]{1,0:T(8,128)(2,1)S(1)} %collective-permute-done.12.left_ref, bf16[128,2560]{1,0:T(8,128)(2,1)S(1)} %collective-permute-done.14.right_ref), custom_call_target="tpu_custom_call" | custom-call | flops 1000 | bytes 1000 | tf_op jit(solution)/shard_map/finish/pallas_call | solution.py:194
  (36 shorter events, 9.1 us)
Async XLA Ops:
  0.0 7.5 %copy-start.2 = (f32[1024,5,16]{0,2,1:T(8,128)S(1)}, f32[1024,5,16]{0,2,1:T(8,128)}, u32[]{:S(2)}) copy-start(f32[1024,5,16]{0,2,1:T(8,128)} %param.9) | copy-start | bytes 983044
  0.0 7.5 %copy-start.1 = (bf16[1024,5,128]{2,0,1:T(8,128)(2,1)S(1)}, bf16[1024,5,128]{2,0,1:T(8,128)(2,1)}, u32[]{:S(2)}) copy-start(bf16[1024,5,128]{2,0,1:T(8,128)(2,1)} %param.6) | copy-start | bytes 3932164
  0.0 14.7 %collective-permute-start.3 = (bf16[640,5120]{1,0:T(8,128)(2,1)}, bf16[640,5120]{1,0:T(8,128)(2,1)S(1)}, u32[]{:S(2)}, u32[]{:S(2)}) collective-permute-start(bf16[640,5120]{1,0:T(8,128)(2,1)} %refs_1_.11), channel_id=1, source_target_pairs={{0,1},{1,0},{2,3},{3,2},{4,5},{5,4},{6,7},{7,6},{8,9},{9,8},{10,11... | collective-permute-start | bytes 19660808 | tf_op jit(solution)/shard_map/ppermute | solution.py:221
  3.7 10.3 %collective-permute-start.2 = (bf16[5,128,128]{2,1,0:T(8,128)(2,1)S(1)}, bf16[5,128,128]{2,1,0:T(8,128)(2,1)S(1)}, u32[]{:S(2)}, u32[]{:S(2)}) collective-permute-start(bf16[5,128,128]{2,1,0:T(8,128)(2,1)S(1)} %convolution_convert_fusion), channel_id=1, source_target_pairs={{0,16},{8,24},{16,0},{24,8},{32,48},{40,56},{48,32},{56,40},{64,80... | collective-permute-start | bytes 491528 | tf_op jit(solution)/shard_map/ppermute | solution.py:230
  6.6 8.1 %collective-permute-start.1 = (bf16[5,128,128]{2,1,0:T(8,128)(2,1)S(1)}, bf16[5,128,128]{2,1,0:T(8,128)(2,1)S(1)}, u32[]{:S(2)}, u32[]{:S(2)}) collective-permute-start(bf16[5,128,128]{2,1,0:T(8,128)(2,1)S(1)} %convolution_convert_fusion), channel_id=1, source_target_pairs={{0,8},{8,0},{16,24},{24,16},{32,40},{40,32},{48,56},{56,48},{64,72... | collective-permute-start | bytes 491528 | tf_op jit(solution)/shard_map/ppermute | solution.py:230
  6.9 7.8 %collective-permute-start = (bf16[5,128,128]{2,1,0:T(8,128)(2,1)S(1)}, bf16[5,128,128]{2,1,0:T(8,128)(2,1)S(1)}, u32[]{:S(2)}, u32[]{:S(2)}) collective-permute-start(bf16[5,128,128]{2,1,0:T(8,128)(2,1)S(1)} %convolution_convert_fusion), channel_id=1, source_target_pairs={{0,24},{8,16},{16,8},{24,0},{32,56},{40,48},{48,40},{56,32},{64,88... | collective-permute-start | bytes 491528 | tf_op jit(solution)/shard_map/ppermute | solution.py:230
  7.5 1.3 %copy-start.3 = (bf16[1024,5,128]{2,0,1:T(8,128)(2,1)S(1)}, bf16[1024,5,128]{2,0,1:T(8,128)(2,1)}, u32[]{:S(2)}) copy-start(bf16[1024,5,128]{2,0,1:T(8,128)(2,1)} %param.7) | copy-start | bytes 3932164
  8.8 1.3 %copy-start.4 = (bf16[1024,5,128]{2,0,1:T(8,128)(2,1)S(1)}, bf16[1024,5,128]{2,0,1:T(8,128)(2,1)}, u32[]{:S(2)}) copy-start(bf16[1024,5,128]{2,0,1:T(8,128)(2,1)} %param.8) | copy-start | bytes 3932164
  10.1 8.5 %copy-start = (bf16[640,5120]{1,0:T(8,128)(2,1)S(1)}, bf16[640,5120]{1,0:T(8,128)(2,1)}, u32[]{:S(2)}) copy-start(bf16[640,5120]{1,0:T(8,128)(2,1)} %refs_1_.11) | copy-start | bytes 19660804
  14.8 10.8 %copy-start.5 = (f32[5,128]{1,0:T(8,128)S(1)}, f32[5,128]{1,0:T(8,128)}, u32[]{:S(2)}) copy-start(f32[5,128]{1,0:T(8,128)} %param.10) | copy-start | bytes 7684
  14.8 6.5 %collective-permute-start.6 = (bf16[5,128,128]{2,1,0:T(8,128)(2,1)S(1)}, bf16[5,128,128]{2,1,0:T(8,128)(2,1)S(1)}, u32[]{:S(2)}, u32[]{:S(2)}) collective-permute-start(bf16[5,128,128]{2,1,0:T(8,128)(2,1)S(1)} %get-tuple-element.39), channel_id=1, source_target_pairs={{0,64},{8,72},{16,80},{24,88},{32,96},{40,104},{48,112},{56,120},{... | collective-permute-start | bytes 491528 | tf_op jit(solution)/shard_map/ppermute | solution.py:230
  17.8 7.2 %collective-permute-start.5 = (bf16[5,128,128]{2,1,0:T(8,128)(2,1)S(1)}, bf16[5,128,128]{2,1,0:T(8,128)(2,1)S(1)}, u32[]{:S(2)}, u32[]{:S(2)}) collective-permute-start(bf16[5,128,128]{2,1,0:T(8,128)(2,1)S(1)} %get-tuple-element.39), channel_id=1, source_target_pairs={{0,32},{8,40},{16,48},{24,56},{32,0},{40,8},{48,16},{56,24},{64,96... | collective-permute-start | bytes 491528 | tf_op jit(solution)/shard_map/ppermute | solution.py:230
  18.2 7.3 %collective-permute-start.4 = (bf16[5,128,128]{2,1,0:T(8,128)(2,1)S(1)}, bf16[5,128,128]{2,1,0:T(8,128)(2,1)S(1)}, u32[]{:S(2)}, u32[]{:S(2)}) collective-permute-start(bf16[5,128,128]{2,1,0:T(8,128)(2,1)S(1)} %get-tuple-element.39), channel_id=1, source_target_pairs={{0,96},{8,104},{16,112},{24,120},{32,64},{40,72},{48,80},{56,88},{... | collective-permute-start | bytes 491528 | tf_op jit(solution)/shard_map/ppermute | solution.py:230
  26.2 3.2 %collective-permute-start.7 = (bf16[1,128,640]{2,1,0:T(8,128)(2,1)S(1)}, bf16[1,128,640]{2,1,0:T(8,128)(2,1)S(1)}, u32[]{:S(2)}, u32[]{:S(2)}) collective-permute-start(bf16[1,128,640]{2,1,0:T(8,128)(2,1)S(1)} %far_part.4), channel_id=1, source_target_pairs={{0,1},{1,0},{2,3},{3,2},{4,5},{5,4},{6,7},{7,6},{8,9},{9,8},{10,11... | collective-permute-start | bytes 491528 | tf_op jit(solution)/shard_map/ppermute | solution.py:221
  30.6 18.9 %collective-permute-start.11 = (bf16[128,2560]{1,0:T(8,128)(2,1)S(1)}, bf16[128,2560]{1,0:T(8,128)(2,1)S(1)}, u32[]{:S(2)}, u32[]{:S(2)}) collective-permute-start(bf16[128,2560]{1,0:T(8,128)(2,1)S(1)} %get-tuple-element.37), channel_id=1, source_target_pairs={{0,2},{1,3},{2,4},{3,5},{4,6},{5,7},{6,0},{7,1},{8,10},{9,11},{10,... | collective-permute-start | bytes 1966088 | tf_op jit(solution)/shard_map/ppermute | solution.py:218
  32.3 18.5 %collective-permute-start.13 = (bf16[128,2560]{1,0:T(8,128)(2,1)S(1)}, bf16[128,2560]{1,0:T(8,128)(2,1)S(1)}, u32[]{:S(2)}, u32[]{:S(2)}) collective-permute-start(bf16[128,2560]{1,0:T(8,128)(2,1)S(1)} %get-tuple-element.38), channel_id=1, source_target_pairs={{0,6},{1,7},{2,0},{3,1},{4,2},{5,3},{6,4},{7,5},{8,14},{9,15},{10,... | collective-permute-start | bytes 1966088 | tf_op jit(solution)/shard_map/ppermute | solution.py:218
  35.3 2.1 %collective-permute-start.8 = (bf16[3,128,640]{2,1,0:T(8,128)(2,1)S(1)}, bf16[3,128,640]{2,1,0:T(8,128)(2,1)S(1)}, u32[]{:S(2)}, u32[]{:S(2)}) collective-permute-start(bf16[3,128,640]{2,1,0:T(8,128)(2,1)S(1)} %far_part.7), channel_id=1, source_target_pairs={{0,1},{1,0},{2,3},{3,2},{4,5},{5,4},{6,7},{7,6},{8,9},{9,8},{10,11... | collective-permute-start | bytes 1474568 | tf_op jit(solution)/shard_map/ppermute | solution.py:221
  38.6 24.1 %collective-permute-start.9 = (bf16[128,2560]{1,0:T(8,128)(2,1)S(1)}, bf16[128,2560]{1,0:T(8,128)(2,1)S(1)}, u32[]{:S(2)}, u32[]{:S(2)}) collective-permute-start(bf16[128,2560]{1,0:T(8,128)(2,1)S(1)} %project.9), channel_id=1, source_target_pairs={{0,6},{1,7},{2,0},{3,1},{4,2},{5,3},{6,4},{7,5},{8,14},{9,15},{10,... | collective-permute-start | bytes 1966088 | tf_op jit(solution)/shard_map/ppermute | solution.py:218
  41.5 22.1 %collective-permute-start.10 = (bf16[128,2560]{1,0:T(8,128)(2,1)S(1)}, bf16[128,2560]{1,0:T(8,128)(2,1)S(1)}, u32[]{:S(2)}, u32[]{:S(2)}) collective-permute-start(bf16[128,2560]{1,0:T(8,128)(2,1)S(1)} %project.10), channel_id=1, source_target_pairs={{0,2},{1,3},{2,4},{3,5},{4,6},{5,7},{6,0},{7,1},{8,10},{9,11},{10,... | collective-permute-start | bytes 1966088 | tf_op jit(solution)/shard_map/ppermute | solution.py:218
  50.7 26.9 %collective-permute-start.12 = (bf16[128,2560]{1,0:T(8,128)(2,1)S(1)}, bf16[128,2560]{1,0:T(8,128)(2,1)S(1)}, u32[]{:S(2)}, u32[]{:S(2)}) collective-permute-start(bf16[128,2560]{1,0:T(8,128)(2,1)S(1)} %project.12), channel_id=1, source_target_pairs={{0,2},{1,3},{2,4},{3,5},{4,6},{5,7},{6,0},{7,1},{8,10},{9,11},{10,... | collective-permute-start | bytes 1966088 | tf_op jit(solution)/shard_map/ppermute | solution.py:218
  52.0 25.6 %collective-permute-start.14 = (bf16[128,2560]{1,0:T(8,128)(2,1)S(1)}, bf16[128,2560]{1,0:T(8,128)(2,1)S(1)}, u32[]{:S(2)}, u32[]{:S(2)}) collective-permute-start(bf16[128,2560]{1,0:T(8,128)(2,1)S(1)} %project.13), channel_id=1, source_target_pairs={{0,6},{1,7},{2,0},{3,1},{4,2},{5,3},{6,4},{7,5},{8,14},{9,15},{10,... | collective-permute-start | bytes 1966088 | tf_op jit(solution)/shard_map/ppermute | solution.py:218

commit v5 on v4

--- a/solution.py
+++ b/solution.py
@@ -167,19 +167,13 @@
     )(*args, *[x for x, _ in adds])
 
 
-def finish_body(own_ref, left_ref, right_ref, out_ref, hold_ref, sems):
-    width = own_ref.shape[1]
-    ends, start = left_ref.shape[1], width - right_ref.shape[1]
-    cuts = [0, start, ends, width] if start < ends else [0, ends, width]
+def finish_body(starts, own_ref, *refs):
+    out_ref, hold_ref, sems = refs[-3:]
     copies = []
-    for lo, hi in zip(cuts, cuts[1:]):
-        for n, size in tiles_of(hi - lo, FINISH_TILE):
-            there = slice(lo + n, lo + n + size)
-            total = own_ref[:, there]
-            if lo < ends:
-                total = total + left_ref[:, there].astype(F32)
-            if lo >= start:
-                total = total + right_ref[:, lo + n - start : lo + n - start + size].astype(F32)
+    for late_ref, start in zip(refs, starts):
+        for n, size in tiles_of(late_ref.shape[1], FINISH_TILE):
+            there = slice(start + n, start + n + size)
+            total = own_ref[:, there] + late_ref[:, n : n + size].astype(F32)
             hold_ref[:, there] = total.astype(BF16)
             i = len(copies)
             copies.append(pltpu.make_async_copy(hold_ref.at[:, there], out_ref.at[:, there], sems.at[i]))
@@ -188,19 +182,23 @@
         copy.wait()
 
 
-def finish(own, left, right):
+def finish(own, pieces, so_far=None):
     rows, width = own.shape
-    count = 3 * len(tiles_of(width, FINISH_TILE))
-    return pl.pallas_call(
-        finish_body,
-        in_specs=[VMEM] * 3,
-        out_specs=pl.BlockSpec(memory_space=pl.ANY),
+    starts = [start for _, start in pieces]
+    anywhere = pl.BlockSpec(memory_space=pl.ANY)
+    kept = [] if so_far is None else [so_far]
+    count = sum(len(tiles_of(piece.shape[1], FINISH_TILE)) for piece, _ in pieces)
+    return pl.pallas_call(
+        lambda *refs: finish_body(starts, *refs),
+        in_specs=[VMEM] * (1 + len(pieces)) + [anywhere] * len(kept),
+        out_specs=anywhere,
         out_shape=jax.ShapeDtypeStruct((rows, width), BF16),
         scratch_shapes=[pltpu.VMEM((rows, width), BF16), pltpu.SemaphoreType.DMA((count,))],
+        input_output_aliases={1 + len(pieces): 0} if kept else {},
         cost_estimate=cost(1000, 1000),
         compiler_params=vmem(16),
         name="finish",
-    )(own, left, right)
+    )(own, *[piece for piece, _ in pieces], *kept)
 
 
 def on_device(queries, key_rows, value_rows, level_weight, norm_gain, out_weight):
@@ -264,10 +262,14 @@
 
     direct_up = along_z(project(block(0), split, (rest,))[0], 1)
     direct_down = along_z(project(block(1), 0, (rest,))[0], -1)
-    joined_up = along_z(project(block(0), 0, (split,), ((relay_up, 0),))[0], 1)
-    joined_down = along_z(project(block(1), rest, (split,), ((relay_down, split - rest),))[0], -1)
+    last = width // 20
+    up_b, up_a = project(block(0), 0, (last, split - last), ((relay_up, 0),))
+    down_a, down_b = project(block(1), rest, (split - last, last), ((relay_down, split - rest),))
+    up_a, down_a = along_z(up_a, 1), along_z(down_a, -1)
+    up_b, down_b = along_z(up_b, 1), along_z(down_b, -1)
     (mine,) = project(block(2), 0, (width,), ((direct_down, 0), (direct_up, split)), F32, MINE_FLOPS)
-    return finish(mine, joined_up, joined_down)
+    out = finish(mine, [(up_a, last), (down_a, rest)])
+    return finish(mine, [(up_b, 0), (down_b, width - last)], out)
 
 
 def solution(mesh):

time: 79.1 us -> 78.6 us (level)
  waiting for transfers between devices: 34.3 us -> 29.8 us
  starting transfers between devices: 19.5 us -> 22.9 us
    ppermute x6 -> x8, waiting for transfers between devices: 28.6 us -> 24.2 us  [along_z(): return lax.ppermute(x, 'head', pairs)]
    ppermute x6 -> x8, starting transfers between devices: 8.46 us -> 11.8 us  [along_z(): return lax.ppermute(x, 'head', pairs)]
    pallas_call x1 -> x2, Pallas kernels: 1.21 us -> 1.78 us  [finish(): pl.pallas_call(lambda *refs: finish_body(starts, *refs), in_specs=[VMEM]...]
  transfers between devices with their start and end apart: 15 -> 17, of which waited for: 8 -> 8; matrix products, arithmetic and copies ran while one was open for 3% -> 3% of each run, Pallas kernels for 21% -> 23%
where the time goes in v5:
time: 78.6 us; the launch traced here: 78.4 us
  waiting for transfers between devices  29.8 us (38%)
  starting transfers between devices  22.9 us (29%)
  Pallas kernels  20.2 us (26%)
  local copies, waits for them, and re-layouts  2.79 us (4%)
  matrix products  2.26 us (3%)
    ppermute x8, waiting for transfers between devices, along_z(): return lax.ppermute(x, 'head', pairs)  24.2 us
    ppermute x8, starting transfers between devices, along_z(): return lax.ppermute(x, 'head', pairs)  11.8 us
    pallas_call x7, Pallas kernels, project(): pl.pallas_call(lambda *refs: project_body(blocks, col_start, [lo for _, l...  9.32 us
    ppermute x6, starting transfers between devices, swaps(): got.append(lax.ppermute(x, 'ctx', pairs))  7.54 us
    pallas_call x2, Pallas kernels, local_part(): pl.pallas_call(lambda *refs: local_body(heads, *refs[:4], refs[-1]), in_s...  6.59 us
    ppermute x6, waiting for transfers between devices, swaps(): got.append(lax.ppermute(x, 'ctx', pairs))  4.91 us
    ppermute x3, starting transfers between devices, across_cores(): return lax.ppermute(x, 'head', [(i, i ^ 1) for i in range(8)])  3.52 us
    unnamed x12, local copies, waits for them, and re-layouts  2.65 us
  transfers between devices with their start and end apart: 17, of which 8 were waited for; matrix products, arithmetic and copies ran while one was open for 3% of the time, Pallas kernels for 23%

profile of v5, /device:TPU:1, one launch (start us, length us, event | category | flops | bytes accessed | tf_op | source)
XLA Modules:
  0.0 78.4 jit_solution(3973899559515533775)
XLA Ops:
  0.0 1.4 %collective-permute-start.3 = (bf16[640,5120]{1,0:T(8,128)(2,1)}, bf16[640,5120]{1,0:T(8,128)(2,1)S(1)}, u32[]{:S(2)}, u32[]{:S(2)}) collective-permute-start(bf16[640,5120]{1,0:T(8,128)(2,1)} %refs_1_.11), channel_id=1, source_target_pairs={{0,1},{1,0},{2,3},{3,2},{4,5},{5,4},{6,7},{7,6},{8,9},{9,8},{10,11... | collective-permute-start | bytes 19660808 | tf_op jit(solution)/shard_map/ppermute | solution.py:219
  1.4 2.3 %convolution_convert_fusion = bf16[5,128,128]{2,1,0:T(8,128)(2,1)S(1)} fusion(bf16[1024,5,128]{2,0,1:T(8,128)(2,1)} %param.7, bf16[1024,5,128]{2,0,1:T(8,128)(2,1)} %param.8), kind=kOutput, calls=%fused_computation | convolution fusion | flops 167854080 | bytes 2785280 | tf_op jit(solution)/shard_map/hse,hsd->hed/dot_general | solution.py:232
  3.7 2.9 %collective-permute-start.2 = (bf16[5,128,128]{2,1,0:T(8,128)(2,1)S(1)}, bf16[5,128,128]{2,1,0:T(8,128)(2,1)S(1)}, u32[]{:S(2)}, u32[]{:S(2)}) collective-permute-start(bf16[5,128,128]{2,1,0:T(8,128)(2,1)S(1)} %convolution_convert_fusion), channel_id=1, source_target_pairs={{0,16},{8,24},{16,0},{24,8},{32,48},{40,56},{48,32},{56,40},{64,80... | collective-permute-start | bytes 491528 | tf_op jit(solution)/shard_map/ppermute | solution.py:228
  7.5 1.3 %copy-done.3 = bf16[1024,5,128]{2,0,1:T(8,128)(2,1)S(1)} copy-done((bf16[1024,5,128]{2,0,1:T(8,128)(2,1)S(1)}, bf16[1024,5,128]{2,0,1:T(8,128)(2,1)}, u32[]{:S(2)}) %copy-start.3) | copy-done | bytes 1310744
  8.8 1.3 %copy-done.4 = bf16[1024,5,128]{2,0,1:T(8,128)(2,1)S(1)} copy-done((bf16[1024,5,128]{2,0,1:T(8,128)(2,1)S(1)}, bf16[1024,5,128]{2,0,1:T(8,128)(2,1)}, u32[]{:S(2)}) %copy-start.4) | copy-done | bytes 1310744
  10.1 3.9 %local_part.2.refs_4_ = f32[3,128,1024]{2,1,0:T(8,128)S(1)} custom-call(bf16[5,1024,128]{2,1,0:T(8,128)(2,1)S(1)} %bitcast.8, bf16[5,1024,128]{2,1,0:T(8,128)(2,1)S(1)} %bitcast.20, bf16[5,1024,128]{2,1,0:T(8,128)(2,1)S(1)} %bitcast.22, f32[5,16,1024]{2,1,0:T(8,128)S(1)} %bitcast.14), custom_call_target="tpu_custom_call" | custom-call | flops 503316480 | bytes 3932160 | tf_op jit(solution)/shard_map/local_part/pallas_call | solution.py:79
  14.8 3.0 %collective-permute-start.6 = (bf16[5,128,128]{2,1,0:T(8,128)(2,1)S(1)}, bf16[5,128,128]{2,1,0:T(8,128)(2,1)S(1)}, u32[]{:S(2)}, u32[]{:S(2)}) collective-permute-start(bf16[5,128,128]{2,1,0:T(8,128)(2,1)S(1)} %get-tuple-element.47), channel_id=1, source_target_pairs={{0,64},{8,72},{16,80},{24,88},{32,96},{40,104},{48,112},{56,120},{... | collective-permute-start | bytes 491528 | tf_op jit(solution)/shard_map/ppermute | solution.py:228
  18.6 2.7 %local_part.3.refs_5_ = f32[2,128,1024]{2,1,0:T(8,128)S(1)} custom-call(bf16[5,1024,128]{2,1,0:T(8,128)(2,1)S(1)} %bitcast.9, bf16[5,1024,128]{2,1,0:T(8,128)(2,1)S(1)} %bitcast.21, bf16[5,1024,128]{2,1,0:T(8,128)(2,1)S(1)} %bitcast.23, f32[5,16,1024]{2,1,0:T(8,128)S(1)} %bitcast.15, bf16[640,5120]{1,0:T(8,128)(2,1)S(1)} %copy-done), custom_call_target="tpu_custom_call" | custom-call | flops 335544320 | bytes 2621440 | tf_op jit(solution)/shard_map/local_part/pallas_call | solution.py:79
  21.3 3.7 %collective-permute-done.5.refs_2_ = bf16[5,128,128]{2,1,0:T(8,128)(2,1)S(1)} collective-permute-done((bf16[5,128,128]{2,1,0:T(8,128)(2,1)S(1)}, bf16[5,128,128]{2,1,0:T(8,128)(2,1)S(1)}, u32[]{:S(2)}, u32[]{:S(2)}) %collective-permute-start.5) | collective-permute-done | bytes 163872 | tf_op jit(solution)/shard_map/ppermute | solution.py:228
  26.2 1.5 %collective-permute-start.7 = (bf16[1,128,640]{2,1,0:T(8,128)(2,1)S(1)}, bf16[1,128,640]{2,1,0:T(8,128)(2,1)S(1)}, u32[]{:S(2)}, u32[]{:S(2)}) collective-permute-start(bf16[1,128,640]{2,1,0:T(8,128)(2,1)S(1)} %far_part.4), channel_id=1, source_target_pairs={{0,1},{1,0},{2,3},{3,2},{4,5},{5,4},{6,7},{7,6},{8,9},{9,8},{10,11... | collective-permute-start | bytes 491528 | tf_op jit(solution)/shard_map/ppermute | solution.py:219
  28.2 1.2 %project.7.refs_2_ = f32[128,5120]{1,0:T(8,128)S(1)} custom-call(bf16[1,128,640]{2,1,0:T(8,128)(2,1)S(1)} %far_part.5.refs_0_, bf16[640,5120]{1,0:T(8,128)(2,1)S(1)} %copy-done), custom_call_target="tpu_custom_call" | custom-call | flops 1000 | bytes 1000 | tf_op jit(solution)/shard_map/project/pallas_call | solution.py:159
  29.4 1.2 %project.8 = (bf16[128,2560]{1,0:T(8,128)(2,1)S(1)}, bf16[128,2560]{1,0:T(8,128)(2,1)S(1)}) custom-call(bf16[1,128,640]{2,1,0:T(8,128)(2,1)S(1)} %collective-permute-done.7.refs_0_, bf16[640,5120]{1,0:T(8,128)(2,1)S(1)} %collective-permute-done.3.refs_1_.refs_3_, f32[128,5120]{1,0:T(8,128)S(1)} %project.7.refs_2_), custom_call_target="tpu_custom_call" | custom-call | flops 1000 | bytes 1000 | tf_op jit(solution)/shard_map/project/pallas_call | solution.py:159
  30.6 1.7 %collective-permute-start.11 = (bf16[128,2560]{1,0:T(8,128)(2,1)S(1)}, bf16[128,2560]{1,0:T(8,128)(2,1)S(1)}, u32[]{:S(2)}, u32[]{:S(2)}) collective-permute-start(bf16[128,2560]{1,0:T(8,128)(2,1)S(1)} %get-tuple-element.41), channel_id=1, source_target_pairs={{0,2},{1,3},{2,4},{3,5},{4,6},{5,7},{6,0},{7,1},{8,10},{9,11},{10,... | collective-permute-start | bytes 1966088 | tf_op jit(solution)/shard_map/ppermute | solution.py:216
  32.3 2.2 %collective-permute-start.13 = (bf16[128,2560]{1,0:T(8,128)(2,1)S(1)}, bf16[128,2560]{1,0:T(8,128)(2,1)S(1)}, u32[]{:S(2)}, u32[]{:S(2)}) collective-permute-start(bf16[128,2560]{1,0:T(8,128)(2,1)S(1)} %get-tuple-element.43), channel_id=1, source_target_pairs={{0,6},{1,7},{2,0},{3,1},{4,2},{5,3},{6,4},{7,5},{8,14},{9,15},{10,... | collective-permute-start | bytes 1966088 | tf_op jit(solution)/shard_map/ppermute | solution.py:216
  37.4 1.2 %project.9 = bf16[128,2560]{1,0:T(8,128)(2,1)S(1)} custom-call(bf16[3,128,640]{2,1,0:T(8,128)(2,1)S(1)} %far_part.6.refs_0_, bf16[640,5120]{1,0:T(8,128)(2,1)S(1)} %copy-done, bf16[3,128,640]{2,1,0:T(8,128)(2,1)S(1)} %collective-permute-done.8.refs_2_, bf16[640,5120]{1,0:T(8,128)(2,1)S(1)} %collective-permute-done.3.refs_1_.refs_3_), custom_call_target="tpu_custom_call" | custom-call | flops 1000 | bytes 1000 | tf_op jit(solution)/shard_map/project/pallas_call | solution.py:159
  38.6 1.7 %collective-permute-start.9 = (bf16[128,2560]{1,0:T(8,128)(2,1)S(1)}, bf16[128,2560]{1,0:T(8,128)(2,1)S(1)}, u32[]{:S(2)}, u32[]{:S(2)}) collective-permute-start(bf16[128,2560]{1,0:T(8,128)(2,1)S(1)} %project.9), channel_id=1, source_target_pairs={{0,6},{1,7},{2,0},{3,1},{4,2},{5,3},{6,4},{7,5},{8,14},{9,15},{10,... | collective-permute-start | bytes 1966088 | tf_op jit(solution)/shard_map/ppermute | solution.py:216
  41.5 7.9 %collective-permute-done.11.refs_4_ = bf16[128,2560]{1,0:T(8,128)(2,1)S(1)} collective-permute-done((bf16[128,2560]{1,0:T(8,128)(2,1)S(1)}, bf16[128,2560]{1,0:T(8,128)(2,1)S(1)}, u32[]{:S(2)}, u32[]{:S(2)}) %collective-permute-start.11) | collective-permute-done | bytes 655392 | tf_op jit(solution)/shard_map/ppermute | solution.py:216
  49.5 1.2 %project.12 = (bf16[128,256]{1,0:T(8,128)(2,1)S(1)}, bf16[128,2304]{1,0:T(8,128)(2,1)S(1)}) custom-call(bf16[3,128,640]{2,1,0:T(8,128)(2,1)S(1)} %far_part.6.refs_0_, bf16[640,5120]{1,0:T(8,128)(2,1)S(1)} %copy-done, bf16[3,128,640]{2,1,0:T(8,128)(2,1)S(1)} %collective-permute-done.8.refs_2_, bf16[640,5120]{1,0:T(8,128)(2,1)S(1)} %collective-permute-done.3.refs_1_.refs_3_, ...), custom_call_target="tpu_custom_call" | custom-call | flops 1000 | bytes 1000 | tf_op jit(solution)/shard_map/project/pallas_call | solution.py:159
  50.8 1.2 %project.13 = (bf16[128,2304]{1,0:T(8,128)(2,1)S(1)}, bf16[128,256]{1,0:T(8,128)(2,1)S(1)}) custom-call(bf16[3,128,640]{2,1,0:T(8,128)(2,1)S(1)} %far_part.6.refs_0_, bf16[640,5120]{1,0:T(8,128)(2,1)S(1)} %copy-done, bf16[3,128,640]{2,1,0:T(8,128)(2,1)S(1)} %collective-permute-done.8.refs_2_, bf16[640,5120]{1,0:T(8,128)(2,1)S(1)} %collective-permute-done.3.refs_1_.refs_3_, ...), custom_call_target="tpu_custom_call" | custom-call | flops 1000 | bytes 1000 | tf_op jit(solution)/shard_map/project/pallas_call | solution.py:159
  52.0 2.7 %collective-permute-start.16 = (bf16[128,2304]{1,0:T(8,128)(2,1)S(1)}, bf16[128,2304]{1,0:T(8,128)(2,1)S(1)}, u32[]{:S(2)}, u32[]{:S(2)}) collective-permute-start(bf16[128,2304]{1,0:T(8,128)(2,1)S(1)} %get-tuple-element.46), channel_id=1, source_target_pairs={{0,6},{1,7},{2,0},{3,1},{4,2},{5,3},{6,4},{7,5},{8,14},{9,15},{10,... | collective-permute-start | bytes 1769480 | tf_op jit(solution)/shard_map/ppermute | solution.py:216
  54.7 8.0 %collective-permute-done.9.refs_4_ = bf16[128,2560]{1,0:T(8,128)(2,1)S(1)} collective-permute-done((bf16[128,2560]{1,0:T(8,128)(2,1)S(1)}, bf16[128,2560]{1,0:T(8,128)(2,1)S(1)}, u32[]{:S(2)}, u32[]{:S(2)}) %collective-permute-start.9) | collective-permute-done | bytes 655392 | tf_op jit(solution)/shard_map/ppermute | solution.py:216
  62.7 3.4 %collective-permute-start.14 = (bf16[128,256]{1,0:T(8,128)(2,1)S(1)}, bf16[128,256]{1,0:T(8,128)(2,1)S(1)}, u32[]{:S(2)}, u32[]{:S(2)}) collective-permute-start(bf16[128,256]{1,0:T(8,128)(2,1)S(1)} %get-tuple-element.44), channel_id=1, source_target_pairs={{0,6},{1,7},{2,0},{3,1},{4,2},{5,3},{6,4},{7,5},{8,14},{9,15},{10,... | collective-permute-start | bytes 196616 | tf_op jit(solution)/shard_map/ppermute | solution.py:216
  66.1 2.2 %project.11.refs_0_ = f32[128,5120]{1,0:T(8,128)S(1)} custom-call(bf16[3,128,640]{2,1,0:T(8,128)(2,1)S(1)} %far_part.6.refs_0_, bf16[640,5120]{1,0:T(8,128)(2,1)S(1)} %copy-done, bf16[3,128,640]{2,1,0:T(8,128)(2,1)S(1)} %collective-permute-done.8.refs_2_, bf16[640,5120]{1,0:T(8,128)(2,1)S(1)} %collective-permute-done.3.refs_1_.refs_3_, ...), custom_call_target="tpu_custom_call" | custom-call | flops 1000 | bytes 1000 | tf_op jit(solution)/shard_map/project/pallas_call | solution.py:159
  68.3 7.9 %collective-permute-done.15.refs_1_ = bf16[128,2304]{1,0:T(8,128)(2,1)S(1)} collective-permute-done((bf16[128,2304]{1,0:T(8,128)(2,1)S(1)}, bf16[128,2304]{1,0:T(8,128)(2,1)S(1)}, u32[]{:S(2)}, u32[]{:S(2)}) %collective-permute-start.15) | collective-permute-done | bytes 589856 | tf_op jit(solution)/shard_map/ppermute | solution.py:216
  (41 shorter events, 10.4 us)
Async XLA Ops:
  0.0 7.5 %copy-start.2 = (f32[1024,5,16]{0,2,1:T(8,128)S(1)}, f32[1024,5,16]{0,2,1:T(8,128)}, u32[]{:S(2)}) copy-start(f32[1024,5,16]{0,2,1:T(8,128)} %param.9) | copy-start | bytes 983044
  0.0 7.5 %copy-start.1 = (bf16[1024,5,128]{2,0,1:T(8,128)(2,1)S(1)}, bf16[1024,5,128]{2,0,1:T(8,128)(2,1)}, u32[]{:S(2)}) copy-start(bf16[1024,5,128]{2,0,1:T(8,128)(2,1)} %param.6) | copy-start | bytes 3932164
  0.0 14.7 %collective-permute-start.3 = (bf16[640,5120]{1,0:T(8,128)(2,1)}, bf16[640,5120]{1,0:T(8,128)(2,1)S(1)}, u32[]{:S(2)}, u32[]{:S(2)}) collective-permute-start(bf16[640,5120]{1,0:T(8,128)(2,1)} %refs_1_.11), channel_id=1, source_target_pairs={{0,1},{1,0},{2,3},{3,2},{4,5},{5,4},{6,7},{7,6},{8,9},{9,8},{10,11... | collective-permute-start | bytes 19660808 | tf_op jit(solution)/shard_map/ppermute | solution.py:219
  3.7 10.3 %collective-permute-start.2 = (bf16[5,128,128]{2,1,0:T(8,128)(2,1)S(1)}, bf16[5,128,128]{2,1,0:T(8,128)(2,1)S(1)}, u32[]{:S(2)}, u32[]{:S(2)}) collective-permute-start(bf16[5,128,128]{2,1,0:T(8,128)(2,1)S(1)} %convolution_convert_fusion), channel_id=1, source_target_pairs={{0,16},{8,24},{16,0},{24,8},{32,48},{40,56},{48,32},{56,40},{64,80... | collective-permute-start | bytes 491528 | tf_op jit(solution)/shard_map/ppermute | solution.py:228
  6.6 8.1 %collective-permute-start.1 = (bf16[5,128,128]{2,1,0:T(8,128)(2,1)S(1)}, bf16[5,128,128]{2,1,0:T(8,128)(2,1)S(1)}, u32[]{:S(2)}, u32[]{:S(2)}) collective-permute-start(bf16[5,128,128]{2,1,0:T(8,128)(2,1)S(1)} %convolution_convert_fusion), channel_id=1, source_target_pairs={{0,8},{8,0},{16,24},{24,16},{32,40},{40,32},{48,56},{56,48},{64,72... | collective-permute-start | bytes 491528 | tf_op jit(solution)/shard_map/ppermute | solution.py:228
  6.9 7.8 %collective-permute-start = (bf16[5,128,128]{2,1,0:T(8,128)(2,1)S(1)}, bf16[5,128,128]{2,1,0:T(8,128)(2,1)S(1)}, u32[]{:S(2)}, u32[]{:S(2)}) collective-permute-start(bf16[5,128,128]{2,1,0:T(8,128)(2,1)S(1)} %convolution_convert_fusion), channel_id=1, source_target_pairs={{0,24},{8,16},{16,8},{24,0},{32,56},{40,48},{48,40},{56,32},{64,88... | collective-permute-start | bytes 491528 | tf_op jit(solution)/shard_map/ppermute | solution.py:228
  7.5 1.3 %copy-start.3 = (bf16[1024,5,128]{2,0,1:T(8,128)(2,1)S(1)}, bf16[1024,5,128]{2,0,1:T(8,128)(2,1)}, u32[]{:S(2)}) copy-start(bf16[1024,5,128]{2,0,1:T(8,128)(2,1)} %param.7) | copy-start | bytes 3932164
  8.8 1.3 %copy-start.4 = (bf16[1024,5,128]{2,0,1:T(8,128)(2,1)S(1)}, bf16[1024,5,128]{2,0,1:T(8,128)(2,1)}, u32[]{:S(2)}) copy-start(bf16[1024,5,128]{2,0,1:T(8,128)(2,1)} %param.8) | copy-start | bytes 3932164
  10.1 8.5 %copy-start = (bf16[640,5120]{1,0:T(8,128)(2,1)S(1)}, bf16[640,5120]{1,0:T(8,128)(2,1)}, u32[]{:S(2)}) copy-start(bf16[640,5120]{1,0:T(8,128)(2,1)} %refs_1_.11) | copy-start | bytes 19660804
  14.8 10.8 %copy-start.5 = (f32[5,128]{1,0:T(8,128)S(1)}, f32[5,128]{1,0:T(8,128)}, u32[]{:S(2)}) copy-start(f32[5,128]{1,0:T(8,128)} %param.10) | copy-start | bytes 7684
  14.8 6.5 %collective-permute-start.6 = (bf16[5,128,128]{2,1,0:T(8,128)(2,1)S(1)}, bf16[5,128,128]{2,1,0:T(8,128)(2,1)S(1)}, u32[]{:S(2)}, u32[]{:S(2)}) collective-permute-start(bf16[5,128,128]{2,1,0:T(8,128)(2,1)S(1)} %get-tuple-element.47), channel_id=1, source_target_pairs={{0,64},{8,72},{16,80},{24,88},{32,96},{40,104},{48,112},{56,120},{... | collective-permute-start | bytes 491528 | tf_op jit(solution)/shard_map/ppermute | solution.py:228
  17.8 7.2 %collective-permute-start.5 = (bf16[5,128,128]{2,1,0:T(8,128)(2,1)S(1)}, bf16[5,128,128]{2,1,0:T(8,128)(2,1)S(1)}, u32[]{:S(2)}, u32[]{:S(2)}) collective-permute-start(bf16[5,128,128]{2,1,0:T(8,128)(2,1)S(1)} %get-tuple-element.47), channel_id=1, source_target_pairs={{0,32},{8,40},{16,48},{24,56},{32,0},{40,8},{48,16},{56,24},{64,96... | collective-permute-start | bytes 491528 | tf_op jit(solution)/shard_map/ppermute | solution.py:228
  18.2 7.3 %collective-permute-start.4 = (bf16[5,128,128]{2,1,0:T(8,128)(2,1)S(1)}, bf16[5,128,128]{2,1,0:T(8,128)(2,1)S(1)}, u32[]{:S(2)}, u32[]{:S(2)}) collective-permute-start(bf16[5,128,128]{2,1,0:T(8,128)(2,1)S(1)} %get-tuple-element.47), channel_id=1, source_target_pairs={{0,96},{8,104},{16,112},{24,120},{32,64},{40,72},{48,80},{56,88},{... | collective-permute-start | bytes 491528 | tf_op jit(solution)/shard_map/ppermute | solution.py:228
  26.2 3.2 %collective-permute-start.7 = (bf16[1,128,640]{2,1,0:T(8,128)(2,1)S(1)}, bf16[1,128,640]{2,1,0:T(8,128)(2,1)S(1)}, u32[]{:S(2)}, u32[]{:S(2)}) collective-permute-start(bf16[1,128,640]{2,1,0:T(8,128)(2,1)S(1)} %far_part.4), channel_id=1, source_target_pairs={{0,1},{1,0},{2,3},{3,2},{4,5},{5,4},{6,7},{7,6},{8,9},{9,8},{10,11... | collective-permute-start | bytes 491528 | tf_op jit(solution)/shard_map/ppermute | solution.py:219
  30.6 18.9 %collective-permute-start.11 = (bf16[128,2560]{1,0:T(8,128)(2,1)S(1)}, bf16[128,2560]{1,0:T(8,128)(2,1)S(1)}, u32[]{:S(2)}, u32[]{:S(2)}) collective-permute-start(bf16[128,2560]{1,0:T(8,128)(2,1)S(1)} %get-tuple-element.41), channel_id=1, source_target_pairs={{0,2},{1,3},{2,4},{3,5},{4,6},{5,7},{6,0},{7,1},{8,10},{9,11},{10,... | collective-permute-start | bytes 1966088 | tf_op jit(solution)/shard_map/ppermute | solution.py:216
  32.3 18.5 %collective-permute-start.13 = (bf16[128,2560]{1,0:T(8,128)(2,1)S(1)}, bf16[128,2560]{1,0:T(8,128)(2,1)S(1)}, u32[]{:S(2)}, u32[]{:S(2)}) collective-permute-start(bf16[128,2560]{1,0:T(8,128)(2,1)S(1)} %get-tuple-element.43), channel_id=1, source_target_pairs={{0,6},{1,7},{2,0},{3,1},{4,2},{5,3},{6,4},{7,5},{8,14},{9,15},{10,... | collective-permute-start | bytes 1966088 | tf_op jit(solution)/shard_map/ppermute | solution.py:216
  35.3 2.1 %collective-permute-start.8 = (bf16[3,128,640]{2,1,0:T(8,128)(2,1)S(1)}, bf16[3,128,640]{2,1,0:T(8,128)(2,1)S(1)}, u32[]{:S(2)}, u32[]{:S(2)}) collective-permute-start(bf16[3,128,640]{2,1,0:T(8,128)(2,1)S(1)} %far_part.7), channel_id=1, source_target_pairs={{0,1},{1,0},{2,3},{3,2},{4,5},{5,4},{6,7},{7,6},{8,9},{9,8},{10,11... | collective-permute-start | bytes 1474568 | tf_op jit(solution)/shard_map/ppermute | solution.py:219
  38.6 24.1 %collective-permute-start.9 = (bf16[128,2560]{1,0:T(8,128)(2,1)S(1)}, bf16[128,2560]{1,0:T(8,128)(2,1)S(1)}, u32[]{:S(2)}, u32[]{:S(2)}) collective-permute-start(bf16[128,2560]{1,0:T(8,128)(2,1)S(1)} %project.9), channel_id=1, source_target_pairs={{0,6},{1,7},{2,0},{3,1},{4,2},{5,3},{6,4},{7,5},{8,14},{9,15},{10,... | collective-permute-start | bytes 1966088 | tf_op jit(solution)/shard_map/ppermute | solution.py:216
  41.5 24.6 %collective-permute-start.10 = (bf16[128,2560]{1,0:T(8,128)(2,1)S(1)}, bf16[128,2560]{1,0:T(8,128)(2,1)S(1)}, u32[]{:S(2)}, u32[]{:S(2)}) collective-permute-start(bf16[128,2560]{1,0:T(8,128)(2,1)S(1)} %project.10), channel_id=1, source_target_pairs={{0,2},{1,3},{2,4},{3,5},{4,6},{5,7},{6,0},{7,1},{8,10},{9,11},{10,... | collective-permute-start | bytes 1966088 | tf_op jit(solution)/shard_map/ppermute | solution.py:216
  50.7 25.5 %collective-permute-start.15 = (bf16[128,2304]{1,0:T(8,128)(2,1)S(1)}, bf16[128,2304]{1,0:T(8,128)(2,1)S(1)}, u32[]{:S(2)}, u32[]{:S(2)}) collective-permute-start(bf16[128,2304]{1,0:T(8,128)(2,1)S(1)} %get-tuple-element.45), channel_id=1, source_target_pairs={{0,2},{1,3},{2,4},{3,5},{4,6},{5,7},{6,0},{7,1},{8,10},{9,11},{10,... | collective-permute-start | bytes 1769480 | tf_op jit(solution)/shard_map/ppermute | solution.py:216
  52.0 24.2 %collective-permute-start.16 = (bf16[128,2304]{1,0:T(8,128)(2,1)S(1)}, bf16[128,2304]{1,0:T(8,128)(2,1)S(1)}, u32[]{:S(2)}, u32[]{:S(2)}) collective-permute-start(bf16[128,2304]{1,0:T(8,128)(2,1)S(1)} %get-tuple-element.46), channel_id=1, source_target_pairs={{0,6},{1,7},{2,0},{3,1},{4,2},{5,3},{6,4},{7,5},{8,14},{9,15},{10,... | collective-permute-start | bytes 1769480 | tf_op jit(solution)/shard_map/ppermute | solution.py:216
  54.7 22.9 %collective-permute-start.12 = (bf16[128,256]{1,0:T(8,128)(2,1)S(1)}, bf16[128,256]{1,0:T(8,128)(2,1)S(1)}, u32[]{:S(2)}, u32[]{:S(2)}) collective-permute-start(bf16[128,256]{1,0:T(8,128)(2,1)S(1)} %get-tuple-element.42), channel_id=1, source_target_pairs={{0,2},{1,3},{2,4},{3,5},{4,6},{5,7},{6,0},{7,1},{8,10},{9,11},{10,... | collective-permute-start | bytes 196616 | tf_op jit(solution)/shard_map/ppermute | solution.py:216
  62.7 14.9 %collective-permute-start.14 = (bf16[128,256]{1,0:T(8,128)(2,1)S(1)}, bf16[128,256]{1,0:T(8,128)(2,1)S(1)}, u32[]{:S(2)}, u32[]{:S(2)}) collective-permute-start(bf16[128,256]{1,0:T(8,128)(2,1)S(1)} %get-tuple-element.44), channel_id=1, source_target_pairs={{0,6},{1,7},{2,0},{3,1},{4,2},{5,3},{6,4},{7,5},{8,14},{9,15},{10,... | collective-permute-start | bytes 196616 | tf_op jit(solution)/shard_map/ppermute | solution.py:216
